TPU v7x, 32 devices: a whole 2x2x4 slice. The times are simulated.
32 devices in a mesh: segment: 2 (over x), rep: 16 (over z, y, core).
Axes of the slice: x: 2, y: 2, z: 4, core: 2. Of those that a mesh axis runs over, the one named last changes fastest.
Arguments:
- feature_maps: bfloat16 [256, 7, 7, 1024], P(('segment', 'rep')), may hold values from -6 to 6
- path_lists: int32 [1, 256, 1], P(None, ('segment', 'rep')), may hold values from 0 to 1; in each aligned block of 8 rows (0 to 7, 8 to 15, ..., all dimensions but the last counted through in order) at most 4 rows name the same one
- point_weight: bfloat16 [1, 2, 1024, 1024], P(None, 'segment'), may hold values from -0.1875 to 0.1875
- depth_kernel: float32 [1, 2, 25, 1024], P(None, 'segment'), may hold values from -1.8 to 1.8
- cotangent: bfloat16 [256, 7, 7, 1024], P(('segment', 'rep')), may hold values from -6 to 6
Outputs:
- final_maps: bfloat16 [256, 7, 7, 1024], P(('segment', 'rep'))
- input_grad: bfloat16 [256, 7, 7, 1024], P(('segment', 'rep'))
- point_grad: float32 [1, 2, 1024, 1024], P(None, 'segment', 'rep')
- depth_grad: float32 [1, 2, 25, 1024], P(None, 'segment')
Inputs may be any that keep to these rules, and one draw needn't show every extreme that they name: `path_lists`: in each layer, among the 8 samples of one device no operator is chosen by more than 4 samples.
All inputs are finite; a program needn't handle non-finite values.
Results may differ from a plain program's by a relative error of at most 0.0032.
Values may be sent and summed in bfloat16 or wider, within the bound.
No kernel may reach another device: no remote copies, remote signals or barrier semaphores. Data moves between devices by JAX's collectives and lax.ppermute only.
A program may use at most 128 MiB of HBM per device.

v0:
```python
import jax
import jax.numpy as jnp
from jax import lax
from jax.sharding import PartitionSpec as P

LAYERS = 1


EPS = 1e-05


def tap_mask(op_kind):
    tap_index = jnp.arange(25, dtype=jnp.int32)
    row_shift = tap_index // 5 - 2
    col_shift = tap_index % 5 - 2
    narrow = (jnp.abs(row_shift) <= 1) & (jnp.abs(col_shift) <= 1)
    spaced = (row_shift % 2 == 0) & (col_shift % 2 == 0)
    tap_keep = jnp.where(op_kind == 0, narrow, jnp.where(op_kind == 1, True, spaced))
    return tap_keep.astype(jnp.float32)


def shift_window(padded, row_shift, col_shift, map_side):
    return padded[
        :, 2 + row_shift : 2 + row_shift + map_side, 2 + col_shift : 2 + col_shift + map_side, :
    ]


def depthwise(source, kernel):
    map_side = source.shape[1]
    padded = jnp.pad(source, ((0, 0), (2, 2), (2, 2), (0, 0)))
    summed = jnp.zeros_like(source)
    for offset in range(25):
        summed = summed + kernel[offset] * shift_window(
            padded, offset // 5 - 2, offset % 5 - 2, map_side
        )
    return summed


def depthwise_back(grad_maps, kernel):
    map_side = grad_maps.shape[1]
    padded = jnp.pad(grad_maps, ((0, 0), (2, 2), (2, 2), (0, 0)))
    summed = jnp.zeros_like(grad_maps)
    for offset in range(25):
        summed = summed + kernel[offset] * shift_window(
            padded, 2 - offset // 5, 2 - offset % 5, map_side
        )
    return summed


def kernel_grad(grad_maps, source):
    map_side = source.shape[1]
    padded = jnp.pad(source, ((0, 0), (2, 2), (2, 2), (0, 0)))
    tap_rows = [
        jnp.sum(
            grad_maps * shift_window(padded, offset // 5 - 2, offset % 5 - 2, map_side),
            axis=(0, 1, 2),
        )
        for offset in range(25)
    ]
    return jnp.stack(tap_rows)


def block_forward(inputs, pointwise, kernel):
    channels = inputs.shape[-1]
    source = inputs.astype(jnp.float32)
    mixed_taps = depthwise(source, kernel)
    scaled = mixed_taps * lax.rsqrt(jnp.mean(mixed_taps * mixed_taps, axis=-1, keepdims=True) + EPS)
    active = (scaled * jax.nn.sigmoid(scaled)).astype(jnp.bfloat16)
    branch = jnp.dot(active.reshape(-1, channels), pointwise, preferred_element_type=jnp.float32)
    return (source + branch.reshape(source.shape)).astype(jnp.bfloat16)


def block_backward(inputs, grad_maps, pointwise, kernel):
    channels = inputs.shape[-1]
    source = inputs.astype(jnp.float32)
    mixed_taps = depthwise(source, kernel)
    inverse = lax.rsqrt(jnp.mean(mixed_taps * mixed_taps, axis=-1, keepdims=True) + EPS)
    scaled = mixed_taps * inverse
    logistic = jax.nn.sigmoid(scaled)
    active = (scaled * logistic).astype(jnp.bfloat16)
    flat_grads = grad_maps.reshape(-1, channels)
    back_act = lax.dot_general(
        flat_grads, pointwise, (((1,), (1,)), ((), ())), preferred_element_type=jnp.float32
    ).reshape(source.shape)
    grad_scaled = back_act * logistic * (1.0 + scaled * (1.0 - logistic))
    grad_mixed = inverse * (
        grad_scaled - scaled * jnp.mean(grad_scaled * scaled, axis=-1, keepdims=True)
    )
    grad_in = (grad_maps.astype(jnp.float32) + depthwise_back(grad_mixed, kernel)).astype(
        jnp.bfloat16
    )
    return (grad_in, active.reshape(-1, channels), flat_grads, kernel_grad(grad_mixed, source))


def point_term(active, flat_grads):
    return lax.dot_general(
        active, flat_grads, (((0,), (0,)), ((), ())), preferred_element_type=jnp.float32
    )


def dispatch_table(path_row, sections, capacity):
    samples = path_row.shape[0]
    earlier = (
        jnp.arange(samples, dtype=jnp.int32)[None, :]
        < jnp.arange(samples, dtype=jnp.int32)[:, None]
    )
    same_path = (path_row[None, :] == path_row[:, None]) & earlier
    path_rank = jnp.sum(same_path.astype(jnp.int32), axis=1)
    slot_of = path_row * capacity + path_rank
    return (jnp.arange(sections * capacity, dtype=jnp.int32)[:, None] == slot_of[None, :]).astype(
        jnp.bfloat16
    )


def apply_block(slot_items, pointwise, kernel):
    flat_rows = slot_items.reshape((-1,) + slot_items.shape[2:])
    return (block_forward(flat_rows, pointwise, kernel).reshape(slot_items.shape), slot_items)


def body(feature_maps, path_lists, point_weight, depth_kernel, cotangent):
    sections = lax.axis_size("segment")
    section = lax.axis_index("segment")
    samples_here = feature_maps.shape[0]
    capacity = max(max(2, samples_here // 4), (samples_here + sections - 1) // sections)
    tap_keep = tap_mask(section % 3)[:, None]
    map_side = feature_maps.shape[1]
    channels = feature_maps.shape[3]
    current = feature_maps
    layer_at = 0
    routing = dispatch_table(path_lists[layer_at, :, 0], sections, capacity)
    outgoing = jnp.einsum(
        "ks,shwc->khwc", routing, current, preferred_element_type=jnp.float32
    ).astype(jnp.bfloat16)
    outgoing = outgoing.reshape(sections, capacity, map_side, map_side, channels)
    kernel = depth_kernel[layer_at, 0] * tap_keep
    results, received = apply_block(
        lax.all_to_all(outgoing, "segment", split_axis=0, concat_axis=0, tiled=True),
        pointwise=point_weight[layer_at, 0],
        kernel=kernel,
    )
    returned = lax.all_to_all(results, "segment", split_axis=0, concat_axis=0, tiled=True)
    returned = returned.reshape(-1, map_side, map_side, channels)
    current = jnp.einsum(
        "ks,khwc->shwc", routing, returned, preferred_element_type=jnp.float32
    ).astype(jnp.bfloat16)
    tables = [routing]
    stored = [received.reshape(-1, map_side, map_side, channels)]
    grad_maps = cotangent
    point_parts = []
    depth_parts = []
    for layer_at in reversed(range(LAYERS)):
        routing = tables[layer_at]
        outgoing = jnp.einsum(
            "ks,shwc->khwc", routing, grad_maps, preferred_element_type=jnp.float32
        ).astype(jnp.bfloat16)
        outgoing = outgoing.reshape(sections, capacity, map_side, map_side, channels)
        arriving = lax.all_to_all(outgoing, "segment", split_axis=0, concat_axis=0, tiled=True)
        arriving = arriving.reshape(-1, map_side, map_side, channels)
        kernel = depth_kernel[layer_at, 0] * tap_keep
        grad_in, active, flat_grads, depth_term = block_backward(
            stored[layer_at], arriving, point_weight[layer_at, 0], kernel
        )
        depth_parts.append(depth_term * tap_keep)
        point_parts.append(point_term(active, flat_grads))
        sendback = lax.all_to_all(
            grad_in.reshape(sections, capacity, map_side, map_side, channels),
            "segment",
            split_axis=0,
            concat_axis=0,
            tiled=True,
        )
        sendback = sendback.reshape(-1, map_side, map_side, channels)
        grad_maps = jnp.einsum(
            "ks,khwc->shwc", routing, sendback, preferred_element_type=jnp.float32
        ).astype(jnp.bfloat16)
    point_parts = point_parts[::-1]
    depth_parts = depth_parts[::-1]
    point_grad = lax.psum_scatter(jnp.stack(point_parts), "rep", scatter_dimension=1, tiled=True)
    depth_grad = lax.psum(jnp.stack(depth_parts), "rep")
    return (current, grad_maps, point_grad[:, None], depth_grad[:, None])


def solution(mesh):
    placed = (
        P(("segment", "rep"), None, None, None),
        P(None, ("segment", "rep"), None),
        P(None, "segment", None, None),
        P(None, "segment", None, None),
        P(("segment", "rep"), None, None, None),
    )
    return jax.shard_map(
        body,
        mesh=mesh,
        in_specs=placed,
        out_specs=(
            P(("segment", "rep"), None, None, None),
            P(("segment", "rep"), None, None, None),
            P(None, "segment", "rep", None),
            P(None, "segment", None, None),
        ),
        check_vma=False,
    )
```

profile of v0, /device:TPU:0, one launch (start us, length us, event | category | flops | bytes accessed | tf_op | source)
XLA Modules:
  0.0 247.4 jit_solution(6566931507070552726)
XLA Ops:
  7.2 1.0 convert_reduce_fusion
  8.2 0.7 multiply_add_fusion.1
  8.8 2.5 %convolution_convert_fusion.1 = bf16[8,7,7,1024]{3,0,2,1:T(8,128)(2,1)} fusion(bf16[8,7,7,1024]{3,0,2,1:T(8,128)(2,1)} %param.9, s32[8]{0:T(128)S(1)} %multiply_add_fusion.1), kind=kOutput, calls=%fused_computation.137 | convolution fusion | flops 6824000 | bytes 1605664 | tf_op jit(solution)/shard_map/ks,shwc->khwc/dot_general | solution.py:153
  11.4 1.7 reshape.517
  13.1 1.2 copy.34
  14.2 4.2 %all-to-all-start.2 = ((bf16[2,4,7,7,1024]{4,1,3,2,0:T(4,128)(2,1)}), bf16[2,4,7,7,1024]{4,1,3,2,0:T(4,128)(2,1)S(1)}, u32[]{:S(2)}, u32[]{:S(2)}) async-start(bf16[2,4,7,7,1024]{4,1,3,2,0:T(4,128)(2,1)} %copy.34), calls=%async_computation.2 | async-start | bytes 1605632 | tf_op jit(solution)/shard_map/all_to_all | solution.py:157
  18.5 2.5 %convolution_convert_fusion.3 = bf16[8,7,7,1024]{3,0,2,1:T(8,128)(2,1)} fusion(bf16[8,7,7,1024]{3,0,2,1:T(8,128)(2,1)} %param.5, s32[8]{0:T(128)S(1)} %multiply_add_fusion.1), kind=kOutput, calls=%fused_computation.139 | convolution fusion | flops 6824000 | bytes 1605664 | tf_op jit(solution)/shard_map/ks,shwc->khwc/dot_general | solution.py:131
  21.0 2.4 reshape.514
  23.4 2.3 copy.29
  25.7 0.1 bitcast_multiply_fusion
  25.8 4.4 %all-to-all-done.2 = bf16[2,4,7,7,1024]{4,1,3,2,0:T(4,128)(2,1)S(1)} async-done(((bf16[2,4,7,7,1024]{4,1,3,2,0:T(4,128)(2,1)}), bf16[2,4,7,7,1024]{4,1,3,2,0:T(4,128)(2,1)S(1)}, u32[]{:S(2)}, u32[]{:S(2)}) %all-to-all-start.2) | async-done | bytes 802848 | tf_op jit(solution)/shard_map/all_to_all | solution.py:157
  30.2 4.3 %all-to-all-start = ((bf16[2,4,7,7,1024]{4,1,3,2,0:T(4,128)(2,1)}), bf16[2,4,7,7,1024]{4,1,3,2,0:T(4,128)(2,1)}, u32[]{:S(2)}, u32[]{:S(2)}) async-start(bf16[2,4,7,7,1024]{4,1,3,2,0:T(4,128)(2,1)} %copy.29), calls=%async_computation | async-start | bytes 1605632 | tf_op jit(solution)/shard_map/all_to_all | solution.py:137
  34.6 0.2 all-reduce.4.cloned.1.call-start
  34.9 1.3 copy.35
  36.2 2.3 reshape.518
  38.5 1.2 copy.39
  39.7 2.2 reshape_reshape.3
  41.9 3.4 %all-to-all-done = bf16[2,4,7,7,1024]{4,1,3,2,0:T(4,128)(2,1)} async-done(((bf16[2,4,7,7,1024]{4,1,3,2,0:T(4,128)(2,1)}), bf16[2,4,7,7,1024]{4,1,3,2,0:T(4,128)(2,1)}, u32[]{:S(2)}, u32[]{:S(2)}) %all-to-all-start) | async-done | bytes 802848 | tf_op jit(solution)/shard_map/all_to_all | solution.py:137
  45.3 2.8 %copy.30 = f32[2,4,7,7,1024]{4,1,0,3,2:T(4,128)} copy(bf16[2,4,7,7,1024]{4,1,3,2,0:T(4,128)(2,1)} %all-to-all-done) | data formatting | bytes 2408448 | tf_op jit(solution)/shard_map/convert_element_type | solution.py:65
  48.1 2.8 %reshape.522 = f32[8,7,7,1024]{3,0,2,1:T(8,128)} reshape(f32[2,4,7,7,1024]{4,1,0,3,2:T(4,128)} %copy.30) | data formatting | bytes 3211264 | tf_op jit(solution)/shard_map/convert_element_type | solution.py:65
  50.9 14.2 %multiply_reduce_fusion.26 = (f32[8,7,7]{0,2,1:T(8,128)S(1)}, f32[8,7,7,1024]{3,0,2,1:T(8,128)S(1)}) fusion(f32[1024]{0:T(1024)S(1)} %bitcast.129, f32[1024]{0:T(1024)S(1)} %bitcast.131, f32[1024]{0:T(1024)S(1)} %bitcast.133, f32[1024]{0:T(1024)S(1)} %bitcast.135, f32[1024]{0:T(1024)S(1)} %bitcast.137, f32[1024]{0:T(1024)S(1)} %bitcast.139, ...), kind=kLoop, calls=%fused_computation.134 | loop fusion | flops 20471416 | bytes 3315232 | tf_op jit(solution)/shard_map/reduce_sum | solution.py:67
  65.1 2.4 multiply_convert_fusion
  67.5 3.1 %multiply_reduce_fusion = (f32[1024]{0:T(1024)S(1)}, f32[1024]{0:T(1024)S(1)}, f32[1024]{0:T(1024)S(1)}, f32[1024]{0:T(1024)S(1)}, f32[1024]{0:T(1024)S(1)}, /*i...) fusion(f32[8,7,7,1024]{3,0,2,1:T(8,128)S(1)} %copy-done.1, ...), kind=kLoop, calls=%fused_computation.103 | loop fusion | flops 16037888 | bytes 6499392 | tf_op jit(solution)/shard_map/reduce_sum | solution.py:54
  70.7 1.1 multiply_reduce_fusion.18
  71.8 0.1 copy-done.2
  72.2 0.8 multiply_bitcast_fusion
  73.0 0.3 reduce-scatter.2.cloned.1.call-start
  73.3 1.6 copy.38
  74.9 1.2 reshape.521
  76.0 4.6 %convolution_bitcast_fusion = f32[1,1024,1024]{2,1,0:T(8,128)} fusion(bf16[392,1024]{1,0:T(8,128)(2,1)} %reshape.521, bf16[392,1024]{1,0:T(8,128)(2,1)} %reshape_reshape.3), kind=kOutput, calls=%fused_computation.48 | convolution fusion | flops 822083584 | bytes 5799936 | tf_op jit(solution)/shard_map/dot_general | solution.py:96
  80.6 3.0 %add_convert_fusion = bf16[8,7,7,1024]{3,0,2,1:T(8,128)(2,1)S(1)} fusion(f32[8,7,7,1024]{3,0,2,1:T(8,128)} %reshape.522, bf16[1,1,1024,1024]{3,2,1,0:T(8,128)(2,1)S(1)} %copy-done, f32[8,7,7,1024]{3,0,2,1:T(8,128)} %copy-done.3, f32[8,7,7]{0,2,1:T(8,128)S(1)} %add_rsqrt_fusion), kind=kOutput, calls=%fused_computation.131 | convolution fusion | flops 825294848 | bytes 6112800 | tf_op jit(solution)/shard_map/dot_general | solution.py:69
  83.6 1.2 reshape.515
  84.8 2.4 copy.31
  87.2 4.3 %all-to-all-start.1 = ((bf16[2,4,7,7,1024]{4,1,3,2,0:T(4,128)(2,1)}), bf16[2,4,7,7,1024]{4,1,3,2,0:T(4,128)(2,1)}, u32[]{:S(2)}, u32[]{:S(2)}) async-start(bf16[2,4,7,7,1024]{4,1,3,2,0:T(4,128)(2,1)} %copy.31), calls=%async_computation.1 | async-start | bytes 1605632 | tf_op jit(solution)/shard_map/all_to_all | solution.py:141
  91.5 15.0 %fusion.51 = bf16[8,7,7,1024]{3,0,2,1:T(8,128)(2,1)} fusion(f32[8,7,7,1024]{3,0,2,1:T(8,128)} %copy-done.2, bf16[8,7,7,1024]{3,0,2,1:T(8,128)(2,1)S(1)} %copy-done.5, f32[1024]{0:T(1024)S(1)} %bitcast.130, f32[1024]{0:T(1024)S(1)} %bitcast.132, f32[1024]{0:T(1024)S(1)} %bitcast.134, f32[1024]{0:T(1024)S(1)} %bitcast.136, f32[1024]{0:T(1024)S(1)} %bitcast.138, ...), kind=kLoop, calls=%fused_computation.100 | loop fusion | flops 20873216 | bytes 3313664 | tf_op jit(solution)/shard_map/convert_element_type | solution.py:89
  106.5 1.7 reshape.519
  108.2 1.2 copy.36
  109.4 3.5 %all-to-all-start.3 = ((bf16[2,4,7,7,1024]{4,1,3,2,0:T(4,128)(2,1)}), bf16[2,4,7,7,1024]{4,1,3,2,0:T(4,128)(2,1)S(1)}, u32[]{:S(2)}, u32[]{:S(2)}) async-start(bf16[2,4,7,7,1024]{4,1,3,2,0:T(4,128)(2,1)} %copy.36), calls=%async_computation.3 | async-start | bytes 1605632 | tf_op jit(solution)/shard_map/all_to_all | solution.py:165
  112.9 2.5 %copy.32 = bf16[2,4,7,7,1024]{4,1,0,3,2:T(4,128)(2,1)} copy(bf16[2,4,7,7,1024]{4,1,3,2,0:T(4,128)(2,1)} %all-to-all-done.1) | data formatting | bytes 1605632 | tf_op jit(solution)/shard_map/all_to_all | solution.py:141
  115.4 2.3 reshape.516
  117.7 5.1 %all-to-all-done.3 = bf16[2,4,7,7,1024]{4,1,3,2,0:T(4,128)(2,1)S(1)} async-done(((bf16[2,4,7,7,1024]{4,1,3,2,0:T(4,128)(2,1)}), bf16[2,4,7,7,1024]{4,1,3,2,0:T(4,128)(2,1)S(1)}, u32[]{:S(2)}, u32[]{:S(2)}) %all-to-all-start.3) | async-done | bytes 802848 | tf_op jit(solution)/shard_map/all_to_all | solution.py:165
  122.7 1.3 copy.37
  124.1 2.3 reshape.520
  126.4 1.3 convolution_convert_fusion.2
  127.7 1.3 convolution_convert_fusion
  129.0 30.3 %all-reduce.4.cloned.1.call-done = f32[1,1,25,1024]{3,1,2,0:T(1,128)} async-done(((f32[1,1,25,1024]{3,1,2,0:T(1,128)}), f32[1,1,25,1024]{3,1,2,0:T(1,128)}) %all-reduce.4.cloned.1.call-update) | async-done | bytes 102416 | tf_op jit(solution)/shard_map/psum | solution.py:179
  159.4 79.6 %reduce-scatter.2.cloned.1.call-done = f32[1,64,1024]{2,1,0:T(8,128)} async-done(((f32[1,1024,1024]{2,1,0:T(8,128)}), f32[1,64,1024]{2,1,0:T(8,128)}) %reduce-scatter.2.cloned.1.call-update) | async-done | bytes 262160 | tf_op jit(solution)/shard_map/reduce_scatter | solution.py:178
  239.0 1.5 copy.73
  (50 shorter events, 0.4 us)
Async XLA Ops:
  7.2 58.0 %copy-start = (bf16[1,1,1024,1024]{3,2,1,0:T(8,128)(2,1)S(1)}, bf16[1,1,1024,1024]{3,2,1,0:T(8,128)(2,1)}, u32[]{:S(2)}) copy-start(bf16[1,1,1024,1024]{3,2,1,0:T(8,128)(2,1)} %param.7) | copy-start | bytes 6291460
  14.2 16.0 %all-to-all-start.2 = ((bf16[2,4,7,7,1024]{4,1,3,2,0:T(4,128)(2,1)}), bf16[2,4,7,7,1024]{4,1,3,2,0:T(4,128)(2,1)S(1)}, u32[]{:S(2)}, u32[]{:S(2)}) async-start(bf16[2,4,7,7,1024]{4,1,3,2,0:T(4,128)(2,1)} %copy.34), calls=%async_computation.2 | async-start | bytes 1605632 | tf_op jit(solution)/shard_map/all_to_all | solution.py:157
  21.0 4.8 %copy-start.8 = (f32[1,1,25,1024]{3,1,2,0:T(1,128)S(1)}, f32[1,1,25,1024]{3,1,2,0:T(1,128)}, u32[]{:S(2)}) copy-start(f32[1,1,25,1024]{3,1,2,0:T(1,128)} %param.8) | copy-start | bytes 307204
  30.2 15.1 %all-to-all-start = ((bf16[2,4,7,7,1024]{4,1,3,2,0:T(4,128)(2,1)}), bf16[2,4,7,7,1024]{4,1,3,2,0:T(4,128)(2,1)}, u32[]{:S(2)}, u32[]{:S(2)}) async-start(bf16[2,4,7,7,1024]{4,1,3,2,0:T(4,128)(2,1)} %copy.29), calls=%async_computation | async-start | bytes 1605632 | tf_op jit(solution)/shard_map/all_to_all | solution.py:137
  34.6 124.8 %all-reduce.4.cloned.1.call-start = ((), (), s32[]{:S(2)}) async-start(), calls=%async_computation.6 | async-start | bytes 204800 | tf_op jit(solution)/shard_map/psum | solution.py:179
  50.9 14.3 %copy-start.4 = (bf16[8,7,7,1024]{3,0,2,1:T(8,128)(2,1)S(1)}, bf16[8,7,7,1024]{3,0,2,1:T(8,128)(2,1)}, u32[]{:S(2)}) copy-start(bf16[8,7,7,1024]{3,0,2,1:T(8,128)(2,1)} %reshape.518) | copy-start | bytes 2408452
  65.1 2.4 copy-start.3
  65.1 2.4 copy-start.1
  70.6 1.3 copy-start.2
  73.0 166.0 %reduce-scatter.2.cloned.1.call-start = ((), (), s32[]{:S(2)}) async-start(), calls=%async_computation.5 | async-start | bytes 4456448 | tf_op jit(solution)/shard_map/reduce_scatter | solution.py:178
  84.8 6.7 %copy-start.5 = (bf16[8,7,7,1024]{3,0,2,1:T(8,128)(2,1)S(1)}, bf16[8,7,7,1024]{3,0,2,1:T(8,128)(2,1)}, u32[]{:S(2)}) copy-start(bf16[8,7,7,1024]{3,0,2,1:T(8,128)(2,1)} %reshape.518) | copy-start | bytes 2408452
  87.2 22.2 %all-to-all-start.1 = ((bf16[2,4,7,7,1024]{4,1,3,2,0:T(4,128)(2,1)}), bf16[2,4,7,7,1024]{4,1,3,2,0:T(4,128)(2,1)}, u32[]{:S(2)}, u32[]{:S(2)}) async-start(bf16[2,4,7,7,1024]{4,1,3,2,0:T(4,128)(2,1)} %copy.31), calls=%async_computation.1 | async-start | bytes 1605632 | tf_op jit(solution)/shard_map/all_to_all | solution.py:141
  109.4 13.4 %all-to-all-start.3 = ((bf16[2,4,7,7,1024]{4,1,3,2,0:T(4,128)(2,1)}), bf16[2,4,7,7,1024]{4,1,3,2,0:T(4,128)(2,1)S(1)}, u32[]{:S(2)}, u32[]{:S(2)}) async-start(bf16[2,4,7,7,1024]{4,1,3,2,0:T(4,128)(2,1)} %copy.36), calls=%async_computation.3 | async-start | bytes 1605632 | tf_op jit(solution)/shard_map/all_to_all | solution.py:165
  124.1 2.3 copy-start.6
  126.4 1.3 copy-start.7
Sparse Core Ops, SparseCore 0:
  73.1 86.2 all-reduce.3
  163.8 75.1 reduce-scatter.1
where the time goes:
time: 248 us; the launch traced here: 247 us
  waiting for transfers between devices  123 us (50%)
  local copies, waits for them, and re-layouts  39.8 us (16%)
  other arithmetic  36 us (15%)
  matrix products  17.6 us (7%)
  starting transfers between devices  16.9 us (7%)
  between operations  14.3 us (6%)
    reduce_scatter x1, waiting for transfers between devices, body(): lax.psum_scatter(jnp.stack(point_parts), 'rep', scatter_dimension=1, tile...  79.6 us
    psum x1, waiting for transfers between devices, body(): depth_grad = lax.psum(jnp.stack(depth_parts), 'rep')  30.3 us
    convert_element_type x1, other arithmetic, block_backward(): (grad_maps.astype(jnp.float32) + depthwise_back(grad_mixed, kernel)).asty...  15 us
    reduce_sum x1, other arithmetic, block_forward(): jnp.mean(mixed_taps * mixed_taps, axis=-1, keepdims=True) + EPS  14.2 us
    all_to_all x2, starting transfers between devices, body(): lax.all_to_all(outgoing, 'segment', split_axis=0, concat_axis=0, tiled=True)  8.56 us
    all_to_all x2, waiting for transfers between devices, body(): lax.all_to_all(outgoing, 'segment', split_axis=0, concat_axis=0, tiled=True)  7.81 us
    reshape x4, local copies, waits for them, and re-layouts, body(): outgoing.reshape(sections, capacity, map_side, map_side, channels)  7.58 us
    convert_element_type x2, local copies, waits for them, and re-layouts, block_forward(): source = inputs.astype(jnp.float32)  5.57 us
  transfers between devices with their start and end apart: 6, of which 5 were waited for; matrix products, arithmetic and copies ran while one was open for 23% of the time, Pallas kernels for 0%

commit v1 on v0

v1 whole, which is shorter than its diff:
```python
import functools

import jax
import jax.numpy as jnp
from jax import lax
from jax.experimental import pallas as pl
from jax.experimental.pallas import tpu as pltpu
from jax.sharding import PartitionSpec as P

EPS = 1e-05
LANES = 128
F32 = jnp.float32
BF16 = jnp.bfloat16

VMEM = pl.BlockSpec(memory_space=pltpu.VMEM)
SMEM = pl.BlockSpec(memory_space=pltpu.SMEM)


def iota2(shape, axis):
    return lax.broadcasted_iota(jnp.int32, shape, axis)


def split(value, size):
    if size & (size - 1) == 0:
        return value >> (size.bit_length() - 1), value & (size - 1)
    quotient = lax.div(value, jnp.int32(size))
    return quotient, value - quotient * size


def slot_codes(path_ref, samples, capacity):
    names = [path_ref[i] for i in range(samples)]
    codes = []
    for i in range(samples):
        rank = jnp.int32(0)
        for j in range(i):
            rank = rank + jnp.where(names[j] == names[i], 1, 0)
        codes.append(names[i] * capacity + rank)
    return codes


def spread_codes(codes, which):
    out = jnp.zeros(which.shape, jnp.int32)
    for i, code in enumerate(codes):
        out = jnp.where(which == i, code, out)
    return out


def one_hot(mask):
    return jnp.where(mask, 1.0, 0.0).astype(BF16)


def pick(matrix, rows):
    return lax.dot_general(matrix, rows, (((1,), (0,)), ((), ())), preferred_element_type=F32)


def pack_kernel(path_ref, at_ref, maps_ref, *out_refs, sizes):
    places, samples, sections, capacity = sizes
    codes = slot_codes(path_ref, samples, capacity)
    shape = (places * capacity, places * samples)
    row_place, row_slot = split(iota2(shape, 0), capacity)
    col = iota2((1, places * samples), 1)
    col_place, col_sample = split(col, samples)
    col_code = spread_codes(codes, col_sample)
    for shift in range(1, sections):
        target = lax.rem(at_ref[0] + shift, sections)
        mask = (row_place == col_place) & (col_code == target * capacity + row_slot)
        out_refs[shift - 1][...] = pick(one_hot(mask), maps_ref[...]).astype(BF16)


def gather_slots(path_ref, at_ref, maps_ref, got_refs, sizes):
    places, samples, sections, capacity = sizes
    slots = sections * capacity
    codes = slot_codes(path_ref, samples, capacity)
    shape = (places * slots, places * samples)
    row_place, row_slot = split(iota2(shape, 0), slots)
    col_place, col_sample = split(iota2((1, places * samples), 1), samples)
    col_code = spread_codes(codes, col_sample)
    mask = (
        (row_place == col_place)
        & (row_slot < capacity)
        & (col_code == at_ref[0] * capacity + row_slot)
    )
    total = pick(one_hot(mask), maps_ref[...])
    shape = (places * slots, places * capacity)
    row_place, row_slot = split(iota2(shape, 0), slots)
    col_place, col_slot = split(iota2((1, places * capacity), 1), capacity)
    for shift in range(1, sections):
        mask = (row_place == col_place) & (row_slot == shift * capacity + col_slot)
        total = total + pick(one_hot(mask), got_refs[shift - 1][...])
    return total


def return_slots(slot_rows, out_refs, sizes):
    places, samples, sections, capacity = sizes
    slots = sections * capacity
    shape = (places * capacity, places * slots)
    row_place, row_slot = split(iota2(shape, 0), capacity)
    col_place, col_slot = split(iota2((1, places * slots), 1), slots)
    for shift in range(1, sections):
        mask = (row_place == col_place) & (col_slot == shift * capacity + row_slot)
        out_refs[shift - 1][...] = pick(one_hot(mask), slot_rows).astype(BF16)


def unpack_kernel(path_ref, at_ref, slots_ref, *refs, sizes):
    places, samples, sections, capacity = sizes
    slots = sections * capacity
    got_refs, out_ref = refs[:-1], refs[-1]
    codes = slot_codes(path_ref, samples, capacity)
    row = iota2((places * samples, 1), 0)
    row_place, row_sample = split(row, samples)
    row_code = spread_codes(codes, row_sample)
    col_place, col_slot = split(iota2((places * samples, places * slots), 1), slots)
    mask = (
        (row_place == col_place)
        & (col_slot < capacity)
        & (row_code == at_ref[0] * capacity + col_slot)
    )
    total = pick(one_hot(mask), slots_ref[...])
    col_place, col_slot = split(iota2((places * samples, places * capacity), 1), capacity)
    for shift in range(1, sections):
        target = lax.rem(at_ref[0] + shift, sections)
        mask = (row_place == col_place) & (row_code == target * capacity + col_slot)
        total = total + pick(one_hot(mask), got_refs[shift - 1][...])
    out_ref[...] = total.astype(BF16)


def tap_keep(kind, tap):
    row_shift, col_shift = tap // 5 - 2, tap % 5 - 2
    narrow = abs(row_shift) <= 1 and abs(col_shift) <= 1
    spaced = row_shift % 2 == 0 and col_shift % 2 == 0
    keep = kind == 1
    if narrow:
        keep = keep | (kind == 0)
    if spaced:
        keep = keep | (kind == 2)
    return jnp.where(keep, 1.0, 0.0).astype(F32)


def correlate(source_ref, kernel_ref, kind, side, slots, sign, emit):
    channels = source_ref.shape[-1]

    def chunk(at, carry):
        lanes = pl.ds(pl.multiple_of(at * LANES, LANES), LANES)
        taps = [
            jnp.broadcast_to(kernel_ref[tap, :, lanes], (slots, LANES)) * tap_keep(kind, tap)
            for tap in range(25)
        ]
        for row in range(side):
            sums = [None] * side
            for row_shift in range(-2, 3):
                source_row = row + sign * row_shift
                if not 0 <= source_row < side:
                    continue
                cells = [
                    source_ref[pl.ds((source_row * side + col) * slots, slots), lanes]
                    for col in range(side)
                ]
                for col_shift in range(-2, 3):
                    tap = taps[(row_shift + 2) * 5 + col_shift + 2]
                    for col in range(side):
                        source_col = col + sign * col_shift
                        if not 0 <= source_col < side:
                            continue
                        term = tap * cells[source_col]
                        sums[col] = term if sums[col] is None else sums[col] + term
            for col in range(side):
                emit(pl.ds((row * side + col) * slots, slots), lanes, sums[col])
        return carry

    lax.fori_loop(0, channels // LANES, chunk, 0)


def forward_kernel(path_ref, at_ref, maps_ref, weight_ref, kernel_ref, *refs, sizes, side):
    places, samples, sections, capacity = sizes
    slots = sections * capacity
    got_refs, refs = refs[: sections - 1], refs[sections - 1 :]
    back_refs, refs = refs[: sections - 1], refs[sections - 1 :]
    final_ref, active_ref, scaled_ref, inverse_ref, source_ref = refs
    kind = lax.rem(at_ref[0], 3)
    source_ref[...] = gather_slots(path_ref, at_ref, maps_ref, got_refs, sizes)

    def emit(rows, lanes, value):
        scaled_ref[rows, lanes] = value

    correlate(source_ref, kernel_ref, kind, side, slots, 1, emit)
    block = side * slots
    for row in range(side):
        rows = pl.ds(row * block, block)
        mixed = scaled_ref[rows, :]
        inverse = lax.rsqrt(jnp.mean(mixed * mixed, axis=-1, keepdims=True) + EPS)
        scaled = mixed * inverse
        scaled_ref[rows, :] = scaled
        inverse_ref[rows, :] = jnp.broadcast_to(inverse, (block, LANES))
        active_ref[rows, :] = (scaled * jax.nn.sigmoid(scaled)).astype(BF16)
    branch = pick(active_ref[...], weight_ref[...])
    final_ref[...] = (source_ref[...] + branch).astype(BF16)
    return_slots(final_ref[...], back_refs, sizes)


def point_kernel(path_ref, at_ref, grads_ref, active_ref, *refs, sizes, ways):
    places, samples, sections, capacity = sizes
    got_refs, refs = refs[: sections - 1], refs[sections - 1 :]
    slot_grads_ref, send_ref, keep_ref, total_ref = refs
    slot_grads_ref[...] = gather_slots(path_ref, at_ref, grads_ref, got_refs, sizes).astype(BF16)
    total = lax.dot_general(
        active_ref[...], slot_grads_ref[...], (((0,), (0,)), ((), ())), preferred_element_type=F32
    )
    rows = total.shape[0] // ways
    total_ref[...] = total.reshape(ways, rows, total.shape[1])
    low = at_ref[1] & 1
    for at in range(ways // 2):
        send_ref[at] = total_ref[2 * at + 1 - low].astype(BF16)
        keep_ref[at] = total_ref[2 * at + low]


def fold_kernel(at_ref, keep_ref, got_ref, send_ref, left_ref, *, stride, bit):
    count = keep_ref.shape[0]
    mine = (at_ref[1] // bit) & 1
    at = 0
    for base in range(0, count, 2 * stride):
        for offset in range(stride):
            give = base + offset + stride * (1 - mine)
            hold = base + offset + stride * mine
            send_ref[at] = (keep_ref[give] + got_ref[give].astype(F32)).astype(BF16)
            left_ref[at] = keep_ref[hold] + got_ref[hold].astype(F32)
            at += 1


def last_kernel(keep_a_ref, got_a_ref, keep_b_ref, got_b_ref, out_ref):
    half = keep_a_ref.shape[-1]
    out_ref[:, :half] = keep_a_ref[0] + got_a_ref[0].astype(F32)
    out_ref[:, half:] = keep_b_ref[0] + got_b_ref[0].astype(F32)


def backward_kernel(
    at_ref, slot_grads_ref, weight_ref, kernel_ref, scaled_ref, inverse_ref, *refs, sizes, side
):
    places, samples, sections, capacity = sizes
    slots = sections * capacity
    back_refs, refs = refs[: sections - 1], refs[sections - 1 :]
    grad_in_ref, mixed_ref, work_ref = refs
    kind = lax.rem(at_ref[0], 3)
    work_ref[...] = lax.dot_general(
        slot_grads_ref[...], weight_ref[...], (((1,), (1,)), ((), ())), preferred_element_type=F32
    )
    block = side * slots
    for row in range(side):
        rows = pl.ds(row * block, block)
        scaled = scaled_ref[rows, :]
        logistic = jax.nn.sigmoid(scaled)
        grad_scaled = work_ref[rows, :] * logistic * (1.0 + scaled * (1.0 - logistic))
        mean = jnp.mean(grad_scaled * scaled, axis=-1, keepdims=True)
        mixed_ref[rows, :] = inverse_ref[rows, :1] * (grad_scaled - scaled * mean)

    def emit(rows, lanes, value):
        work_ref[rows, lanes] = value

    correlate(mixed_ref, kernel_ref, kind, side, slots, -1, emit)
    grad_in_ref[...] = (slot_grads_ref[...].astype(F32) + work_ref[...]).astype(BF16)
    return_slots(grad_in_ref[...], back_refs, sizes)


def taps_kernel(at_ref, mixed_ref, source_ref, out_ref, *, side, slots):
    kind = lax.rem(at_ref[0], 3)
    channels = mixed_ref.shape[-1]

    def chunk(at, carry):
        lanes = pl.ds(pl.multiple_of(at * LANES, LANES), LANES)

        def cells(ref, row):
            return [ref[pl.ds((row * side + col) * slots, slots), lanes] for col in range(side)]

        sums = [None] * 25
        for row in range(side):
            grads = cells(mixed_ref, row)
            for row_shift in range(-2, 3):
                if not 0 <= row + row_shift < side:
                    continue
                source = cells(source_ref, row + row_shift)
                for col_shift in range(-2, 3):
                    tap = (row_shift + 2) * 5 + col_shift + 2
                    for col in range(side):
                        if not 0 <= col + col_shift < side:
                            continue
                        term = grads[col] * source[col + col_shift]
                        sums[tap] = term if sums[tap] is None else sums[tap] + term
        for tap in range(25):
            out_ref[tap, :, lanes] = (
                jnp.sum(sums[tap], axis=0, keepdims=True) * tap_keep(kind, tap)
            )
        return carry

    lax.fori_loop(0, channels // LANES, chunk, 0)


def call(kernel, name, outs, in_specs, scratch=()):
    return pl.pallas_call(
        kernel,
        out_shape=outs,
        in_specs=in_specs,
        out_specs=jax.tree.map(lambda _: VMEM, outs),
        scratch_shapes=list(scratch),
        compiler_params=pltpu.CompilerParams(vmem_limit_bytes=56 * 1024 * 1024),
        name=name,
    )


def body(feature_maps, path_lists, point_weight, depth_kernel, cotangent):
    sections = lax.axis_size("segment")
    ways = lax.axis_size("rep")
    section = lax.axis_index("segment").astype(jnp.int32)
    replica = lax.axis_index("rep").astype(jnp.int32)
    samples, side, _, channels = feature_maps.shape
    places = side * side
    capacity = max(max(2, samples // 4), (samples + sections - 1) // sections)
    slots = sections * capacity
    sizes = (places, samples, sections, capacity)
    at = jnp.stack([section, replica])
    path = path_lists[0, :, 0]
    weight = point_weight[0, 0]
    kernel = depth_kernel[0, 0].reshape(25, 1, channels)
    others = range(1, sections)

    def rows_of(maps):
        return jnp.transpose(maps, (1, 2, 0, 3)).reshape(places * samples, channels)

    def maps_of(rows):
        return jnp.transpose(rows.reshape(side, side, samples, channels), (2, 0, 1, 3))

    def shape(*dims, dtype=F32):
        return jax.ShapeDtypeStruct(dims, dtype)

    packed = shape(places * capacity, channels, dtype=BF16)

    def pack(rows):
        return call(
            functools.partial(pack_kernel, sizes=sizes),
            "pack",
            [packed for _ in others],
            [SMEM, SMEM, VMEM],
        )(path, at, rows)

    def swap(pieces, direction):
        return [
            lax.ppermute(
                piece,
                "segment",
                [(i, (i + direction * shift) % sections) for i in range(sections)],
            )
            for shift, piece in zip(others, pieces)
        ]

    def unpack(slot_rows, pieces):
        return call(
            functools.partial(unpack_kernel, sizes=sizes),
            "unpack",
            shape(places * samples, channels, dtype=BF16),
            [SMEM, SMEM, VMEM] + [VMEM for _ in others],
        )(path, at, slot_rows, *pieces)

    def trade(value, bit):
        return lax.ppermute(value, "rep", [(i, i ^ bit) for i in range(ways)])

    maps, grads = rows_of(feature_maps), rows_of(cotangent)
    got_maps = swap(pack(maps), 1)
    got_grads = swap(pack(grads), 1)

    slot_shape = shape(places * slots, channels)
    slot_half = shape(places * slots, channels, dtype=BF16)
    results = call(
        functools.partial(forward_kernel, sizes=sizes, side=side),
        "forward",
        [packed for _ in others]
        + [slot_half, slot_half, slot_shape, shape(places * slots, LANES), slot_shape],
        [SMEM, SMEM, VMEM, VMEM, VMEM] + [VMEM for _ in others],
    )(path, at, maps, weight, kernel, *got_maps)
    back = results[: sections - 1]
    slot_final, active, scaled, inverse, source = results[sections - 1 :]
    got_final = swap(back, -1)

    block = channels // ways
    slot_grads, send, keep = call(
        functools.partial(point_kernel, sizes=sizes, ways=ways),
        "point",
        [slot_half, shape(ways // 2, block, channels, dtype=BF16), shape(ways // 2, block, channels)],
        [SMEM, SMEM, VMEM, VMEM] + [VMEM for _ in others],
        [pltpu.VMEM((ways, block, channels), F32)],
    )(path, at, grads, active, *got_grads)

    got = trade(send, 1)

    results = call(
        functools.partial(backward_kernel, sizes=sizes, side=side),
        "backward",
        [packed for _ in others] + [slot_half, slot_shape],
        [SMEM, VMEM, VMEM, VMEM, VMEM, VMEM],
        [pltpu.VMEM((places * slots, channels), F32)],
    )(at, slot_grads, weight, kernel, scaled, inverse)
    back = results[: sections - 1]
    slot_in, mixed = results[sections - 1 :]
    got_in = swap(back, -1)

    taps = call(
        functools.partial(taps_kernel, side=side, slots=slots),
        "taps",
        shape(25, 1, channels),
        [SMEM, VMEM, VMEM],
    )(at, mixed, source)

    bits = [1 << i for i in range(1, ways.bit_length() - 1)]
    half = channels // 2
    finished = []
    for part in range(2):
        order = list(bits)
        if part == 1 and len(order) > 1:
            order[0], order[1] = order[1], order[0]
        left = list(bits)
        columns = slice(part * half, (part + 1) * half)
        keep_part, got_part = keep[:, :, columns], got[:, :, columns]
        for bit in order:
            stride = 1
            for other in left:
                if other < bit:
                    stride *= 2
            left.remove(bit)
            count = keep_part.shape[0] // 2
            send_part, keep_part = call(
                functools.partial(fold_kernel, stride=stride, bit=bit),
                "fold",
                [shape(count, block, half, dtype=BF16), shape(count, block, half)],
                [SMEM, VMEM, VMEM],
            )(at, keep_part, got_part)
            got_part = trade(send_part, bit)
        finished += [keep_part, got_part]
    point_grad = call(
        last_kernel, "last", shape(block, channels), [VMEM, VMEM, VMEM, VMEM]
    )(*finished)

    for bit in [1] + bits:
        taps = taps + trade(taps, bit)

    final_maps = maps_of(unpack(slot_final, got_final))
    input_grad = maps_of(unpack(slot_in, got_in))
    return (
        final_maps,
        input_grad,
        point_grad.reshape(1, 1, block, channels),
        taps.reshape(1, 1, 25, channels),
    )


def solution(mesh):
    placed = (
        P(("segment", "rep"), None, None, None),
        P(None, ("segment", "rep"), None),
        P(None, "segment", None, None),
        P(None, "segment", None, None),
        P(("segment", "rep"), None, None, None),
    )
    return jax.shard_map(
        body,
        mesh=mesh,
        in_specs=placed,
        out_specs=(
            P(("segment", "rep"), None, None, None),
            P(("segment", "rep"), None, None, None),
            P(None, "segment", "rep", None),
            P(None, "segment", None, None),
        ),
        check_vma=False,
    )
```

time: 248 us -> 95.4 us (0.38)
  waiting for transfers between devices: 123 us -> 14.7 us
  Pallas kernels: 0 us -> 50.1 us
  other arithmetic: 36 us -> 1.74 us
  local copies, waits for them, and re-layouts: 39.8 us -> 9.11 us
  matrix products: 17.6 us -> 0 us
  between operations: 14.3 us -> 0.68 us
    reduce_scatter x1 -> x0, waiting for transfers between devices: 79.6 us -> none  [body(): lax.psum_scatter(jnp.stack(point_parts), 'rep', scatter_dimension=1, tile...]
    pallas_call x0 -> x15, Pallas kernels: none -> 50.1 us  [the longest x6 12 us: body(): call(functools.partial(fold_kernel, stride=stride, bit=bit), 'fold', [sha...]
    psum x1 -> x0, waiting for transfers between devices: 30.3 us -> none  [body(): depth_grad = lax.psum(jnp.stack(depth_parts), 'rep')]
    reshape x12 -> x0, local copies, waits for them, and re-layouts: 22.1 us -> none  [the longest x4 7.58 us: body(): outgoing.reshape(sections, capacity, map_side, map_side, channels)]
    reduce_sum x4 -> x0, other arithmetic: 19.4 us -> none  [the longest x1 14.2 us: block_forward(): jnp.mean(mixed_taps * mixed_taps, axis=-1, keepdims=True) + EPS]
    ppermute x0 -> x15, starting transfers between devices: none -> 18.7 us  [the longest x11 13.6 us: trade(): return lax.ppermute(value, 'rep', [(i, i ^ bit) for i in range(ways)])]
    dot_general x7 -> x0, matrix products: 17.6 us -> none  [the longest x1 4.6 us: point_term(): lax.dot_general(active, flat_grads, (((0,), (0,)), ((), ())), preferred_e...]
    all_to_all x4 -> x0, starting transfers between devices: 16.4 us -> none  [the longest x2 8.56 us: body(): lax.all_to_all(outgoing, 'segment', split_axis=0, concat_axis=0, tiled=True)]
  transfers between devices with their start and end apart: 6 -> 15, of which waited for: 5 -> 5; matrix products, arithmetic and copies ran while one was open for 23% -> 4% of each run, Pallas kernels for 0% -> 43%
where the time goes in v1:
time: 95.4 us; the launch traced here: 95 us
  Pallas kernels  50.1 us (53%)
  starting transfers between devices  18.7 us (20%)
  waiting for transfers between devices  14.7 us (15%)
  local copies, waits for them, and re-layouts  9.11 us (10%)
  other arithmetic  1.74 us (2%)
    ppermute x11, starting transfers between devices, trade(): return lax.ppermute(value, 'rep', [(i, i ^ bit) for i in range(ways)])  13.6 us
    pallas_call x6, Pallas kernels, body(): call(functools.partial(fold_kernel, stride=stride, bit=bit), 'fold', [sha...  12 us
    ppermute x4, waiting for transfers between devices, swap(): lax.ppermute(piece, 'segment', [(i, (i + direction * shift) % sections) f...  8.35 us
    pallas_call x1, Pallas kernels, body(): call(functools.partial(backward_kernel, sizes=sizes, side=side), 'backwar...  7.46 us
    pallas_call x1, Pallas kernels, body(): call(functools.partial(forward_kernel, sizes=sizes, side=side), 'forward'...  7.01 us
    unnamed x26, local copies, waits for them, and re-layouts  6.41 us
    ppermute x11, waiting for transfers between devices, trade(): return lax.ppermute(value, 'rep', [(i, i ^ bit) for i in range(ways)])  6.31 us
    pallas_call x2, Pallas kernels, unpack(): call(functools.partial(unpack_kernel, sizes=sizes), 'unpack', shape(place...  6.04 us
  transfers between devices with their start and end apart: 15, of which 5 were waited for; matrix products, arithmetic and copies ran while one was open for 4% of the time, Pallas kernels for 43%

profile of v1, /device:TPU:0, one launch (start us, length us, event | category | flops | bytes accessed | tf_op | source)
XLA Modules:
  0.0 95.0 jit_solution(2662558550284568564)
XLA Ops:
  0.6 0.7 pad_add_fusion.at_ref
  1.3 2.3 %pack.2 = bf16[196,1024]{1,0:T(8,128)(2,1)} custom-call(s32[8]{0:T(128)} %bitcast.33, s32[2]{0:T(128)} %pad_add_fusion.at_ref, bf16[392,1024]{1,0:T(8,128)(2,1)} %bitcast.26), custom_call_target="tpu_custom_call" | custom-call | tf_op jit(solution)/shard_map/pack/pallas_call | solution.py:336
  3.6 3.0 %collective-permute-start = (bf16[196,1024]{1,0:T(8,128)(2,1)}, bf16[196,1024]{1,0:T(8,128)(2,1)S(1)}, u32[]{:S(2)}, u32[]{:S(2)}) collective-permute-start(bf16[196,1024]{1,0:T(8,128)(2,1)} %pack.2), channel_id=1, source_target_pairs={{0,16},{16,0},{1,17},{17,1},{2,18},{18,2},{3,19},{19,3},{4,20},{20... | collective-permute-start | bytes 1204232 | tf_op jit(solution)/shard_map/ppermute | solution.py:345
  6.6 2.3 %pack.3 = bf16[196,1024]{1,0:T(8,128)(2,1)} custom-call(s32[8]{0:T(128)} %bitcast.34, s32[2]{0:T(128)} %pad_add_fusion.at_ref, bf16[392,1024]{1,0:T(8,128)(2,1)} %bitcast.24), custom_call_target="tpu_custom_call" | custom-call | tf_op jit(solution)/shard_map/pack/pallas_call | solution.py:336
  8.9 8.2 %collective-permute-done.refs_0_ = bf16[196,1024]{1,0:T(8,128)(2,1)S(1)} collective-permute-done((bf16[196,1024]{1,0:T(8,128)(2,1)}, bf16[196,1024]{1,0:T(8,128)(2,1)S(1)}, u32[]{:S(2)}, u32[]{:S(2)}) %collective-permute-start) | collective-permute-done | bytes 401440 | tf_op jit(solution)/shard_map/ppermute | solution.py:345
  17.1 0.8 copy-done.4
  17.9 7.0 %forward.1 = (bf16[196,1024]{1,0:T(8,128)(2,1)}, bf16[392,1024]{1,0:T(8,128)(2,1)}, bf16[392,1024]{1,0:T(8,128)(2,1)}, f32[392,1024]{1,0:T(8,128)}, f32[392,128]{1,0:T(8,128)}, /*index=5*/f32[392,1024]{1,0:T(8,128)}) custom-call(s32[8]{0:T(128)} %bitcast.35, s32[2]{0:T(128)} %pad_add_fusion.at_ref, bf16[392,1024]{1,0:T(8,128)(2,1)} %bitcast.27, ...), custom_call_target="tpu_custom_call" | custom-call | tf_op jit(solution)/shard_map/forward/pallas_call | solution.py:370
  24.9 0.2 collective-permute-done.2.refs_0_
  25.0 0.8 copy-done.3
  25.8 5.6 %point.1 = (bf16[392,1024]{1,0:T(8,128)(2,1)}, bf16[8,64,1024]{2,1,0:T(8,128)(2,1)}, f32[8,64,1024]{2,1,0:T(8,128)}) custom-call(s32[8]{0:T(128)} %bitcast.36, s32[2]{0:T(128)} %pad_add_fusion.at_ref, bf16[392,1024]{1,0:T(8,128)(2,1)} %bitcast.25, bf16[392,1024]{1,0:T(8,128)(2,1)} %get-tuple-element.30.active_ref, bf16[196,1024]{1,0:T(8,128)(2,1)} %copy-done.3), custom_call_target="tpu_custom_call" | custom-call | tf_op jit(solution)/shard_map/point/pallas_call | solution.py:382
  31.4 1.9 %collective-permute-start.1 = (bf16[196,1024]{1,0:T(8,128)(2,1)}, bf16[196,1024]{1,0:T(8,128)(2,1)S(1)}, u32[]{:S(2)}, u32[]{:S(2)}) collective-permute-start(bf16[196,1024]{1,0:T(8,128)(2,1)} %get-tuple-element.29), channel_id=1, source_target_pairs={{0,16},{16,0},{1,17},{17,1},{2,18},{18,2},{3,19},{19,3},{4,20},{20... | collective-permute-start | bytes 1204232 | tf_op jit(solution)/shard_map/ppermute | solution.py:345
  33.3 7.5 %backward.1 = (bf16[196,1024]{1,0:T(8,128)(2,1)}, bf16[392,1024]{1,0:T(8,128)(2,1)}, f32[392,1024]{1,0:T(8,128)}) custom-call(s32[2]{0:T(128)} %pad_add_fusion.at_ref, bf16[392,1024]{1,0:T(8,128)(2,1)} %get-tuple-element.31.slot_grads_ref, bf16[1024,1024]{1,0:T(8,128)(2,1)} %bitcast.23, f32[25,1,1024]{2,1,0:T(1,128)} %bitcast.31, ...), custom_call_target="tpu_custom_call" | custom-call | tf_op jit(solution)/shard_map/backward/pallas_call | solution.py:392
  40.7 5.6 %taps.1 = f32[25,1,1024]{2,1,0:T(1,128)} custom-call(s32[2]{0:T(128)} %pad_add_fusion.at_ref, f32[392,1024]{1,0:T(8,128)} %get-tuple-element.50.mixed_ref, f32[392,1024]{1,0:T(8,128)} %get-tuple-element.51.source_ref), custom_call_target="tpu_custom_call" | custom-call | tf_op jit(solution)/shard_map/taps/pallas_call | solution.py:403
  46.3 0.2 collective-permute-start.11
  46.6 0.3 collective-permute-start.3
  46.9 1.6 %fusion = (f32[8,64,512]{2,1,0:T(8,128)}, f32[8,64,512]{2,1,0:T(8,128)}) fusion(f32[8,64,1024]{2,1,0:T(8,128)S(1)} %copy-done), kind=kLoop, calls=%fused_computation.2 | loop fusion | bytes 4194304 | tf_op jit(solution)/shard_map/slice | solution.py:419
  48.5 1.1 %fusion.1 = (bf16[8,64,512]{2,1,0:T(8,128)(2,1)}, bf16[8,64,512]{2,1,0:T(8,128)(2,1)}) fusion(bf16[8,64,1024]{2,1,0:T(8,128)(2,1)S(1)} %collective-permute-done.4), kind=kLoop, calls=%fused_computation.3 | loop fusion | bytes 2097152 | tf_op jit(solution)/shard_map/slice | solution.py:419
  49.6 2.4 %fold.6 = (bf16[4,64,512]{2,1,0:T(8,128)(2,1)}, f32[4,64,512]{2,1,0:T(8,128)}) custom-call(s32[2]{0:T(128)} %pad_add_fusion.at_ref, f32[8,64,512]{2,1,0:T(8,128)} %get-tuple-element.57.keep_ref, bf16[8,64,512]{2,1,0:T(8,128)(2,1)} %get-tuple-element.59.got_ref), custom_call_target="tpu_custom_call" | custom-call | tf_op jit(solution)/shard_map/fold/pallas_call | solution.py:427
  51.9 1.8 %collective-permute-start.5 = (bf16[4,64,512]{2,1,0:T(8,128)(2,1)}, bf16[4,64,512]{2,1,0:T(8,128)(2,1)S(1)}, u32[]{:S(2)}, u32[]{:S(2)}) collective-permute-start(bf16[4,64,512]{2,1,0:T(8,128)(2,1)} %get-tuple-element.39), channel_id=1, source_target_pairs={{0,2},{1,3},{2,0},{3,1},{4,6},{5,7},{6,4},{7,5},{8,10},{9,11},{10,... | collective-permute-start | bytes 786440 | tf_op jit(solution)/shard_map/ppermute | solution.py:362
  53.7 2.3 %fold.9 = (bf16[4,64,512]{2,1,0:T(8,128)(2,1)}, f32[4,64,512]{2,1,0:T(8,128)}) custom-call(s32[2]{0:T(128)} %pad_add_fusion.at_ref, f32[8,64,512]{2,1,0:T(8,128)} %get-tuple-element.56.keep_ref, bf16[8,64,512]{2,1,0:T(8,128)(2,1)} %get-tuple-element.58.got_ref), custom_call_target="tpu_custom_call" | custom-call | tf_op jit(solution)/shard_map/fold/pallas_call | solution.py:427
  56.1 1.6 %collective-permute-start.8 = (bf16[4,64,512]{2,1,0:T(8,128)(2,1)}, bf16[4,64,512]{2,1,0:T(8,128)(2,1)S(1)}, u32[]{:S(2)}, u32[]{:S(2)}) collective-permute-start(bf16[4,64,512]{2,1,0:T(8,128)(2,1)} %get-tuple-element.45), channel_id=1, source_target_pairs={{0,4},{1,5},{2,6},{3,7},{4,0},{5,1},{6,2},{7,3},{8,12},{9,13},{10,... | collective-permute-start | bytes 786440 | tf_op jit(solution)/shard_map/ppermute | solution.py:362
  57.8 0.6 collective-permute-start.12
  58.3 4.3 %collective-permute-done.12 = f32[25,1,1024]{2,1,0:T(1,128)S(1)} collective-permute-done((f32[25,1,1024]{2,1,0:T(1,128)S(1)}, f32[25,1,1024]{2,1,0:T(1,128)S(1)}, u32[]{:S(2)}, u32[]{:S(2)}) %collective-permute-start.12) | collective-permute-done | bytes 102432 | tf_op jit(solution)/shard_map/ppermute | solution.py:362
  62.6 0.1 add.13
  62.7 1.9 %collective-permute-start.13 = (f32[25,1,1024]{2,1,0:T(1,128)S(1)}, f32[25,1,1024]{2,1,0:T(1,128)S(1)}, u32[]{:S(2)}, u32[]{:S(2)}) collective-permute-start(f32[25,1,1024]{2,1,0:T(1,128)S(1)} %add.13), channel_id=1, source_target_pairs={{0,4},{1,5},{2,6},{3,7},{4,0},{5,1},{6,2},{7,3},{8,12},{9,13},{10,... | collective-permute-start | bytes 307208 | tf_op jit(solution)/shard_map/ppermute | solution.py:362
  64.6 0.7 copy-done.7
  65.3 1.9 %fold.7 = (bf16[2,64,512]{2,1,0:T(8,128)(2,1)}, f32[2,64,512]{2,1,0:T(8,128)}) custom-call(s32[2]{0:T(128)} %pad_add_fusion.at_ref, f32[4,64,512]{2,1,0:T(8,128)} %get-tuple-element.38.keep_ref, bf16[4,64,512]{2,1,0:T(8,128)(2,1)} %copy-done.7), custom_call_target="tpu_custom_call" | custom-call | tf_op jit(solution)/shard_map/fold/pallas_call | solution.py:427
  67.2 0.2 collective-permute-start.6
  67.5 0.7 copy-done.6
  68.2 1.9 %fold.10 = (bf16[2,64,512]{2,1,0:T(8,128)(2,1)}, f32[2,64,512]{2,1,0:T(8,128)}) custom-call(s32[2]{0:T(128)} %pad_add_fusion.at_ref, f32[4,64,512]{2,1,0:T(8,128)} %get-tuple-element.44.keep_ref, bf16[4,64,512]{2,1,0:T(8,128)(2,1)} %copy-done.6), custom_call_target="tpu_custom_call" | custom-call | tf_op jit(solution)/shard_map/fold/pallas_call | solution.py:427
  70.1 1.7 %collective-permute-start.9 = (bf16[2,64,512]{2,1,0:T(8,128)(2,1)}, bf16[2,64,512]{2,1,0:T(8,128)(2,1)S(1)}, u32[]{:S(2)}, u32[]{:S(2)}) collective-permute-start(bf16[2,64,512]{2,1,0:T(8,128)(2,1)} %get-tuple-element.47), channel_id=1, source_target_pairs={{0,2},{1,3},{2,0},{3,1},{4,6},{5,7},{6,4},{7,5},{8,10},{9,11},{10,... | collective-permute-start | bytes 393224 | tf_op jit(solution)/shard_map/ppermute | solution.py:362
  71.8 0.1 add.14
  72.0 2.7 %collective-permute-start.14 = (f32[25,1,1024]{2,1,0:T(1,128)S(1)}, f32[25,1,1024]{2,1,0:T(1,128)S(1)}, u32[]{:S(2)}, u32[]{:S(2)}) collective-permute-start(f32[25,1,1024]{2,1,0:T(1,128)S(1)} %add.14), channel_id=1, source_target_pairs={{0,8},{1,9},{2,10},{3,11},{4,12},{5,13},{6,14},{7,15},{8,0},{9,1},... | collective-permute-start | bytes 307208 | tf_op jit(solution)/shard_map/ppermute | solution.py:362
  74.6 0.8 copy-done.1
  75.4 3.0 %unpack.2 = bf16[392,1024]{1,0:T(8,128)(2,1)} custom-call(s32[8]{0:T(128)} %bitcast.37, s32[2]{0:T(128)} %pad_add_fusion.at_ref, bf16[392,1024]{1,0:T(8,128)(2,1)} %get-tuple-element.28.slots_ref, bf16[196,1024]{1,0:T(8,128)(2,1)} %copy-done.1), custom_call_target="tpu_custom_call" | custom-call | tf_op jit(solution)/shard_map/unpack/pallas_call | solution.py:354
  78.4 0.8 copy-done.2
  79.2 3.0 %unpack.3 = bf16[392,1024]{1,0:T(8,128)(2,1)} custom-call(s32[8]{0:T(128)} %bitcast.38, s32[2]{0:T(128)} %pad_add_fusion.at_ref, bf16[392,1024]{1,0:T(8,128)(2,1)} %get-tuple-element.34.slots_ref, bf16[196,1024]{1,0:T(8,128)(2,1)} %copy-done.2), custom_call_target="tpu_custom_call" | custom-call | tf_op jit(solution)/shard_map/unpack/pallas_call | solution.py:354
  82.2 0.7 copy-done.9
  82.8 1.7 %fold.8 = (bf16[1,64,512]{2,1,0:T(8,128)(2,1)}, f32[1,64,512]{2,1,0:T(8,128)}) custom-call(s32[2]{0:T(128)} %pad_add_fusion.at_ref, f32[2,64,512]{2,1,0:T(8,128)} %get-tuple-element.40.keep_ref, bf16[2,64,512]{2,1,0:T(8,128)(2,1)} %copy-done.9), custom_call_target="tpu_custom_call" | custom-call | tf_op jit(solution)/shard_map/fold/pallas_call | solution.py:427
  84.5 0.3 collective-permute-start.7
  84.9 0.7 copy-done.8
  85.5 1.7 %fold.11 = (bf16[1,64,512]{2,1,0:T(8,128)(2,1)}, f32[1,64,512]{2,1,0:T(8,128)}) custom-call(s32[2]{0:T(128)} %pad_add_fusion.at_ref, f32[2,64,512]{2,1,0:T(8,128)} %get-tuple-element.46.keep_ref, bf16[2,64,512]{2,1,0:T(8,128)(2,1)} %copy-done.8), custom_call_target="tpu_custom_call" | custom-call | tf_op jit(solution)/shard_map/fold/pallas_call | solution.py:427
  87.2 2.6 %collective-permute-start.10 = (bf16[1,64,512]{2,1,0:T(8,128)(2,1)}, bf16[1,64,512]{2,1,0:T(8,128)(2,1)S(1)}, u32[]{:S(2)}, u32[]{:S(2)}) collective-permute-start(bf16[1,64,512]{2,1,0:T(8,128)(2,1)} %get-tuple-element.49), channel_id=1, source_target_pairs={{0,8},{1,9},{2,10},{3,11},{4,12},{5,13},{6,14},{7,15},{8,0},{9,1},... | collective-permute-start | bytes 196616 | tf_op jit(solution)/shard_map/ppermute | solution.py:362
  89.8 0.8 add_bitcast_fusion
  90.6 0.9 collective-permute-done.7.got_a_ref
  91.5 1.1 %collective-permute-done.10.got_b_ref = bf16[1,64,512]{2,1,0:T(8,128)(2,1)S(1)} collective-permute-done((bf16[1,64,512]{2,1,0:T(8,128)(2,1)}, bf16[1,64,512]{2,1,0:T(8,128)(2,1)S(1)}, u32[]{:S(2)}, u32[]{:S(2)}) %collective-permute-start.10) | collective-permute-done | bytes 65568 | tf_op jit(solution)/shard_map/ppermute | solution.py:362
  92.6 0.6 copy-done.11
  93.3 1.7 %last.1 = f32[64,1024]{1,0:T(8,128)} custom-call(f32[1,64,512]{2,1,0:T(8,128)} %get-tuple-element.42.keep_a_ref, bf16[1,64,512]{2,1,0:T(8,128)(2,1)} %copy-done.10, f32[1,64,512]{2,1,0:T(8,128)} %get-tuple-element.48.keep_b_ref, bf16[1,64,512]{2,1,0:T(8,128)(2,1)} %copy-done.11), custom_call_target="tpu_custom_call" | custom-call | tf_op jit(solution)/shard_map/last/pallas_call | solution.py:435
  (30 shorter events, 0.2 us)
Async XLA Ops:
  3.6 13.5 %collective-permute-start = (bf16[196,1024]{1,0:T(8,128)(2,1)}, bf16[196,1024]{1,0:T(8,128)(2,1)S(1)}, u32[]{:S(2)}, u32[]{:S(2)}) collective-permute-start(bf16[196,1024]{1,0:T(8,128)(2,1)} %pack.2), channel_id=1, source_target_pairs={{0,16},{16,0},{1,17},{17,1},{2,18},{18,2},{3,19},{19,3},{4,20},{20... | collective-permute-start | bytes 1204232 | tf_op jit(solution)/shard_map/ppermute | solution.py:345
  8.9 16.1 %collective-permute-start.2 = (bf16[196,1024]{1,0:T(8,128)(2,1)}, bf16[196,1024]{1,0:T(8,128)(2,1)S(1)}, u32[]{:S(2)}, u32[]{:S(2)}) collective-permute-start(bf16[196,1024]{1,0:T(8,128)(2,1)} %pack.3), channel_id=1, source_target_pairs={{0,16},{16,0},{1,17},{17,1},{2,18},{18,2},{3,19},{19,3},{4,20},{20... | collective-permute-start | bytes 1204232 | tf_op jit(solution)/shard_map/ppermute | solution.py:345
  17.1 0.8 copy-start.4
  25.0 0.8 copy-start.3
  31.4 17.1 %collective-permute-start.4 = (bf16[8,64,1024]{2,1,0:T(8,128)(2,1)}, bf16[8,64,1024]{2,1,0:T(8,128)(2,1)S(1)}, u32[]{:S(2)}, u32[]{:S(2)}) collective-permute-start(bf16[8,64,1024]{2,1,0:T(8,128)(2,1)} %get-tuple-element.37), channel_id=1, source_target_pairs={{0,1},{1,0},{2,3},{3,2},{4,5},{5,4},{6,7},{7,6},{8,9},{9,8},{10,11... | collective-permute-start | bytes 3145736 | tf_op jit(solution)/shard_map/ppermute | solution.py:362
  31.4 43.2 %collective-permute-start.1 = (bf16[196,1024]{1,0:T(8,128)(2,1)}, bf16[196,1024]{1,0:T(8,128)(2,1)S(1)}, u32[]{:S(2)}, u32[]{:S(2)}) collective-permute-start(bf16[196,1024]{1,0:T(8,128)(2,1)} %get-tuple-element.29), channel_id=1, source_target_pairs={{0,16},{16,0},{1,17},{17,1},{2,18},{18,2},{3,19},{19,3},{4,20},{20... | collective-permute-start | bytes 1204232 | tf_op jit(solution)/shard_map/ppermute | solution.py:345
  40.7 5.8 %copy-start.12 = (bf16[196,1024]{1,0:T(8,128)(2,1)S(1)}, bf16[196,1024]{1,0:T(8,128)(2,1)}, u32[]{:S(2)}) copy-start(bf16[196,1024]{1,0:T(8,128)(2,1)} %get-tuple-element.35) | copy-start | bytes 1204228
  40.7 6.1 %copy-start = (f32[8,64,1024]{2,1,0:T(8,128)S(1)}, f32[8,64,1024]{2,1,0:T(8,128)}, u32[]{:S(2)}) copy-start(f32[8,64,1024]{2,1,0:T(8,128)} %get-tuple-element.36) | copy-start | bytes 6291460
  46.3 11.3 %collective-permute-start.11 = (f32[25,1,1024]{2,1,0:T(1,128)}, f32[25,1,1024]{2,1,0:T(1,128)S(1)}, u32[]{:S(2)}, u32[]{:S(2)}) collective-permute-start(f32[25,1,1024]{2,1,0:T(1,128)} %taps.1), channel_id=1, source_target_pairs={{0,1},{1,0},{2,3},{3,2},{4,5},{5,4},{6,7},{7,6},{8,9},{9,8},{10,11... | collective-permute-start | bytes 307208 | tf_op jit(solution)/shard_map/ppermute | solution.py:362
  46.6 31.8 %collective-permute-start.3 = (bf16[196,1024]{1,0:T(8,128)(2,1)S(1)}, bf16[196,1024]{1,0:T(8,128)(2,1)S(1)}, u32[]{:S(2)}, u32[]{:S(2)}) collective-permute-start(bf16[196,1024]{1,0:T(8,128)(2,1)S(1)} %copy-done.12), channel_id=1, source_target_pairs={{0,16},{16,0},{1,17},{17,1},{2,18},{18,2},{3,19},{19,3},{4,20},{20... | collective-permute-start | bytes 1204232 | tf_op jit(solution)/shard_map/ppermute | solution.py:345
  49.6 8.1 %copy-start.5 = (f32[25,1,1024]{2,1,0:T(1,128)S(1)}, f32[25,1,1024]{2,1,0:T(1,128)}, u32[]{:S(2)}) copy-start(f32[25,1,1024]{2,1,0:T(1,128)} %taps.1) | copy-start | bytes 307204
  51.9 12.6 %collective-permute-start.5 = (bf16[4,64,512]{2,1,0:T(8,128)(2,1)}, bf16[4,64,512]{2,1,0:T(8,128)(2,1)S(1)}, u32[]{:S(2)}, u32[]{:S(2)}) collective-permute-start(bf16[4,64,512]{2,1,0:T(8,128)(2,1)} %get-tuple-element.39), channel_id=1, source_target_pairs={{0,2},{1,3},{2,0},{3,1},{4,6},{5,7},{6,4},{7,5},{8,10},{9,11},{10,... | collective-permute-start | bytes 786440 | tf_op jit(solution)/shard_map/ppermute | solution.py:362
  56.1 11.4 %collective-permute-start.8 = (bf16[4,64,512]{2,1,0:T(8,128)(2,1)}, bf16[4,64,512]{2,1,0:T(8,128)(2,1)S(1)}, u32[]{:S(2)}, u32[]{:S(2)}) collective-permute-start(bf16[4,64,512]{2,1,0:T(8,128)(2,1)} %get-tuple-element.45), channel_id=1, source_target_pairs={{0,4},{1,5},{2,6},{3,7},{4,0},{5,1},{6,2},{7,3},{8,12},{9,13},{10,... | collective-permute-start | bytes 786440 | tf_op jit(solution)/shard_map/ppermute | solution.py:362
  57.8 4.8 %collective-permute-start.12 = (f32[25,1,1024]{2,1,0:T(1,128)S(1)}, f32[25,1,1024]{2,1,0:T(1,128)S(1)}, u32[]{:S(2)}, u32[]{:S(2)}) collective-permute-start(f32[25,1,1024]{2,1,0:T(1,128)S(1)} %add.12), channel_id=1, source_target_pairs={{0,2},{1,3},{2,0},{3,1},{4,6},{5,7},{6,4},{7,5},{8,10},{9,11},{10,... | collective-permute-start | bytes 307208 | tf_op jit(solution)/shard_map/ppermute | solution.py:362
  62.7 9.1 %collective-permute-start.13 = (f32[25,1,1024]{2,1,0:T(1,128)S(1)}, f32[25,1,1024]{2,1,0:T(1,128)S(1)}, u32[]{:S(2)}, u32[]{:S(2)}) collective-permute-start(f32[25,1,1024]{2,1,0:T(1,128)S(1)} %add.13), channel_id=1, source_target_pairs={{0,4},{1,5},{2,6},{3,7},{4,0},{5,1},{6,2},{7,3},{8,12},{9,13},{10,... | collective-permute-start | bytes 307208 | tf_op jit(solution)/shard_map/ppermute | solution.py:362
  64.6 0.7 copy-start.7
  67.2 15.0 %collective-permute-start.6 = (bf16[2,64,512]{2,1,0:T(8,128)(2,1)}, bf16[2,64,512]{2,1,0:T(8,128)(2,1)S(1)}, u32[]{:S(2)}, u32[]{:S(2)}) collective-permute-start(bf16[2,64,512]{2,1,0:T(8,128)(2,1)} %get-tuple-element.41), channel_id=1, source_target_pairs={{0,4},{1,5},{2,6},{3,7},{4,0},{5,1},{6,2},{7,3},{8,12},{9,13},{10,... | collective-permute-start | bytes 393224 | tf_op jit(solution)/shard_map/ppermute | solution.py:362
  67.4 0.7 copy-start.6
  70.1 14.8 %collective-permute-start.9 = (bf16[2,64,512]{2,1,0:T(8,128)(2,1)}, bf16[2,64,512]{2,1,0:T(8,128)(2,1)S(1)}, u32[]{:S(2)}, u32[]{:S(2)}) collective-permute-start(bf16[2,64,512]{2,1,0:T(8,128)(2,1)} %get-tuple-element.47), channel_id=1, source_target_pairs={{0,2},{1,3},{2,0},{3,1},{4,6},{5,7},{6,4},{7,5},{8,10},{9,11},{10,... | collective-permute-start | bytes 393224 | tf_op jit(solution)/shard_map/ppermute | solution.py:362
  72.0 17.9 %collective-permute-start.14 = (f32[25,1,1024]{2,1,0:T(1,128)S(1)}, f32[25,1,1024]{2,1,0:T(1,128)S(1)}, u32[]{:S(2)}, u32[]{:S(2)}) collective-permute-start(f32[25,1,1024]{2,1,0:T(1,128)S(1)} %add.14), channel_id=1, source_target_pairs={{0,8},{1,9},{2,10},{3,11},{4,12},{5,13},{6,14},{7,15},{8,0},{9,1},... | collective-permute-start | bytes 307208 | tf_op jit(solution)/shard_map/ppermute | solution.py:362
  74.6 0.8 copy-start.1
  78.4 0.8 copy-start.2
  82.2 0.7 copy-start.9
  84.5 7.0 %collective-permute-start.7 = (bf16[1,64,512]{2,1,0:T(8,128)(2,1)}, bf16[1,64,512]{2,1,0:T(8,128)(2,1)S(1)}, u32[]{:S(2)}, u32[]{:S(2)}) collective-permute-start(bf16[1,64,512]{2,1,0:T(8,128)(2,1)} %get-tuple-element.43), channel_id=1, source_target_pairs={{0,8},{1,9},{2,10},{3,11},{4,12},{5,13},{6,14},{7,15},{8,0},{9,1},... | collective-permute-start | bytes 196616 | tf_op jit(solution)/shard_map/ppermute | solution.py:362
  84.9 0.7 copy-start.8
  87.2 5.4 %collective-permute-start.10 = (bf16[1,64,512]{2,1,0:T(8,128)(2,1)}, bf16[1,64,512]{2,1,0:T(8,128)(2,1)S(1)}, u32[]{:S(2)}, u32[]{:S(2)}) collective-permute-start(bf16[1,64,512]{2,1,0:T(8,128)(2,1)} %get-tuple-element.49), channel_id=1, source_target_pairs={{0,8},{1,9},{2,10},{3,11},{4,12},{5,13},{6,14},{7,15},{8,0},{9,1},... | collective-permute-start | bytes 196616 | tf_op jit(solution)/shard_map/ppermute | solution.py:362
  91.5 1.1 %copy-start.10 = (bf16[1,64,512]{2,1,0:T(8,128)(2,1)}, bf16[1,64,512]{2,1,0:T(8,128)(2,1)S(1)}, u32[]{:S(2)}) copy-start(bf16[1,64,512]{2,1,0:T(8,128)(2,1)S(1)} %collective-permute-done.7.got_a_ref) | copy-start | bytes 196612
  92.6 0.6 copy-start.11

commit v2 on v1

--- a/solution.py
+++ b/solution.py
@@ -197,7 +197,7 @@
     return_slots(final_ref[...], back_refs, sizes)
 
 
-def point_kernel(path_ref, at_ref, grads_ref, active_ref, *refs, sizes, ways):
+def point_kernel(path_ref, at_ref, replica_ref, grads_ref, active_ref, *refs, sizes, ways):
     places, samples, sections, capacity = sizes
     got_refs, refs = refs[: sections - 1], refs[sections - 1 :]
     slot_grads_ref, send_ref, keep_ref, total_ref = refs
@@ -207,29 +207,29 @@
     )
     rows = total.shape[0] // ways
     total_ref[...] = total.reshape(ways, rows, total.shape[1])
-    low = at_ref[1] & 1
+    low = replica_ref[0] & 1
     for at in range(ways // 2):
         send_ref[at] = total_ref[2 * at + 1 - low].astype(BF16)
         keep_ref[at] = total_ref[2 * at + low]
 
 
-def fold_kernel(at_ref, keep_ref, got_ref, send_ref, left_ref, *, stride, bit):
-    count = keep_ref.shape[0]
-    mine = (at_ref[1] // bit) & 1
-    at = 0
-    for base in range(0, count, 2 * stride):
-        for offset in range(stride):
-            give = base + offset + stride * (1 - mine)
-            hold = base + offset + stride * mine
-            send_ref[at] = (keep_ref[give] + got_ref[give].astype(F32)).astype(BF16)
-            left_ref[at] = keep_ref[hold] + got_ref[hold].astype(F32)
-            at += 1
-
-
-def last_kernel(keep_a_ref, got_a_ref, keep_b_ref, got_b_ref, out_ref):
-    half = keep_a_ref.shape[-1]
-    out_ref[:, :half] = keep_a_ref[0] + got_a_ref[0].astype(F32)
-    out_ref[:, half:] = keep_b_ref[0] + got_b_ref[0].astype(F32)
+def fold_kernel(replica_ref, *refs, moves, arriving):
+    ins, outs = refs[:arriving], refs[arriving:]
+    for (stride, bit), (source, came), (target, goes) in moves:
+        keep_ref, got_ref = ins[2 * source], ins[2 * source + 1]
+        send_ref, left_ref = outs[2 * target], outs[2 * target + 1]
+        count = keep_ref.shape[0]
+        mine = (replica_ref[0] // bit) & 1
+        at = 0
+        for base in range(0, count, 2 * stride):
+            for offset in range(stride):
+                give = base + offset + stride * (1 - mine)
+                hold = base + offset + stride * mine
+                send_ref[at, :, goes] = (
+                    keep_ref[give, :, came] + got_ref[give, :, came].astype(F32)
+                ).astype(BF16)
+                left_ref[at, :, goes] = keep_ref[hold, :, came] + got_ref[hold, :, came].astype(F32)
+                at += 1
 
 
 def backward_kernel(
@@ -293,14 +293,14 @@
     lax.fori_loop(0, channels // LANES, chunk, 0)
 
 
-def call(kernel, name, outs, in_specs, scratch=()):
+def call(kernel, name, outs, in_specs, scratch=(), megabytes=20):
     return pl.pallas_call(
         kernel,
         out_shape=outs,
         in_specs=in_specs,
         out_specs=jax.tree.map(lambda _: VMEM, outs),
         scratch_shapes=list(scratch),
-        compiler_params=pltpu.CompilerParams(vmem_limit_bytes=56 * 1024 * 1024),
+        compiler_params=pltpu.CompilerParams(vmem_limit_bytes=megabytes * 1024 * 1024),
         name=name,
     )
 
@@ -308,14 +308,13 @@
 def body(feature_maps, path_lists, point_weight, depth_kernel, cotangent):
     sections = lax.axis_size("segment")
     ways = lax.axis_size("rep")
-    section = lax.axis_index("segment").astype(jnp.int32)
-    replica = lax.axis_index("rep").astype(jnp.int32)
+    at = lax.axis_index("segment").astype(jnp.int32).reshape(1)
+    replica = lax.axis_index("rep").astype(jnp.int32).reshape(1)
     samples, side, _, channels = feature_maps.shape
     places = side * side
     capacity = max(max(2, samples // 4), (samples + sections - 1) // sections)
     slots = sections * capacity
     sizes = (places, samples, sections, capacity)
-    at = jnp.stack([section, replica])
     path = path_lists[0, :, 0]
     weight = point_weight[0, 0]
     kernel = depth_kernel[0, 0].reshape(25, 1, channels)
@@ -383,9 +382,9 @@
         functools.partial(point_kernel, sizes=sizes, ways=ways),
         "point",
         [slot_half, shape(ways // 2, block, channels, dtype=BF16), shape(ways // 2, block, channels)],
-        [SMEM, SMEM, VMEM, VMEM] + [VMEM for _ in others],
+        [SMEM, SMEM, SMEM, VMEM, VMEM] + [VMEM for _ in others],
         [pltpu.VMEM((ways, block, channels), F32)],
-    )(path, at, grads, active, *got_grads)
+    )(path, at, replica, grads, active, *got_grads)
 
     got = trade(send, 1)
 
@@ -408,33 +407,39 @@
     )(at, mixed, source)
 
     bits = [1 << i for i in range(1, ways.bit_length() - 1)]
+    orders = [list(bits), list(bits)]
+    if len(bits) > 2:
+        orders[1][0], orders[1][1] = bits[1], bits[0]
     half = channels // 2
-    finished = []
-    for part in range(2):
-        order = list(bits)
-        if part == 1 and len(order) > 1:
-            order[0], order[1] = order[1], order[0]
-        left = list(bits)
-        columns = slice(part * half, (part + 1) * half)
-        keep_part, got_part = keep[:, :, columns], got[:, :, columns]
-        for bit in order:
-            stride = 1
-            for other in left:
-                if other < bit:
-                    stride *= 2
-            left.remove(bit)
-            count = keep_part.shape[0] // 2
-            send_part, keep_part = call(
-                functools.partial(fold_kernel, stride=stride, bit=bit),
-                "fold",
-                [shape(count, block, half, dtype=BF16), shape(count, block, half)],
-                [SMEM, VMEM, VMEM],
-            )(at, keep_part, got_part)
-            got_part = trade(send_part, bit)
-        finished += [keep_part, got_part]
-    point_grad = call(
-        last_kernel, "last", shape(block, channels), [VMEM, VMEM, VMEM, VMEM]
-    )(*finished)
+    halves = [slice(0, half), slice(half, channels)]
+    held = [keep, got]
+    for step in range(len(bits)):
+        first, final = step == 0, step == len(bits) - 1
+        count = (ways // 4) >> step
+        moves = []
+        for part in range(2):
+            bit = orders[part][step]
+            done = orders[part][:step]
+            stride = 1 << sum(1 for other in bits if other < bit and other not in done)
+            moves.append(
+                (
+                    (stride, bit),
+                    (0, halves[part]) if first else (part, slice(0, half)),
+                    (0, halves[part]) if final else (part, slice(0, half)),
+                )
+            )
+        width, targets = (channels, 1) if final else (half, 2)
+        outs = [shape(count, block, width, dtype=BF16), shape(count, block, width)] * targets
+        results = call(
+            functools.partial(fold_kernel, moves=moves, arriving=len(held)),
+            "fold",
+            outs,
+            [SMEM] + [VMEM] * len(held),
+        )(replica, *held)
+        held = []
+        for part in range(targets):
+            held += [results[2 * part + 1], trade(results[2 * part], orders[part][step])]
+    point_grad = (held[0] + held[1].astype(F32))[0]
 
     for bit in [1] + bits:
         taps = taps + trade(taps, bit)

time: 95.4 us -> 69.9 us (0.73)
  Pallas kernels: 50.1 us -> 22.1 us
  waiting for transfers between devices: 14.7 us -> 22.6 us
  local copies, waits for them, and re-layouts: 9.11 us -> 5.78 us
  starting transfers between devices: 18.7 us -> 16.6 us
    pallas_call x7 -> x3, Pallas kernels: 13.7 us -> 0.34 us  [body(): call(functools.partial(fold_kernel, moves=moves, arriving=len(held)), 'fo...]
    ppermute x11 -> x10, waiting for transfers between devices: 6.31 us -> 13.8 us  [trade(): return lax.ppermute(value, 'rep', [(i, i ^ bit) for i in range(ways)])]
    pallas_call x1, Pallas kernels: 7.46 us -> 3.91 us  [body(): call(functools.partial(backward_kernel, sizes=sizes, side=side), 'backwar...]
    pallas_call x1, Pallas kernels: 5.61 us -> 2.9 us  [body(): call(functools.partial(taps_kernel, side=side, slots=slots), 'taps', shap...]
    slice x2 -> x0, local copies, waits for them, and re-layouts: 2.7 us -> none  [body(): keep_part, got_part = (keep[:, :, columns], got[:, :, columns])]
    pallas_call x1, Pallas kernels: 5.58 us -> 2.95 us  [body(): call(functools.partial(point_kernel, sizes=sizes, ways=ways), 'point', [s...]
    pallas_call x1, Pallas kernels: 7.01 us -> 4.69 us  [body(): call(functools.partial(forward_kernel, sizes=sizes, side=side), 'forward'...]
    ppermute x11 -> x10, starting transfers between devices: 13.6 us -> 11.5 us  [trade(): return lax.ppermute(value, 'rep', [(i, i ^ bit) for i in range(ways)])]
  transfers between devices with their start and end apart: 15 -> 14, of which waited for: 5 -> 5; matrix products, arithmetic and copies ran while one was open for 4% -> 2% of each run, Pallas kernels for 43% -> 25%
where the time goes in v2:
time: 69.9 us; the launch traced here: 69.6 us
  waiting for transfers between devices  22.6 us (32%)
  Pallas kernels  22.1 us (32%)
  starting transfers between devices  16.6 us (24%)
  local copies, waits for them, and re-layouts  5.78 us (8%)
  other arithmetic  1.8 us (3%)
  between operations  0.77 us (1%)
    ppermute x10, waiting for transfers between devices, trade(): return lax.ppermute(value, 'rep', [(i, i ^ bit) for i in range(ways)])  13.8 us
    ppermute x10, starting transfers between devices, trade(): return lax.ppermute(value, 'rep', [(i, i ^ bit) for i in range(ways)])  11.5 us
    ppermute x4, waiting for transfers between devices, swap(): lax.ppermute(piece, 'segment', [(i, (i + direction * shift) % sections) f...  8.87 us
    unnamed x20, local copies, waits for them, and re-layouts  5.78 us
    ppermute x4, starting transfers between devices, swap(): lax.ppermute(piece, 'segment', [(i, (i + direction * shift) % sections) f...  5.09 us
    pallas_call x1, Pallas kernels, body(): call(functools.partial(forward_kernel, sizes=sizes, side=side), 'forward'...  4.69 us
    pallas_call x2, Pallas kernels, unpack(): call(functools.partial(unpack_kernel, sizes=sizes), 'unpack', shape(place...  4.61 us
    pallas_call x1, Pallas kernels, body(): call(functools.partial(backward_kernel, sizes=sizes, side=side), 'backwar...  3.91 us
  transfers between devices with their start and end apart: 14, of which 5 were waited for; matrix products, arithmetic and copies ran while one was open for 2% of the time, Pallas kernels for 25%

profile of v2, /device:TPU:0, one launch (start us, length us, event | category | flops | bytes accessed | tf_op | source)
XLA Modules:
  0.0 69.6 jit_solution(17873132803752035198)
XLA Ops:
  0.6 0.0 copy-start.1
  0.7 1.3 %copy-done.1 = bf16[8,7,7,1024]{3,0,2,1:T(8,128)(2,1)S(1)} copy-done((bf16[8,7,7,1024]{3,0,2,1:T(8,128)(2,1)S(1)}, bf16[8,7,7,1024]{3,0,2,1:T(8,128)(2,1)}, u32[]{:S(2)}) %copy-start.1) | copy-done | bytes 802840
  1.9 0.7 copy-done.7
  2.6 1.7 %pack.2 = bf16[196,1024]{1,0:T(8,128)(2,1)} custom-call(s32[8]{0:T(128)S(1)} %bitcast.31, s32[1]{0:T(128)} %bitcast.1.at_ref, bf16[392,1024]{1,0:T(8,128)(2,1)S(1)} %bitcast.25), custom_call_target="tpu_custom_call" | custom-call | tf_op jit(solution)/shard_map/pack/pallas_call | solution.py:335
  4.3 3.0 %collective-permute-start = (bf16[196,1024]{1,0:T(8,128)(2,1)}, bf16[196,1024]{1,0:T(8,128)(2,1)S(1)}, u32[]{:S(2)}, u32[]{:S(2)}) collective-permute-start(bf16[196,1024]{1,0:T(8,128)(2,1)} %pack.2), channel_id=1, source_target_pairs={{0,16},{16,0},{1,17},{17,1},{2,18},{18,2},{3,19},{19,3},{4,20},{20... | collective-permute-start | bytes 1204232 | tf_op jit(solution)/shard_map/ppermute | solution.py:344
  7.3 1.1 %copy-done.3 = bf16[8,7,7,1024]{3,0,2,1:T(8,128)(2,1)S(1)} copy-done((bf16[8,7,7,1024]{3,0,2,1:T(8,128)(2,1)S(1)}, bf16[8,7,7,1024]{3,0,2,1:T(8,128)(2,1)}, u32[]{:S(2)}) %copy-start.3) | copy-done | bytes 802840
  8.4 1.0 %pack.3 = bf16[196,1024]{1,0:T(8,128)(2,1)S(1)} custom-call(s32[8]{0:T(128)S(1)} %bitcast.32, s32[1]{0:T(128)} %bitcast.1.at_ref, bf16[392,1024]{1,0:T(8,128)(2,1)S(1)} %bitcast.27), custom_call_target="tpu_custom_call" | custom-call | tf_op jit(solution)/shard_map/pack/pallas_call | solution.py:335
  9.4 0.1 collective-permute-start.2
  9.5 8.3 %collective-permute-done.refs_0_ = bf16[196,1024]{1,0:T(8,128)(2,1)S(1)} collective-permute-done((bf16[196,1024]{1,0:T(8,128)(2,1)}, bf16[196,1024]{1,0:T(8,128)(2,1)S(1)}, u32[]{:S(2)}, u32[]{:S(2)}) %collective-permute-start) | collective-permute-done | bytes 401440 | tf_op jit(solution)/shard_map/ppermute | solution.py:344
  17.8 1.1 %copy-done.2 = bf16[8,7,7,1024]{3,0,2,1:T(8,128)(2,1)S(1)} copy-done((bf16[8,7,7,1024]{3,0,2,1:T(8,128)(2,1)S(1)}, bf16[8,7,7,1024]{3,0,2,1:T(8,128)(2,1)}, u32[]{:S(2)}) %copy-start.2) | copy-done | bytes 802840
  18.9 0.9 %copy-done.5 = f32[1,1,25,1024]{3,1,2,0:T(1,128)S(1)} copy-done((f32[1,1,25,1024]{3,1,2,0:T(1,128)S(1)}, f32[1,1,25,1024]{3,1,2,0:T(1,128)}, u32[]{:S(2)}) %copy-start.5) | copy-done | bytes 102424
  19.8 0.7 copy-done.8
  20.5 4.7 %forward.1 = (bf16[196,1024]{1,0:T(8,128)(2,1)S(1)}, bf16[392,1024]{1,0:T(8,128)(2,1)S(1)}, bf16[392,1024]{1,0:T(8,128)(2,1)S(1)}, f32[392,1024]{1,0:T(8,128)S(1...) custom-call(s32[8]{0:T(128)S(1)} %bitcast.33, s32[1]{0:T(128)} %bitcast.1.at_ref, bf16[392,1024]{1,0:T(8,128)(2,1)S(1)} %bitcast.26, ...), custom_call_target="tpu_custom_call" | custom-call | tf_op jit(solution)/shard_map/forward/pallas_call | solution.py:369
  25.2 0.0 copy-start.6
  25.2 0.5 collective-permute-done.2.refs_0_
  25.7 2.9 %point.1 = (bf16[392,1024]{1,0:T(8,128)(2,1)S(1)}, bf16[8,64,1024]{2,1,0:T(8,128)(2,1)S(1)}, f32[8,64,1024]{2,1,0:T(8,128)S(1)}) custom-call(s32[8]{0:T(128)S(1)} %bitcast.34, s32[1]{0:T(128)} %bitcast.1.at_ref, s32[1]{0:T(128)} %bitcast.9.replica_ref, bf16[392,1024]{1,0:T(8,128)(2,1)S(1)} %bitcast.28, bf16[392,1024]{1,0:T(8,128)(2,1)S(1)} %get-tuple-element.28.active_ref, ...), custom_call_target="tpu_custom_call" | custom-call | tf_op jit(solution)/shard_map/point/pallas_call | solution.py:381
  28.7 0.1 collective-permute-start.4
  28.8 3.9 %backward.1 = (bf16[196,1024]{1,0:T(8,128)(2,1)S(1)}, bf16[392,1024]{1,0:T(8,128)(2,1)S(1)}, f32[392,1024]{1,0:T(8,128)S(1)}) custom-call(s32[1]{0:T(128)} %bitcast.1.at_ref, bf16[392,1024]{1,0:T(8,128)(2,1)S(1)} %get-tuple-element.29.slot_grads_ref, bf16[1024,1024]{1,0:T(8,128)(2,1)S(1)} %bitcast.24, f32[25,1,1024]{2,1,0:T(1,128)S(1)} %bitcast.30, ...), custom_call_target="tpu_custom_call" | custom-call | tf_op jit(solution)/shard_map/backward/pallas_call | solution.py:391
  32.7 2.9 %taps.1 = f32[25,1,1024]{2,1,0:T(1,128)S(1)} custom-call(s32[1]{0:T(128)} %bitcast.1.at_ref, f32[392,1024]{1,0:T(8,128)S(1)} %get-tuple-element.46.mixed_ref, f32[392,1024]{1,0:T(8,128)S(1)} %get-tuple-element.47.source_ref), custom_call_target="tpu_custom_call" | custom-call | tf_op jit(solution)/shard_map/taps/pallas_call | solution.py:402
  35.6 0.6 collective-permute-start.10
  36.1 1.7 %collective-permute-start.1 = (bf16[196,1024]{1,0:T(8,128)(2,1)S(1)}, bf16[196,1024]{1,0:T(8,128)(2,1)S(1)}, u32[]{:S(2)}, u32[]{:S(2)}) collective-permute-start(bf16[196,1024]{1,0:T(8,128)(2,1)S(1)} %get-tuple-element.27), channel_id=1, source_target_pairs={{0,16},{16,0},{1,17},{17,1},{2,18},{18,2},{3,19},{19,3},{4,20},{20... | collective-permute-start | bytes 1204232 | tf_op jit(solution)/shard_map/ppermute | solution.py:344
  37.9 0.3 collective-permute-start.3
  38.2 0.0 collective-permute-done.4.refs_1_
  38.2 0.2 fold.3
  38.4 0.0 copy-start.9
  38.4 1.8 %collective-permute-start.5 = (bf16[4,64,512]{2,1,0:T(8,128)(2,1)S(1)}, bf16[4,64,512]{2,1,0:T(8,128)(2,1)S(1)}, u32[]{:S(2)}, u32[]{:S(2)}) collective-permute-start(bf16[4,64,512]{2,1,0:T(8,128)(2,1)S(1)} %get-tuple-element.37), channel_id=1, source_target_pairs={{0,2},{1,3},{2,0},{3,1},{4,6},{5,7},{6,4},{7,5},{8,10},{9,11},{10,... | collective-permute-start | bytes 786440 | tf_op jit(solution)/shard_map/ppermute | solution.py:361
  40.2 1.6 %collective-permute-start.6 = (bf16[4,64,512]{2,1,0:T(8,128)(2,1)S(1)}, bf16[4,64,512]{2,1,0:T(8,128)(2,1)S(1)}, u32[]{:S(2)}, u32[]{:S(2)}) collective-permute-start(bf16[4,64,512]{2,1,0:T(8,128)(2,1)S(1)} %get-tuple-element.39), channel_id=1, source_target_pairs={{0,4},{1,5},{2,6},{3,7},{4,0},{5,1},{6,2},{7,3},{8,12},{9,13},{10,... | collective-permute-start | bytes 786440 | tf_op jit(solution)/shard_map/ppermute | solution.py:361
  41.8 0.0 collective-permute-done.10
  41.8 0.1 add.16
  41.9 0.6 collective-permute-start.11
  42.5 6.0 %collective-permute-done.11 = f32[25,1,1024]{2,1,0:T(1,128)S(1)} collective-permute-done((f32[25,1,1024]{2,1,0:T(1,128)S(1)}, f32[25,1,1024]{2,1,0:T(1,128)S(1)}, u32[]{:S(2)}, u32[]{:S(2)}) %collective-permute-start.11) | collective-permute-done | bytes 102432 | tf_op jit(solution)/shard_map/ppermute | solution.py:361
  48.5 0.1 add.17
  48.6 1.8 %collective-permute-start.12 = (f32[25,1,1024]{2,1,0:T(1,128)S(1)}, f32[25,1,1024]{2,1,0:T(1,128)S(1)}, u32[]{:S(2)}, u32[]{:S(2)}) collective-permute-start(f32[25,1,1024]{2,1,0:T(1,128)S(1)} %add.17), channel_id=1, source_target_pairs={{0,4},{1,5},{2,6},{3,7},{4,0},{5,1},{6,2},{7,3},{8,12},{9,13},{10,... | collective-permute-start | bytes 307208 | tf_op jit(solution)/shard_map/ppermute | solution.py:361
  50.4 0.0 collective-permute-done.6.refs_3_
  50.4 0.1 fold.4
  50.5 0.4 collective-permute-start.7
  50.8 1.7 %collective-permute-start.8 = (bf16[2,64,512]{2,1,0:T(8,128)(2,1)S(1)}, bf16[2,64,512]{2,1,0:T(8,128)(2,1)S(1)}, u32[]{:S(2)}, u32[]{:S(2)}) collective-permute-start(bf16[2,64,512]{2,1,0:T(8,128)(2,1)S(1)} %get-tuple-element.43), channel_id=1, source_target_pairs={{0,2},{1,3},{2,0},{3,1},{4,6},{5,7},{6,4},{7,5},{8,10},{9,11},{10,... | collective-permute-start | bytes 393224 | tf_op jit(solution)/shard_map/ppermute | solution.py:361
  52.5 1.5 %collective-permute-done.12 = f32[25,1,1024]{2,1,0:T(1,128)S(1)} collective-permute-done((f32[25,1,1024]{2,1,0:T(1,128)S(1)}, f32[25,1,1024]{2,1,0:T(1,128)S(1)}, u32[]{:S(2)}, u32[]{:S(2)}) %collective-permute-start.12) | collective-permute-done | bytes 102432 | tf_op jit(solution)/shard_map/ppermute | solution.py:361
  54.0 0.1 add.18
  54.1 2.8 %collective-permute-start.13 = (f32[25,1,1024]{2,1,0:T(1,128)S(1)}, f32[25,1,1024]{2,1,0:T(1,128)S(1)}, u32[]{:S(2)}, u32[]{:S(2)}) collective-permute-start(f32[25,1,1024]{2,1,0:T(1,128)S(1)} %add.18), channel_id=1, source_target_pairs={{0,8},{1,9},{2,10},{3,11},{4,12},{5,13},{6,14},{7,15},{8,0},{9,1},... | collective-permute-start | bytes 307208 | tf_op jit(solution)/shard_map/ppermute | solution.py:361
  56.9 0.0 collective-permute-done.1.refs_0_
  56.9 2.3 %unpack.2 = bf16[392,1024]{1,0:T(8,128)(2,1)} custom-call(s32[8]{0:T(128)S(1)} %bitcast.35, s32[1]{0:T(128)} %bitcast.1.at_ref, bf16[392,1024]{1,0:T(8,128)(2,1)S(1)} %get-tuple-element.26.slots_ref, bf16[196,1024]{1,0:T(8,128)(2,1)S(1)} %collective-permute-done.1.refs_0_), custom_call_target="tpu_custom_call" | custom-call | tf_op jit(solution)/shard_map/unpack/pallas_call | solution.py:353
  59.2 0.0 collective-permute-done.3.refs_0_
  59.2 2.3 %unpack.3 = bf16[392,1024]{1,0:T(8,128)(2,1)} custom-call(s32[8]{0:T(128)S(1)} %bitcast.36, s32[1]{0:T(128)} %bitcast.1.at_ref, bf16[392,1024]{1,0:T(8,128)(2,1)S(1)} %get-tuple-element.32.slots_ref, bf16[196,1024]{1,0:T(8,128)(2,1)S(1)} %collective-permute-done.3.refs_0_), custom_call_target="tpu_custom_call" | custom-call | tf_op jit(solution)/shard_map/unpack/pallas_call | solution.py:353
  61.6 0.3 collective-permute-start.9
  61.9 0.8 %add_bitcast_fusion.1 = f32[1,1,25,1024]{3,1,2,0:T(1,128)} fusion(f32[25,1,1024]{2,1,0:T(1,128)S(1)} %add.18, f32[25,1,1024]{2,1,0:T(1,128)S(1)} %collective-permute-done.13), kind=kLoop, calls=%fused_computation.1 | loop fusion | flops 25600 | bytes 307200
  62.6 6.3 %collective-permute-done.9 = bf16[1,64,1024]{2,1,0:T(8,128)(2,1)S(1)} collective-permute-done((bf16[1,64,1024]{2,1,0:T(8,128)(2,1)S(1)}, bf16[1,64,1024]{2,1,0:T(8,128)(2,1)S(1)}, u32[]{:S(2)}, u32[]{:S(2)}) %collective-permute-start.9) | collective-permute-done | bytes 131104 | tf_op jit(solution)/shard_map/ppermute | solution.py:361
  68.9 0.7 %add_bitcast_fusion = f32[1,1,64,1024]{3,2,1,0:T(8,128)} fusion(f32[1,64,1024]{2,1,0:T(8,128)S(1)} %get-tuple-element.44, bf16[1,64,1024]{2,1,0:T(8,128)(2,1)S(1)} %collective-permute-done.9), kind=kLoop, calls=%fused_computation | loop fusion | flops 131072 | bytes 655360 | tf_op jit(solution)/shard_map/reshape;squeeze | solution.py:452
  (16 shorter events, 0.1 us)
Async XLA Ops:
  0.6 17.2 %copy-start = (bf16[1,1,1024,1024]{3,2,1,0:T(8,128)(2,1)S(1)}, bf16[1,1,1024,1024]{3,2,1,0:T(8,128)(2,1)}, u32[]{:S(2)}) copy-start(bf16[1,1,1024,1024]{3,2,1,0:T(8,128)(2,1)} %param.7) | copy-start | bytes 6291460
  0.6 1.3 %copy-start.1 = (bf16[8,7,7,1024]{3,0,2,1:T(8,128)(2,1)S(1)}, bf16[8,7,7,1024]{3,0,2,1:T(8,128)(2,1)}, u32[]{:S(2)}) copy-start(bf16[8,7,7,1024]{3,0,2,1:T(8,128)(2,1)} %param.5) | copy-start | bytes 2408452
  1.9 0.7 copy-start.7
  4.3 13.5 %collective-permute-start = (bf16[196,1024]{1,0:T(8,128)(2,1)}, bf16[196,1024]{1,0:T(8,128)(2,1)S(1)}, u32[]{:S(2)}, u32[]{:S(2)}) collective-permute-start(bf16[196,1024]{1,0:T(8,128)(2,1)} %pack.2), channel_id=1, source_target_pairs={{0,16},{16,0},{1,17},{17,1},{2,18},{18,2},{3,19},{19,3},{4,20},{20... | collective-permute-start | bytes 1204232 | tf_op jit(solution)/shard_map/ppermute | solution.py:344
  7.3 1.1 %copy-start.3 = (bf16[8,7,7,1024]{3,0,2,1:T(8,128)(2,1)S(1)}, bf16[8,7,7,1024]{3,0,2,1:T(8,128)(2,1)}, u32[]{:S(2)}) copy-start(bf16[8,7,7,1024]{3,0,2,1:T(8,128)(2,1)} %param.9) | copy-start | bytes 2408452
  9.4 16.4 %collective-permute-start.2 = (bf16[196,1024]{1,0:T(8,128)(2,1)S(1)}, bf16[196,1024]{1,0:T(8,128)(2,1)S(1)}, u32[]{:S(2)}, u32[]{:S(2)}) collective-permute-start(bf16[196,1024]{1,0:T(8,128)(2,1)S(1)} %pack.3), channel_id=1, source_target_pairs={{0,16},{16,0},{1,17},{17,1},{2,18},{18,2},{3,19},{19,3},{4,20},{20... | collective-permute-start | bytes 1204232 | tf_op jit(solution)/shard_map/ppermute | solution.py:344
  17.8 1.1 %copy-start.2 = (bf16[8,7,7,1024]{3,0,2,1:T(8,128)(2,1)S(1)}, bf16[8,7,7,1024]{3,0,2,1:T(8,128)(2,1)}, u32[]{:S(2)}) copy-start(bf16[8,7,7,1024]{3,0,2,1:T(8,128)(2,1)} %param.5) | copy-start | bytes 2408452
  18.9 0.9 %copy-start.5 = (f32[1,1,25,1024]{3,1,2,0:T(1,128)S(1)}, f32[1,1,25,1024]{3,1,2,0:T(1,128)}, u32[]{:S(2)}) copy-start(f32[1,1,25,1024]{3,1,2,0:T(1,128)} %param.8) | copy-start | bytes 307204
  19.8 0.7 copy-start.8
  20.5 5.2 %copy-start.4 = (bf16[8,7,7,1024]{3,0,2,1:T(8,128)(2,1)S(1)}, bf16[8,7,7,1024]{3,0,2,1:T(8,128)(2,1)}, u32[]{:S(2)}) copy-start(bf16[8,7,7,1024]{3,0,2,1:T(8,128)(2,1)} %param.9) | copy-start | bytes 2408452
  25.2 3.6 %copy-start.6 = (f32[1,1,25,1024]{3,1,2,0:T(1,128)S(1)}, f32[1,1,25,1024]{3,1,2,0:T(1,128)}, u32[]{:S(2)}) copy-start(f32[1,1,25,1024]{3,1,2,0:T(1,128)} %param.8) | copy-start | bytes 307204
  28.7 9.5 %collective-permute-start.4 = (bf16[8,64,1024]{2,1,0:T(8,128)(2,1)S(1)}, bf16[8,64,1024]{2,1,0:T(8,128)(2,1)S(1)}, u32[]{:S(2)}, u32[]{:S(2)}) collective-permute-start(bf16[8,64,1024]{2,1,0:T(8,128)(2,1)S(1)} %get-tuple-element.35), channel_id=1, source_target_pairs={{0,1},{1,0},{2,3},{3,2},{4,5},{5,4},{6,7},{7,6},{8,9},{9,8},{10,11... | collective-permute-start | bytes 3145736 | tf_op jit(solution)/shard_map/ppermute | solution.py:361
  35.6 6.2 %collective-permute-start.10 = (f32[25,1,1024]{2,1,0:T(1,128)S(1)}, f32[25,1,1024]{2,1,0:T(1,128)S(1)}, u32[]{:S(2)}, u32[]{:S(2)}) collective-permute-start(f32[25,1,1024]{2,1,0:T(1,128)S(1)} %taps.1), channel_id=1, source_target_pairs={{0,1},{1,0},{2,3},{3,2},{4,5},{5,4},{6,7},{7,6},{8,9},{9,8},{10,11... | collective-permute-start | bytes 307208 | tf_op jit(solution)/shard_map/ppermute | solution.py:361
  36.1 20.7 %collective-permute-start.1 = (bf16[196,1024]{1,0:T(8,128)(2,1)S(1)}, bf16[196,1024]{1,0:T(8,128)(2,1)S(1)}, u32[]{:S(2)}, u32[]{:S(2)}) collective-permute-start(bf16[196,1024]{1,0:T(8,128)(2,1)S(1)} %get-tuple-element.27), channel_id=1, source_target_pairs={{0,16},{16,0},{1,17},{17,1},{2,18},{18,2},{3,19},{19,3},{4,20},{20... | collective-permute-start | bytes 1204232 | tf_op jit(solution)/shard_map/ppermute | solution.py:344
  37.9 21.3 %collective-permute-start.3 = (bf16[196,1024]{1,0:T(8,128)(2,1)S(1)}, bf16[196,1024]{1,0:T(8,128)(2,1)S(1)}, u32[]{:S(2)}, u32[]{:S(2)}) collective-permute-start(bf16[196,1024]{1,0:T(8,128)(2,1)S(1)} %get-tuple-element.33), channel_id=1, source_target_pairs={{0,16},{16,0},{1,17},{17,1},{2,18},{18,2},{3,19},{19,3},{4,20},{20... | collective-permute-start | bytes 1204232 | tf_op jit(solution)/shard_map/ppermute | solution.py:344
  38.4 18.5 %copy-start.9 = (s32[1,8,1]{1,2,0:T(1,128)S(1)}, s32[1,8,1]{1,2,0:T(1,128)}, u32[]{:S(2)}) copy-start(s32[1,8,1]{1,2,0:T(1,128)} %param.6) | copy-start | bytes 100
  38.4 12.0 %collective-permute-start.5 = (bf16[4,64,512]{2,1,0:T(8,128)(2,1)S(1)}, bf16[4,64,512]{2,1,0:T(8,128)(2,1)S(1)}, u32[]{:S(2)}, u32[]{:S(2)}) collective-permute-start(bf16[4,64,512]{2,1,0:T(8,128)(2,1)S(1)} %get-tuple-element.37), channel_id=1, source_target_pairs={{0,2},{1,3},{2,0},{3,1},{4,6},{5,7},{6,4},{7,5},{8,10},{9,11},{10,... | collective-permute-start | bytes 786440 | tf_op jit(solution)/shard_map/ppermute | solution.py:361
  40.2 10.1 %collective-permute-start.6 = (bf16[4,64,512]{2,1,0:T(8,128)(2,1)S(1)}, bf16[4,64,512]{2,1,0:T(8,128)(2,1)S(1)}, u32[]{:S(2)}, u32[]{:S(2)}) collective-permute-start(bf16[4,64,512]{2,1,0:T(8,128)(2,1)S(1)} %get-tuple-element.39), channel_id=1, source_target_pairs={{0,4},{1,5},{2,6},{3,7},{4,0},{5,1},{6,2},{7,3},{8,12},{9,13},{10,... | collective-permute-start | bytes 786440 | tf_op jit(solution)/shard_map/ppermute | solution.py:361
  41.9 6.6 %collective-permute-start.11 = (f32[25,1,1024]{2,1,0:T(1,128)S(1)}, f32[25,1,1024]{2,1,0:T(1,128)S(1)}, u32[]{:S(2)}, u32[]{:S(2)}) collective-permute-start(f32[25,1,1024]{2,1,0:T(1,128)S(1)} %add.16), channel_id=1, source_target_pairs={{0,2},{1,3},{2,0},{3,1},{4,6},{5,7},{6,4},{7,5},{8,10},{9,11},{10,... | collective-permute-start | bytes 307208 | tf_op jit(solution)/shard_map/ppermute | solution.py:361
  48.6 5.4 %collective-permute-start.12 = (f32[25,1,1024]{2,1,0:T(1,128)S(1)}, f32[25,1,1024]{2,1,0:T(1,128)S(1)}, u32[]{:S(2)}, u32[]{:S(2)}) collective-permute-start(f32[25,1,1024]{2,1,0:T(1,128)S(1)} %add.17), channel_id=1, source_target_pairs={{0,4},{1,5},{2,6},{3,7},{4,0},{5,1},{6,2},{7,3},{8,12},{9,13},{10,... | collective-permute-start | bytes 307208 | tf_op jit(solution)/shard_map/ppermute | solution.py:361
  50.5 11.0 %collective-permute-start.7 = (bf16[2,64,512]{2,1,0:T(8,128)(2,1)S(1)}, bf16[2,64,512]{2,1,0:T(8,128)(2,1)S(1)}, u32[]{:S(2)}, u32[]{:S(2)}) collective-permute-start(bf16[2,64,512]{2,1,0:T(8,128)(2,1)S(1)} %get-tuple-element.41), channel_id=1, source_target_pairs={{0,4},{1,5},{2,6},{3,7},{4,0},{5,1},{6,2},{7,3},{8,12},{9,13},{10,... | collective-permute-start | bytes 393224 | tf_op jit(solution)/shard_map/ppermute | solution.py:361
  50.8 10.7 %collective-permute-start.8 = (bf16[2,64,512]{2,1,0:T(8,128)(2,1)S(1)}, bf16[2,64,512]{2,1,0:T(8,128)(2,1)S(1)}, u32[]{:S(2)}, u32[]{:S(2)}) collective-permute-start(bf16[2,64,512]{2,1,0:T(8,128)(2,1)S(1)} %get-tuple-element.43), channel_id=1, source_target_pairs={{0,2},{1,3},{2,0},{3,1},{4,6},{5,7},{6,4},{7,5},{8,10},{9,11},{10,... | collective-permute-start | bytes 393224 | tf_op jit(solution)/shard_map/ppermute | solution.py:361
  54.1 7.7 %collective-permute-start.13 = (f32[25,1,1024]{2,1,0:T(1,128)S(1)}, f32[25,1,1024]{2,1,0:T(1,128)S(1)}, u32[]{:S(2)}, u32[]{:S(2)}) collective-permute-start(f32[25,1,1024]{2,1,0:T(1,128)S(1)} %add.18), channel_id=1, source_target_pairs={{0,8},{1,9},{2,10},{3,11},{4,12},{5,13},{6,14},{7,15},{8,0},{9,1},... | collective-permute-start | bytes 307208 | tf_op jit(solution)/shard_map/ppermute | solution.py:361
  61.6 7.3 %collective-permute-start.9 = (bf16[1,64,1024]{2,1,0:T(8,128)(2,1)S(1)}, bf16[1,64,1024]{2,1,0:T(8,128)(2,1)S(1)}, u32[]{:S(2)}, u32[]{:S(2)}) collective-permute-start(bf16[1,64,1024]{2,1,0:T(8,128)(2,1)S(1)} %get-tuple-element.45), channel_id=1, source_target_pairs={{0,8},{1,9},{2,10},{3,11},{4,12},{5,13},{6,14},{7,15},{8,0},{9,1},... | collective-permute-start | bytes 393224 | tf_op jit(solution)/shard_map/ppermute | solution.py:361

commit v3 on v2

--- a/solution.py
+++ b/solution.py
@@ -6,6 +6,7 @@
 from jax.experimental import pallas as pl
 from jax.experimental.pallas import tpu as pltpu
 from jax.sharding import PartitionSpec as P
+
 
 EPS = 1e-05
 LANES = 128
@@ -67,12 +68,13 @@
         out_refs[shift - 1][...] = pick(one_hot(mask), maps_ref[...]).astype(BF16)
 
 
-def gather_slots(path_ref, at_ref, maps_ref, got_refs, sizes):
+def prepare_kernel(
+    path_ref, at_ref, maps_ref, grads_ref, kernel_ref, own_maps_ref, own_grads_ref, taps_ref, *, sizes
+):
     places, samples, sections, capacity = sizes
     slots = sections * capacity
     codes = slot_codes(path_ref, samples, capacity)
-    shape = (places * slots, places * samples)
-    row_place, row_slot = split(iota2(shape, 0), slots)
+    row_place, row_slot = split(iota2((places * slots, places * samples), 0), slots)
     col_place, col_sample = split(iota2((1, places * samples), 1), samples)
     col_code = spread_codes(codes, col_sample)
     mask = (
@@ -80,9 +82,19 @@
         & (row_slot < capacity)
         & (col_code == at_ref[0] * capacity + row_slot)
     )
-    total = pick(one_hot(mask), maps_ref[...])
-    shape = (places * slots, places * capacity)
-    row_place, row_slot = split(iota2(shape, 0), slots)
+    matrix = one_hot(mask)
+    own_maps_ref[...] = pick(matrix, maps_ref[...]).astype(BF16)
+    own_grads_ref[...] = pick(matrix, grads_ref[...]).astype(BF16)
+    kind = lax.rem(at_ref[0], 3)
+    for tap in range(25):
+        taps_ref[tap] = kernel_ref[tap] * tap_keep(kind, tap)
+
+
+def gather_slots(own_ref, got_refs, sizes):
+    places, _, sections, capacity = sizes
+    slots = sections * capacity
+    total = own_ref[...].astype(F32)
+    row_place, row_slot = split(iota2((places * slots, places * capacity), 0), slots)
     col_place, col_slot = split(iota2((1, places * capacity), 1), capacity)
     for shift in range(1, sections):
         mask = (row_place == col_place) & (row_slot == shift * capacity + col_slot)
@@ -91,7 +103,7 @@
 
 
 def return_slots(slot_rows, out_refs, sizes):
-    places, samples, sections, capacity = sizes
+    places, _, sections, capacity = sizes
     slots = sections * capacity
     shape = (places * capacity, places * slots)
     row_place, row_slot = split(iota2(shape, 0), capacity)
@@ -136,14 +148,13 @@
     return jnp.where(keep, 1.0, 0.0).astype(F32)
 
 
-def correlate(source_ref, kernel_ref, kind, side, slots, sign, emit):
+def correlate(source_ref, kernel_ref, side, slots, sign, emit):
     channels = source_ref.shape[-1]
 
     def chunk(at, carry):
         lanes = pl.ds(pl.multiple_of(at * LANES, LANES), LANES)
         taps = [
-            jnp.broadcast_to(kernel_ref[tap, :, lanes], (slots, LANES)) * tap_keep(kind, tap)
-            for tap in range(25)
+            jnp.broadcast_to(kernel_ref[tap, :, lanes], (slots, LANES)) for tap in range(25)
         ]
         for row in range(side):
             sums = [None] * side
@@ -170,19 +181,18 @@
     lax.fori_loop(0, channels // LANES, chunk, 0)
 
 
-def forward_kernel(path_ref, at_ref, maps_ref, weight_ref, kernel_ref, *refs, sizes, side):
-    places, samples, sections, capacity = sizes
+def forward_kernel(own_ref, weight_ref, kernel_ref, *refs, sizes, side):
+    _, _, sections, capacity = sizes
     slots = sections * capacity
     got_refs, refs = refs[: sections - 1], refs[sections - 1 :]
     back_refs, refs = refs[: sections - 1], refs[sections - 1 :]
     final_ref, active_ref, scaled_ref, inverse_ref, source_ref = refs
-    kind = lax.rem(at_ref[0], 3)
-    source_ref[...] = gather_slots(path_ref, at_ref, maps_ref, got_refs, sizes)
+    source_ref[...] = gather_slots(own_ref, got_refs, sizes)
 
     def emit(rows, lanes, value):
         scaled_ref[rows, lanes] = value
 
-    correlate(source_ref, kernel_ref, kind, side, slots, 1, emit)
+    correlate(source_ref, kernel_ref, side, slots, 1, emit)
     block = side * slots
     for row in range(side):
         rows = pl.ds(row * block, block)
@@ -197,11 +207,11 @@
     return_slots(final_ref[...], back_refs, sizes)
 
 
-def point_kernel(path_ref, at_ref, replica_ref, grads_ref, active_ref, *refs, sizes, ways):
-    places, samples, sections, capacity = sizes
+def point_kernel(replica_ref, own_ref, active_ref, *refs, sizes, ways):
+    _, _, sections, _ = sizes
     got_refs, refs = refs[: sections - 1], refs[sections - 1 :]
     slot_grads_ref, send_ref, keep_ref, total_ref = refs
-    slot_grads_ref[...] = gather_slots(path_ref, at_ref, grads_ref, got_refs, sizes).astype(BF16)
+    slot_grads_ref[...] = gather_slots(own_ref, got_refs, sizes).astype(BF16)
     total = lax.dot_general(
         active_ref[...], slot_grads_ref[...], (((0,), (0,)), ((), ())), preferred_element_type=F32
     )
@@ -232,14 +242,18 @@
                 at += 1
 
 
+def last_kernel(keep_ref, got_ref, taps_ref, came_ref, point_ref, out_ref):
+    point_ref[...] = keep_ref[0] + got_ref[0].astype(F32)
+    out_ref[...] = taps_ref[...] + came_ref[...]
+
+
 def backward_kernel(
-    at_ref, slot_grads_ref, weight_ref, kernel_ref, scaled_ref, inverse_ref, *refs, sizes, side
+    slot_grads_ref, weight_ref, kernel_ref, scaled_ref, inverse_ref, *refs, sizes, side
 ):
-    places, samples, sections, capacity = sizes
+    _, _, sections, capacity = sizes
     slots = sections * capacity
     back_refs, refs = refs[: sections - 1], refs[sections - 1 :]
     grad_in_ref, mixed_ref, work_ref = refs
-    kind = lax.rem(at_ref[0], 3)
     work_ref[...] = lax.dot_general(
         slot_grads_ref[...], weight_ref[...], (((1,), (1,)), ((), ())), preferred_element_type=F32
     )
@@ -255,7 +269,7 @@
     def emit(rows, lanes, value):
         work_ref[rows, lanes] = value
 
-    correlate(mixed_ref, kernel_ref, kind, side, slots, -1, emit)
+    correlate(mixed_ref, kernel_ref, side, slots, -1, emit)
     grad_in_ref[...] = (slot_grads_ref[...].astype(F32) + work_ref[...]).astype(BF16)
     return_slots(grad_in_ref[...], back_refs, sizes)
 
@@ -293,7 +307,7 @@
     lax.fori_loop(0, channels // LANES, chunk, 0)
 
 
-def call(kernel, name, outs, in_specs, scratch=(), megabytes=20):
+def call(kernel, outs, in_specs, scratch=(), megabytes=20):
     return pl.pallas_call(
         kernel,
         out_shape=outs,
@@ -301,11 +315,10 @@
         out_specs=jax.tree.map(lambda _: VMEM, outs),
         scratch_shapes=list(scratch),
         compiler_params=pltpu.CompilerParams(vmem_limit_bytes=megabytes * 1024 * 1024),
-        name=name,
-    )
-
-
-def body(feature_maps, path_lists, point_weight, depth_kernel, cotangent):
+    )
+
+
+def window(feature_maps, path_lists, point_weight, depth_kernel, cotangent):
     sections = lax.axis_size("segment")
     ways = lax.axis_size("rep")
     at = lax.axis_index("segment").astype(jnp.int32).reshape(1)
@@ -331,12 +344,12 @@
 
     packed = shape(places * capacity, channels, dtype=BF16)
 
-    def pack(rows):
+    def pack(rows, megabytes):
         return call(
             functools.partial(pack_kernel, sizes=sizes),
-            "pack",
             [packed for _ in others],
             [SMEM, SMEM, VMEM],
+            megabytes=megabytes,
         )(path, at, rows)
 
     def swap(pieces, direction):
@@ -352,7 +365,6 @@
     def unpack(slot_rows, pieces):
         return call(
             functools.partial(unpack_kernel, sizes=sizes),
-            "unpack",
             shape(places * samples, channels, dtype=BF16),
             [SMEM, SMEM, VMEM] + [VMEM for _ in others],
         )(path, at, slot_rows, *pieces)
@@ -361,18 +373,23 @@
         return lax.ppermute(value, "rep", [(i, i ^ bit) for i in range(ways)])
 
     maps, grads = rows_of(feature_maps), rows_of(cotangent)
-    got_maps = swap(pack(maps), 1)
-    got_grads = swap(pack(grads), 1)
+    got_maps = swap(pack(maps, 56), 1)
+    got_grads = swap(pack(grads, 20), 1)
 
     slot_shape = shape(places * slots, channels)
     slot_half = shape(places * slots, channels, dtype=BF16)
+    tap_shape = shape(25, 1, channels)
+    own_maps, own_grads, kernel = call(
+        functools.partial(prepare_kernel, sizes=sizes),
+        [slot_half, slot_half, tap_shape],
+        [SMEM, SMEM, VMEM, VMEM, VMEM],
+    )(path, at, maps, grads, kernel)
     results = call(
         functools.partial(forward_kernel, sizes=sizes, side=side),
-        "forward",
         [packed for _ in others]
         + [slot_half, slot_half, slot_shape, shape(places * slots, LANES), slot_shape],
-        [SMEM, SMEM, VMEM, VMEM, VMEM] + [VMEM for _ in others],
-    )(path, at, maps, weight, kernel, *got_maps)
+        [VMEM, VMEM, VMEM] + [VMEM for _ in others],
+    )(own_maps, weight, kernel, *got_maps)
     back = results[: sections - 1]
     slot_final, active, scaled, inverse, source = results[sections - 1 :]
     got_final = swap(back, -1)
@@ -380,30 +397,29 @@
     block = channels // ways
     slot_grads, send, keep = call(
         functools.partial(point_kernel, sizes=sizes, ways=ways),
-        "point",
-        [slot_half, shape(ways // 2, block, channels, dtype=BF16), shape(ways // 2, block, channels)],
-        [SMEM, SMEM, SMEM, VMEM, VMEM] + [VMEM for _ in others],
+        [
+            slot_half,
+            shape(ways // 2, block, channels, dtype=BF16),
+            shape(ways // 2, block, channels),
+        ],
+        [SMEM, VMEM, VMEM] + [VMEM for _ in others],
         [pltpu.VMEM((ways, block, channels), F32)],
-    )(path, at, replica, grads, active, *got_grads)
+    )(replica, own_grads, active, *got_grads)
 
     got = trade(send, 1)
 
     results = call(
         functools.partial(backward_kernel, sizes=sizes, side=side),
-        "backward",
         [packed for _ in others] + [slot_half, slot_shape],
-        [SMEM, VMEM, VMEM, VMEM, VMEM, VMEM],
+        [VMEM, VMEM, VMEM, VMEM, VMEM],
         [pltpu.VMEM((places * slots, channels), F32)],
-    )(at, slot_grads, weight, kernel, scaled, inverse)
+    )(slot_grads, weight, kernel, scaled, inverse)
     back = results[: sections - 1]
     slot_in, mixed = results[sections - 1 :]
     got_in = swap(back, -1)
 
     taps = call(
-        functools.partial(taps_kernel, side=side, slots=slots),
-        "taps",
-        shape(25, 1, channels),
-        [SMEM, VMEM, VMEM],
+        functools.partial(taps_kernel, side=side, slots=slots), tap_shape, [SMEM, VMEM, VMEM]
     )(at, mixed, source)
 
     bits = [1 << i for i in range(1, ways.bit_length() - 1)]
@@ -432,17 +448,20 @@
         outs = [shape(count, block, width, dtype=BF16), shape(count, block, width)] * targets
         results = call(
             functools.partial(fold_kernel, moves=moves, arriving=len(held)),
-            "fold",
             outs,
             [SMEM] + [VMEM] * len(held),
         )(replica, *held)
         held = []
         for part in range(targets):
             held += [results[2 * part + 1], trade(results[2 * part], orders[part][step])]
-    point_grad = (held[0] + held[1].astype(F32))[0]
-
-    for bit in [1] + bits:
-        taps = taps + trade(taps, bit)
+    tap_bits = [1] + bits[::-1]
+    for step, bit in enumerate(tap_bits):
+        came = trade(taps, bit)
+        if step < len(bits):
+            taps = taps + came
+    point_grad, taps = call(
+        last_kernel, [shape(block, channels), tap_shape], [VMEM] * 4
+    )(*held, taps, came)
 
     final_maps = maps_of(unpack(slot_final, got_final))
     input_grad = maps_of(unpack(slot_in, got_in))
@@ -463,7 +482,7 @@
         P(("segment", "rep"), None, None, None),
     )
     return jax.shard_map(
-        body,
+        window,
         mesh=mesh,
         in_specs=placed,
         out_specs=(

time: 69.9 us -> 63.8 us (0.913)
  Pallas kernels: 22.1 us -> 25 us
  local copies, waits for them, and re-layouts: 5.78 us -> 2.95 us
  waiting for transfers between devices: 22.6 us -> 20.2 us
  starting transfers between devices: 16.6 us -> 14.3 us
  other arithmetic: 1.8 us -> 0.32 us
    ppermute x10, waiting for transfers between devices: 13.8 us -> 10.1 us  [trade(): return lax.ppermute(value, 'rep', [(i, i ^ bit) for i in range(ways)])]
    pallas_call x11 -> x13, Pallas kernels: 22.1 us -> 25 us  [the longest x1 4.69 us: window(): call(functools.partial(forward_kernel, sizes=sizes, side=side), [packed f...]
    unnamed x20 -> x14, local copies, waits for them, and re-layouts: 5.78 us -> 2.95 us
    ppermute x10, starting transfers between devices: 11.5 us -> 9.09 us  [trade(): return lax.ppermute(value, 'rep', [(i, i ^ bit) for i in range(ways)])]
    ppermute x4, waiting for transfers between devices: 8.87 us -> 10.1 us  [swap(): lax.ppermute(piece, 'segment', [(i, (i + direction * shift) % sections) f...]
    unnamed x1 -> x0, other arithmetic: 0.75 us -> none
    another operation x1 -> x0, other arithmetic: 0.73 us -> none  [body(): point_grad.reshape(1, 1, block, channels)]
  transfers between devices with their start and end apart: 14 -> 14, of which waited for: 5 -> 7; matrix products, arithmetic and copies ran while one was open for 2% -> 1% of each run, Pallas kernels for 25% -> 31%
where the time goes in v3:
time: 63.8 us; the launch traced here: 63.5 us
  Pallas kernels  25 us (39%)
  waiting for transfers between devices  20.2 us (32%)
  starting transfers between devices  14.3 us (22%)
  local copies, waits for them, and re-layouts  2.95 us (5%)
  between operations  0.77 us (1%)
    ppermute x4, waiting for transfers between devices, swap(): lax.ppermute(piece, 'segment', [(i, (i + direction * shift) % sections) f...  10.1 us
    ppermute x10, waiting for transfers between devices, trade(): return lax.ppermute(value, 'rep', [(i, i ^ bit) for i in range(ways)])  10.1 us
    ppermute x10, starting transfers between devices, trade(): return lax.ppermute(value, 'rep', [(i, i ^ bit) for i in range(ways)])  9.09 us
    ppermute x4, starting transfers between devices, swap(): lax.ppermute(piece, 'segment', [(i, (i + direction * shift) % sections) f...  5.23 us
    pallas_call x1, Pallas kernels, window(): call(functools.partial(forward_kernel, sizes=sizes, side=side), [packed f...  4.69 us
    pallas_call x2, Pallas kernels, unpack(): call(functools.partial(unpack_kernel, sizes=sizes), shape(places * sample...  4.6 us
    pallas_call x2, Pallas kernels, pack(): call(functools.partial(pack_kernel, sizes=sizes), [packed for _ in others...  4.09 us
    pallas_call x1, Pallas kernels, window(): call(functools.partial(backward_kernel, sizes=sizes, side=side), [packed...  3.95 us
  transfers between devices with their start and end apart: 14, of which 7 were waited for; matrix products, arithmetic and copies ran while one was open for 1% of the time, Pallas kernels for 31%

profile of v3, /device:TPU:0, one launch (start us, length us, event | category | flops | bytes accessed | tf_op | source)
XLA Modules:
  0.0 63.5 jit_solution(8412120590044632295)
XLA Ops:
  0.6 0.0 copy-start.6
  0.7 2.4 %shard_map.85 = bf16[196,1024]{1,0:T(8,128)(2,1)} custom-call(s32[8]{0:T(128)} %bitcast.28, s32[1]{0:T(128)} %bitcast.1.at_ref, bf16[392,1024]{1,0:T(8,128)(2,1)} %bitcast.23), custom_call_target="tpu_custom_call" | custom-call | tf_op jit(solution)/shard_map/pallas_call | solution.py:348
  3.1 3.0 %collective-permute-start = (bf16[196,1024]{1,0:T(8,128)(2,1)}, bf16[196,1024]{1,0:T(8,128)(2,1)}, u32[]{:S(2)}, u32[]{:S(2)}) collective-permute-start(bf16[196,1024]{1,0:T(8,128)(2,1)} %shard_map.85), channel_id=1, source_target_pairs={{0,16},{16,0},{1,17},{17,1},{2,18},{18,2},{3,19},{19,3},{4,20},{20... | collective-permute-start | bytes 1204232 | tf_op jit(solution)/shard_map/ppermute | solution.py:357
  6.0 1.1 %copy-done.2 = bf16[8,7,7,1024]{3,0,2,1:T(8,128)(2,1)S(1)} copy-done((bf16[8,7,7,1024]{3,0,2,1:T(8,128)(2,1)S(1)}, bf16[8,7,7,1024]{3,0,2,1:T(8,128)(2,1)}, u32[]{:S(2)}) %copy-start.2) | copy-done | bytes 802840
  7.2 0.7 %copy-done.5 = s32[1,8,1]{1,2,0:T(1,128)S(1)} copy-done((s32[1,8,1]{1,2,0:T(1,128)S(1)}, s32[1,8,1]{1,2,0:T(1,128)}, u32[]{:S(2)}) %copy-start.5) | copy-done | bytes 56
  7.8 1.7 %shard_map.88 = bf16[196,1024]{1,0:T(8,128)(2,1)} custom-call(s32[8]{0:T(128)S(1)} %bitcast.29, s32[1]{0:T(128)} %bitcast.1.at_ref, bf16[392,1024]{1,0:T(8,128)(2,1)S(1)} %bitcast.25), custom_call_target="tpu_custom_call" | custom-call | tf_op jit(solution)/shard_map/pallas_call | solution.py:348
  9.5 0.2 collective-permute-start.2
  9.7 1.1 %copy-done.3 = bf16[8,7,7,1024]{3,0,2,1:T(8,128)(2,1)S(1)} copy-done((bf16[8,7,7,1024]{3,0,2,1:T(8,128)(2,1)S(1)}, bf16[8,7,7,1024]{3,0,2,1:T(8,128)(2,1)}, u32[]{:S(2)}) %copy-start.3) | copy-done | bytes 802840
  10.8 1.6 %shard_map.84 = (bf16[392,1024]{1,0:T(8,128)(2,1)S(1)}, bf16[392,1024]{1,0:T(8,128)(2,1)S(1)}, f32[25,1,1024]{2,1,0:T(1,128)S(1)}) custom-call(s32[8]{0:T(128)S(1)} %bitcast.30, s32[1]{0:T(128)} %bitcast.1.at_ref, bf16[392,1024]{1,0:T(8,128)(2,1)S(1)} %bitcast.24, bf16[392,1024]{1,0:T(8,128)(2,1)S(1)} %bitcast.26, f32[25,1,1024]{2,1,0:T(1,128)S(1)} %bitcast.27), custom_call_target="tpu_custom_call" | custom-call | tf_op jit(solution)/shard_map/pallas_call | solution.py:382
  12.4 4.2 %collective-permute-done.refs_0_ = bf16[196,1024]{1,0:T(8,128)(2,1)} collective-permute-done((bf16[196,1024]{1,0:T(8,128)(2,1)}, bf16[196,1024]{1,0:T(8,128)(2,1)}, u32[]{:S(2)}, u32[]{:S(2)}) %collective-permute-start) | collective-permute-done | bytes 401440 | tf_op jit(solution)/shard_map/ppermute | solution.py:357
  16.7 4.7 %shard_map.86 = (bf16[196,1024]{1,0:T(8,128)(2,1)S(1)}, bf16[392,1024]{1,0:T(8,128)(2,1)S(1)}, bf16[392,1024]{1,0:T(8,128)(2,1)S(1)}, f32[392,1024]{1,0:T(8,128)...) custom-call(bf16[392,1024]{1,0:T(8,128)(2,1)S(1)} %get-tuple-element.31.own_ref, bf16[1024,1024]{1,0:T(8,128)(2,1)S(1)} %bitcast.21, ...), custom_call_target="tpu_custom_call" | custom-call | tf_op jit(solution)/shard_map/pallas_call | solution.py:387
  21.4 3.1 %collective-permute-done.2.refs_0_ = bf16[196,1024]{1,0:T(8,128)(2,1)S(1)} collective-permute-done((bf16[196,1024]{1,0:T(8,128)(2,1)}, bf16[196,1024]{1,0:T(8,128)(2,1)S(1)}, u32[]{:S(2)}, u32[]{:S(2)}) %collective-permute-start.2) | collective-permute-done | bytes 401440 | tf_op jit(solution)/shard_map/ppermute | solution.py:357
  24.5 2.1 %shard_map.89 = (bf16[392,1024]{1,0:T(8,128)(2,1)S(1)}, bf16[8,64,1024]{2,1,0:T(8,128)(2,1)S(1)}, f32[8,64,1024]{2,1,0:T(8,128)S(1)}) custom-call(s32[1]{0:T(128)} %bitcast.11.replica_ref, bf16[392,1024]{1,0:T(8,128)(2,1)S(1)} %get-tuple-element.35.own_ref, bf16[392,1024]{1,0:T(8,128)(2,1)S(1)} %get-tuple-element.36.active_ref, ...), custom_call_target="tpu_custom_call" | custom-call | tf_op jit(solution)/shard_map/pallas_call | solution.py:398
  26.6 0.1 collective-permute-start.4
  26.6 2.6 %collective-permute-done.4.refs_1_ = bf16[8,64,1024]{2,1,0:T(8,128)(2,1)S(1)} collective-permute-done((bf16[8,64,1024]{2,1,0:T(8,128)(2,1)S(1)}, bf16[8,64,1024]{2,1,0:T(8,128)(2,1)S(1)}, u32[]{:S(2)}, u32[]{:S(2)}) %collective-permute-start.4) | collective-permute-done | bytes 1048608 | tf_op jit(solution)/shard_map/ppermute | solution.py:373
  29.3 0.2 shard_map.92
  29.4 1.8 %collective-permute-start.5 = (bf16[4,64,512]{2,1,0:T(8,128)(2,1)S(1)}, bf16[4,64,512]{2,1,0:T(8,128)(2,1)S(1)}, u32[]{:S(2)}, u32[]{:S(2)}) collective-permute-start(bf16[4,64,512]{2,1,0:T(8,128)(2,1)S(1)} %get-tuple-element.45), channel_id=1, source_target_pairs={{0,2},{1,3},{2,0},{3,1},{4,6},{5,7},{6,4},{7,5},{8,10},{9,11},{10,... | collective-permute-start | bytes 786440 | tf_op jit(solution)/shard_map/ppermute | solution.py:373
  31.3 1.6 %collective-permute-start.6 = (bf16[4,64,512]{2,1,0:T(8,128)(2,1)S(1)}, bf16[4,64,512]{2,1,0:T(8,128)(2,1)S(1)}, u32[]{:S(2)}, u32[]{:S(2)}) collective-permute-start(bf16[4,64,512]{2,1,0:T(8,128)(2,1)S(1)} %get-tuple-element.47), channel_id=1, source_target_pairs={{0,4},{1,5},{2,6},{3,7},{4,0},{5,1},{6,2},{7,3},{8,12},{9,13},{10,... | collective-permute-start | bytes 786440 | tf_op jit(solution)/shard_map/ppermute | solution.py:373
  32.9 4.0 %shard_map.90 = (bf16[196,1024]{1,0:T(8,128)(2,1)S(1)}, bf16[392,1024]{1,0:T(8,128)(2,1)S(1)}, f32[392,1024]{1,0:T(8,128)S(1)}) custom-call(bf16[392,1024]{1,0:T(8,128)(2,1)S(1)} %get-tuple-element.37.slot_grads_ref, bf16[1024,1024]{1,0:T(8,128)(2,1)S(1)} %bitcast.22, f32[25,1,1024]{2,1,0:T(1,128)S(1)} %get-tuple-element.32.kernel_ref, ...), custom_call_target="tpu_custom_call" | custom-call | tf_op jit(solution)/shard_map/pallas_call | solution.py:411
  36.8 2.9 %shard_map.95 = f32[25,1,1024]{2,1,0:T(1,128)S(1)} custom-call(s32[1]{0:T(128)} %bitcast.1.at_ref, f32[392,1024]{1,0:T(8,128)S(1)} %get-tuple-element.54.mixed_ref, f32[392,1024]{1,0:T(8,128)S(1)} %get-tuple-element.55.source_ref), custom_call_target="tpu_custom_call" | custom-call | tf_op jit(solution)/shard_map/pallas_call | solution.py:421
  39.7 0.1 collective-permute-start.10
  39.8 1.6 %collective-permute-start.1 = (bf16[196,1024]{1,0:T(8,128)(2,1)S(1)}, bf16[196,1024]{1,0:T(8,128)(2,1)S(1)}, u32[]{:S(2)}, u32[]{:S(2)}) collective-permute-start(bf16[196,1024]{1,0:T(8,128)(2,1)S(1)} %get-tuple-element.34), channel_id=1, source_target_pairs={{0,16},{16,0},{1,17},{17,1},{2,18},{18,2},{3,19},{19,3},{4,20},{20... | collective-permute-start | bytes 1204232 | tf_op jit(solution)/shard_map/ppermute | solution.py:357
  41.4 0.5 collective-permute-start.3
  41.9 0.0 collective-permute-done.10
  41.9 0.1 add.9
  42.0 2.7 %collective-permute-start.11 = (f32[25,1,1024]{2,1,0:T(1,128)S(1)}, f32[25,1,1024]{2,1,0:T(1,128)S(1)}, u32[]{:S(2)}, u32[]{:S(2)}) collective-permute-start(f32[25,1,1024]{2,1,0:T(1,128)S(1)} %add.9), channel_id=1, source_target_pairs={{0,8},{1,9},{2,10},{3,11},{4,12},{5,13},{6,14},{7,15},{8,0},{9,1},... | collective-permute-start | bytes 307208 | tf_op jit(solution)/shard_map/ppermute | solution.py:373
  44.7 0.0 collective-permute-done.5.refs_1_
  44.7 0.0 collective-permute-done.6.refs_3_
  44.7 0.1 shard_map.93
  44.8 0.5 collective-permute-start.7
  45.3 0.5 collective-permute-start.8
  45.8 4.0 %collective-permute-done.11 = f32[25,1,1024]{2,1,0:T(1,128)S(1)} collective-permute-done((f32[25,1,1024]{2,1,0:T(1,128)S(1)}, f32[25,1,1024]{2,1,0:T(1,128)S(1)}, u32[]{:S(2)}, u32[]{:S(2)}) %collective-permute-start.11) | collective-permute-done | bytes 102432 | tf_op jit(solution)/shard_map/ppermute | solution.py:373
  49.8 0.1 add.10
  49.9 0.1 collective-permute-start.12
  50.0 1.9 %collective-permute-done.7.refs_1_ = bf16[2,64,512]{2,1,0:T(8,128)(2,1)S(1)} collective-permute-done((bf16[2,64,512]{2,1,0:T(8,128)(2,1)S(1)}, bf16[2,64,512]{2,1,0:T(8,128)(2,1)S(1)}, u32[]{:S(2)}, u32[]{:S(2)}) %collective-permute-start.7) | collective-permute-done | bytes 131104 | tf_op jit(solution)/shard_map/ppermute | solution.py:373
  51.9 0.0 collective-permute-done.8.refs_3_
  51.9 0.1 shard_map.94
  52.0 1.3 %collective-permute-start.9 = (bf16[1,64,1024]{2,1,0:T(8,128)(2,1)S(1)}, bf16[1,64,1024]{2,1,0:T(8,128)(2,1)S(1)}, u32[]{:S(2)}, u32[]{:S(2)}) collective-permute-start(bf16[1,64,1024]{2,1,0:T(8,128)(2,1)S(1)} %get-tuple-element.53), channel_id=1, source_target_pairs={{0,8},{1,9},{2,10},{3,11},{4,12},{5,13},{6,14},{7,15},{8,0},{9,1},... | collective-permute-start | bytes 393224 | tf_op jit(solution)/shard_map/ppermute | solution.py:373
  53.2 1.5 %collective-permute-done.12 = f32[25,1,1024]{2,1,0:T(1,128)S(1)} collective-permute-done((f32[25,1,1024]{2,1,0:T(1,128)S(1)}, f32[25,1,1024]{2,1,0:T(1,128)S(1)}, u32[]{:S(2)}, u32[]{:S(2)}) %collective-permute-start.12) | collective-permute-done | bytes 102432 | tf_op jit(solution)/shard_map/ppermute | solution.py:373
  54.7 0.1 add.11.taps_ref
  54.9 0.5 collective-permute-start.13
  55.4 0.0 collective-permute-done.1.refs_0_
  55.4 2.3 %shard_map.87 = bf16[392,1024]{1,0:T(8,128)(2,1)} custom-call(s32[8]{0:T(128)S(1)} %bitcast.31, s32[1]{0:T(128)} %bitcast.1.at_ref, bf16[392,1024]{1,0:T(8,128)(2,1)S(1)} %get-tuple-element.33.slots_ref, bf16[196,1024]{1,0:T(8,128)(2,1)S(1)} %collective-permute-done.1.refs_0_), custom_call_target="tpu_custom_call" | custom-call | tf_op jit(solution)/shard_map/pallas_call | solution.py:366
  57.7 2.8 %collective-permute-done.3.refs_0_ = bf16[196,1024]{1,0:T(8,128)(2,1)S(1)} collective-permute-done((bf16[196,1024]{1,0:T(8,128)(2,1)S(1)}, bf16[196,1024]{1,0:T(8,128)(2,1)S(1)}, u32[]{:S(2)}, u32[]{:S(2)}) %collective-permute-start.3) | collective-permute-done | bytes 401440 | tf_op jit(solution)/shard_map/ppermute | solution.py:357
  60.5 2.3 %shard_map.91 = bf16[392,1024]{1,0:T(8,128)(2,1)} custom-call(s32[8]{0:T(128)S(1)} %bitcast.32, s32[1]{0:T(128)} %bitcast.1.at_ref, bf16[392,1024]{1,0:T(8,128)(2,1)S(1)} %get-tuple-element.40.slots_ref, bf16[196,1024]{1,0:T(8,128)(2,1)S(1)} %collective-permute-done.3.refs_0_), custom_call_target="tpu_custom_call" | custom-call | tf_op jit(solution)/shard_map/pallas_call | solution.py:366
  62.8 0.0 collective-permute-done.13.came_ref
  62.8 0.0 collective-permute-done.9.got_ref
  62.8 0.8 %shard_map.96 = (f32[64,1024]{1,0:T(8,128)}, f32[25,1,1024]{2,1,0:T(1,128)}) custom-call(f32[1,64,1024]{2,1,0:T(8,128)S(1)} %get-tuple-element.52.keep_ref, bf16[1,64,1024]{2,1,0:T(8,128)(2,1)S(1)} %collective-permute-done.9.got_ref, f32[25,1,1024]{2,1,0:T(1,128)S(1)} %add.11.taps_ref, f32[25,1,1024]{2,1,0:T(1,128)S(1)} %collective-permute-done.13.came_ref), custom_call_target="tpu_custom_call" | custom-call | tf_op jit(solution)/shard_map/pallas_call | solution.py:462
  (10 shorter events, 0.0 us)
Async XLA Ops:
  0.6 9.1 %copy-start.6 = (s32[1,8,1]{1,2,0:T(1,128)S(1)}, s32[1,8,1]{1,2,0:T(1,128)}, u32[]{:S(2)}) copy-start(s32[1,8,1]{1,2,0:T(1,128)} %param.6) | copy-start | bytes 100
  0.6 9.1 %copy-start.1 = (bf16[8,7,7,1024]{3,0,2,1:T(8,128)(2,1)S(1)}, bf16[8,7,7,1024]{3,0,2,1:T(8,128)(2,1)}, u32[]{:S(2)}) copy-start(bf16[8,7,7,1024]{3,0,2,1:T(8,128)(2,1)} %param.5) | copy-start | bytes 2408452
  0.7 9.0 %copy-start.4 = (f32[1,1,25,1024]{3,1,2,0:T(1,128)S(1)}, f32[1,1,25,1024]{3,1,2,0:T(1,128)}, u32[]{:S(2)}) copy-start(f32[1,1,25,1024]{3,1,2,0:T(1,128)} %param.8) | copy-start | bytes 307204
  3.0 13.6 %copy-start = (bf16[1,1,1024,1024]{3,2,1,0:T(8,128)(2,1)S(1)}, bf16[1,1,1024,1024]{3,2,1,0:T(8,128)(2,1)}, u32[]{:S(2)}) copy-start(bf16[1,1,1024,1024]{3,2,1,0:T(8,128)(2,1)} %param.7) | copy-start | bytes 6291460
  3.1 13.6 %collective-permute-start = (bf16[196,1024]{1,0:T(8,128)(2,1)}, bf16[196,1024]{1,0:T(8,128)(2,1)}, u32[]{:S(2)}, u32[]{:S(2)}) collective-permute-start(bf16[196,1024]{1,0:T(8,128)(2,1)} %shard_map.85), channel_id=1, source_target_pairs={{0,16},{16,0},{1,17},{17,1},{2,18},{18,2},{3,19},{19,3},{4,20},{20... | collective-permute-start | bytes 1204232 | tf_op jit(solution)/shard_map/ppermute | solution.py:357
  6.0 1.1 %copy-start.2 = (bf16[8,7,7,1024]{3,0,2,1:T(8,128)(2,1)S(1)}, bf16[8,7,7,1024]{3,0,2,1:T(8,128)(2,1)}, u32[]{:S(2)}) copy-start(bf16[8,7,7,1024]{3,0,2,1:T(8,128)(2,1)} %param.9) | copy-start | bytes 2408452
  7.2 0.7 %copy-start.5 = (s32[1,8,1]{1,2,0:T(1,128)S(1)}, s32[1,8,1]{1,2,0:T(1,128)}, u32[]{:S(2)}) copy-start(s32[1,8,1]{1,2,0:T(1,128)} %param.6) | copy-start | bytes 100
  9.5 14.9 %collective-permute-start.2 = (bf16[196,1024]{1,0:T(8,128)(2,1)}, bf16[196,1024]{1,0:T(8,128)(2,1)S(1)}, u32[]{:S(2)}, u32[]{:S(2)}) collective-permute-start(bf16[196,1024]{1,0:T(8,128)(2,1)} %shard_map.88), channel_id=1, source_target_pairs={{0,16},{16,0},{1,17},{17,1},{2,18},{18,2},{3,19},{19,3},{4,20},{20... | collective-permute-start | bytes 1204232 | tf_op jit(solution)/shard_map/ppermute | solution.py:357
  9.7 1.1 %copy-start.3 = (bf16[8,7,7,1024]{3,0,2,1:T(8,128)(2,1)S(1)}, bf16[8,7,7,1024]{3,0,2,1:T(8,128)(2,1)}, u32[]{:S(2)}) copy-start(bf16[8,7,7,1024]{3,0,2,1:T(8,128)(2,1)} %param.9) | copy-start | bytes 2408452
  26.6 2.7 %collective-permute-start.4 = (bf16[8,64,1024]{2,1,0:T(8,128)(2,1)S(1)}, bf16[8,64,1024]{2,1,0:T(8,128)(2,1)S(1)}, u32[]{:S(2)}, u32[]{:S(2)}) collective-permute-start(bf16[8,64,1024]{2,1,0:T(8,128)(2,1)S(1)} %get-tuple-element.43), channel_id=1, source_target_pairs={{0,1},{1,0},{2,3},{3,2},{4,5},{5,4},{6,7},{7,6},{8,9},{9,8},{10,11... | collective-permute-start | bytes 3145736 | tf_op jit(solution)/shard_map/ppermute | solution.py:373
  29.4 15.2 %collective-permute-start.5 = (bf16[4,64,512]{2,1,0:T(8,128)(2,1)S(1)}, bf16[4,64,512]{2,1,0:T(8,128)(2,1)S(1)}, u32[]{:S(2)}, u32[]{:S(2)}) collective-permute-start(bf16[4,64,512]{2,1,0:T(8,128)(2,1)S(1)} %get-tuple-element.45), channel_id=1, source_target_pairs={{0,2},{1,3},{2,0},{3,1},{4,6},{5,7},{6,4},{7,5},{8,10},{9,11},{10,... | collective-permute-start | bytes 786440 | tf_op jit(solution)/shard_map/ppermute | solution.py:373
  31.3 13.4 %collective-permute-start.6 = (bf16[4,64,512]{2,1,0:T(8,128)(2,1)S(1)}, bf16[4,64,512]{2,1,0:T(8,128)(2,1)S(1)}, u32[]{:S(2)}, u32[]{:S(2)}) collective-permute-start(bf16[4,64,512]{2,1,0:T(8,128)(2,1)S(1)} %get-tuple-element.47), channel_id=1, source_target_pairs={{0,4},{1,5},{2,6},{3,7},{4,0},{5,1},{6,2},{7,3},{8,12},{9,13},{10,... | collective-permute-start | bytes 786440 | tf_op jit(solution)/shard_map/ppermute | solution.py:373
  39.7 2.2 %collective-permute-start.10 = (f32[25,1,1024]{2,1,0:T(1,128)S(1)}, f32[25,1,1024]{2,1,0:T(1,128)S(1)}, u32[]{:S(2)}, u32[]{:S(2)}) collective-permute-start(f32[25,1,1024]{2,1,0:T(1,128)S(1)} %shard_map.95), channel_id=1, source_target_pairs={{0,1},{1,0},{2,3},{3,2},{4,5},{5,4},{6,7},{7,6},{8,9},{9,8},{10,11... | collective-permute-start | bytes 307208 | tf_op jit(solution)/shard_map/ppermute | solution.py:373
  39.8 15.6 %collective-permute-start.1 = (bf16[196,1024]{1,0:T(8,128)(2,1)S(1)}, bf16[196,1024]{1,0:T(8,128)(2,1)S(1)}, u32[]{:S(2)}, u32[]{:S(2)}) collective-permute-start(bf16[196,1024]{1,0:T(8,128)(2,1)S(1)} %get-tuple-element.34), channel_id=1, source_target_pairs={{0,16},{16,0},{1,17},{17,1},{2,18},{18,2},{3,19},{19,3},{4,20},{20... | collective-permute-start | bytes 1204232 | tf_op jit(solution)/shard_map/ppermute | solution.py:357
  41.4 19.1 %collective-permute-start.3 = (bf16[196,1024]{1,0:T(8,128)(2,1)S(1)}, bf16[196,1024]{1,0:T(8,128)(2,1)S(1)}, u32[]{:S(2)}, u32[]{:S(2)}) collective-permute-start(bf16[196,1024]{1,0:T(8,128)(2,1)S(1)} %get-tuple-element.41), channel_id=1, source_target_pairs={{0,16},{16,0},{1,17},{17,1},{2,18},{18,2},{3,19},{19,3},{4,20},{20... | collective-permute-start | bytes 1204232 | tf_op jit(solution)/shard_map/ppermute | solution.py:357
  42.0 7.8 %collective-permute-start.11 = (f32[25,1,1024]{2,1,0:T(1,128)S(1)}, f32[25,1,1024]{2,1,0:T(1,128)S(1)}, u32[]{:S(2)}, u32[]{:S(2)}) collective-permute-start(f32[25,1,1024]{2,1,0:T(1,128)S(1)} %add.9), channel_id=1, source_target_pairs={{0,8},{1,9},{2,10},{3,11},{4,12},{5,13},{6,14},{7,15},{8,0},{9,1},... | collective-permute-start | bytes 307208 | tf_op jit(solution)/shard_map/ppermute | solution.py:373
  44.8 7.1 %collective-permute-start.7 = (bf16[2,64,512]{2,1,0:T(8,128)(2,1)S(1)}, bf16[2,64,512]{2,1,0:T(8,128)(2,1)S(1)}, u32[]{:S(2)}, u32[]{:S(2)}) collective-permute-start(bf16[2,64,512]{2,1,0:T(8,128)(2,1)S(1)} %get-tuple-element.49), channel_id=1, source_target_pairs={{0,4},{1,5},{2,6},{3,7},{4,0},{5,1},{6,2},{7,3},{8,12},{9,13},{10,... | collective-permute-start | bytes 393224 | tf_op jit(solution)/shard_map/ppermute | solution.py:373
  45.3 6.6 %collective-permute-start.8 = (bf16[2,64,512]{2,1,0:T(8,128)(2,1)S(1)}, bf16[2,64,512]{2,1,0:T(8,128)(2,1)S(1)}, u32[]{:S(2)}, u32[]{:S(2)}) collective-permute-start(bf16[2,64,512]{2,1,0:T(8,128)(2,1)S(1)} %get-tuple-element.51), channel_id=1, source_target_pairs={{0,2},{1,3},{2,0},{3,1},{4,6},{5,7},{6,4},{7,5},{8,10},{9,11},{10,... | collective-permute-start | bytes 393224 | tf_op jit(solution)/shard_map/ppermute | solution.py:373
  49.9 4.8 %collective-permute-start.12 = (f32[25,1,1024]{2,1,0:T(1,128)S(1)}, f32[25,1,1024]{2,1,0:T(1,128)S(1)}, u32[]{:S(2)}, u32[]{:S(2)}) collective-permute-start(f32[25,1,1024]{2,1,0:T(1,128)S(1)} %add.10), channel_id=1, source_target_pairs={{0,4},{1,5},{2,6},{3,7},{4,0},{5,1},{6,2},{7,3},{8,12},{9,13},{10,... | collective-permute-start | bytes 307208 | tf_op jit(solution)/shard_map/ppermute | solution.py:373
  52.0 10.8 %collective-permute-start.9 = (bf16[1,64,1024]{2,1,0:T(8,128)(2,1)S(1)}, bf16[1,64,1024]{2,1,0:T(8,128)(2,1)S(1)}, u32[]{:S(2)}, u32[]{:S(2)}) collective-permute-start(bf16[1,64,1024]{2,1,0:T(8,128)(2,1)S(1)} %get-tuple-element.53), channel_id=1, source_target_pairs={{0,8},{1,9},{2,10},{3,11},{4,12},{5,13},{6,14},{7,15},{8,0},{9,1},... | collective-permute-start | bytes 393224 | tf_op jit(solution)/shard_map/ppermute | solution.py:373
  54.9 7.9 %collective-permute-start.13 = (f32[25,1,1024]{2,1,0:T(1,128)S(1)}, f32[25,1,1024]{2,1,0:T(1,128)S(1)}, u32[]{:S(2)}, u32[]{:S(2)}) collective-permute-start(f32[25,1,1024]{2,1,0:T(1,128)S(1)} %add.11.taps_ref), channel_id=1, source_target_pairs={{0,2},{1,3},{2,0},{3,1},{4,6},{5,7},{6,4},{7,5},{8,10},{9,11},{10,... | collective-permute-start | bytes 307208 | tf_op jit(solution)/shard_map/ppermute | solution.py:373

commit v4 on v3

v4 whole, which is shorter than its diff:
```python
import functools

import jax
import jax.numpy as jnp
from jax import lax
from jax.experimental import pallas as pl
from jax.experimental.pallas import tpu as pltpu
from jax.sharding import PartitionSpec as P


EPS = 1e-05
LANES = 128
F32 = jnp.float32
BF16 = jnp.bfloat16

VMEM = pl.BlockSpec(memory_space=pltpu.VMEM)
SMEM = pl.BlockSpec(memory_space=pltpu.SMEM)


def iota2(shape, axis):
    return lax.broadcasted_iota(jnp.int32, shape, axis)


def split(value, size):
    if size & (size - 1) == 0:
        return value >> (size.bit_length() - 1), value & (size - 1)
    quotient = lax.div(value, jnp.int32(size))
    return quotient, value - quotient * size


def slot_codes(path_ref, samples, capacity):
    names = [path_ref[i] for i in range(samples)]
    codes = []
    for i in range(samples):
        rank = jnp.int32(0)
        for j in range(i):
            rank = rank + jnp.where(names[j] == names[i], 1, 0)
        codes.append(names[i] * capacity + rank)
    return codes


def spread_codes(codes, which):
    out = jnp.zeros(which.shape, jnp.int32)
    for i, code in enumerate(codes):
        out = jnp.where(which == i, code, out)
    return out


def one_hot(mask):
    return jnp.where(mask, 1.0, 0.0).astype(BF16)


def pick(matrix, rows):
    return lax.dot_general(matrix, rows, (((1,), (0,)), ((), ())), preferred_element_type=F32)


def pack_matrix(code_row, at, shift, sizes):
    places, samples, sections, capacity = sizes
    row_place, row_slot = split(iota2((places * capacity, places * samples), 0), capacity)
    col_place, _ = split(iota2((1, places * samples), 1), samples)
    target = lax.rem(at + shift, sections)
    return one_hot((row_place == col_place) & (code_row == target * capacity + row_slot))


def first_pack_kernel(path_ref, at_ref, maps_ref, *refs, sizes):
    places, samples, sections, capacity = sizes
    out_refs, code_ref = refs[:-1], refs[-1]
    codes = slot_codes(path_ref, samples, capacity)
    _, col_sample = split(iota2((1, places * samples), 1), samples)
    code_row = spread_codes(codes, col_sample)
    for shift in range(1, sections):
        matrix = pack_matrix(code_row, at_ref[0], shift, sizes)
        out_refs[shift - 1][...] = pick(matrix, maps_ref[...]).astype(BF16)
    code_ref[...] = jnp.broadcast_to(code_row, code_ref.shape)


def second_pack_kernel(code_ref, at_ref, maps_ref, *out_refs, sizes):
    _, _, sections, _ = sizes
    for shift in range(1, sections):
        matrix = pack_matrix(code_ref[:1, :], at_ref[0], shift, sizes)
        out_refs[shift - 1][...] = pick(matrix, maps_ref[...]).astype(BF16)


def prepare_kernel(path_ref, at_ref, code_ref, maps_ref, grads_ref, kernel_ref, *refs, sizes):
    places, samples, sections, capacity = sizes
    slots = sections * capacity
    own_maps_ref, own_grads_ref, taps_ref, place_ref, fetch_ref, home_ref, merge_ref = refs
    row_place, row_slot = split(iota2((places * slots, places * samples), 0), slots)
    col_place, _ = split(iota2((1, places * samples), 1), samples)
    mask = (
        (row_place == col_place)
        & (row_slot < capacity)
        & (code_ref[:1, :] == at_ref[0] * capacity + row_slot)
    )
    matrix = one_hot(mask)
    own_maps_ref[...] = pick(matrix, maps_ref[...]).astype(BF16)
    own_grads_ref[...] = pick(matrix, grads_ref[...]).astype(BF16)
    kind = lax.rem(at_ref[0], 3)
    for tap in range(25):
        taps_ref[tap] = kernel_ref[tap] * tap_keep(kind, tap)

    row_place, row_slot = split(iota2((places * slots, places * capacity), 0), slots)
    col_place, col_slot = split(iota2((1, places * capacity), 1), capacity)
    for shift in range(1, sections):
        mask = (row_place == col_place) & (row_slot == shift * capacity + col_slot)
        place_ref[shift - 1] = one_hot(mask)
    row_place, row_slot = split(iota2((places * capacity, places * slots), 0), capacity)
    col_place, col_slot = split(iota2((1, places * slots), 1), slots)
    for shift in range(1, sections):
        mask = (row_place == col_place) & (col_slot == shift * capacity + row_slot)
        fetch_ref[shift - 1] = one_hot(mask)

    codes = slot_codes(path_ref, samples, capacity)
    row_place, row_sample = split(iota2((places * samples, 1), 0), samples)
    row_code = spread_codes(codes, row_sample)
    col_place, col_slot = split(iota2((1, places * slots), 1), slots)
    mask = (
        (row_place == col_place)
        & (col_slot < capacity)
        & (row_code == at_ref[0] * capacity + col_slot)
    )
    home_ref[...] = one_hot(mask)
    col_place, col_slot = split(iota2((1, places * capacity), 1), capacity)
    for shift in range(1, sections):
        target = lax.rem(at_ref[0] + shift, sections)
        mask = (row_place == col_place) & (row_code == target * capacity + col_slot)
        merge_ref[shift - 1] = one_hot(mask)


def gather_slots(own_ref, place_ref, got_refs):
    total = own_ref[...].astype(F32)
    for at, got_ref in enumerate(got_refs):
        total = total + pick(place_ref[at], got_ref[...])
    return total


def return_slots(slot_rows, fetch_ref, out_refs):
    for at, out_ref in enumerate(out_refs):
        out_ref[...] = pick(fetch_ref[at], slot_rows).astype(BF16)


def unpack_kernel(home_ref, merge_ref, slots_ref, *refs):
    got_refs, out_ref = refs[:-1], refs[-1]
    total = pick(home_ref[...], slots_ref[...])
    for at, got_ref in enumerate(got_refs):
        total = total + pick(merge_ref[at], got_ref[...])
    out_ref[...] = total.astype(BF16)


def tap_keep(kind, tap):
    row_shift, col_shift = tap // 5 - 2, tap % 5 - 2
    narrow = abs(row_shift) <= 1 and abs(col_shift) <= 1
    spaced = row_shift % 2 == 0 and col_shift % 2 == 0
    keep = kind == 1
    if narrow:
        keep = keep | (kind == 0)
    if spaced:
        keep = keep | (kind == 2)
    return jnp.where(keep, 1.0, 0.0).astype(F32)


def correlate(source_ref, kernel_ref, side, slots, sign, emit):
    channels = source_ref.shape[-1]

    def chunk(at, carry):
        lanes = pl.ds(pl.multiple_of(at * LANES, LANES), LANES)
        taps = [
            jnp.broadcast_to(kernel_ref[tap, :, lanes], (slots, LANES)) for tap in range(25)
        ]
        for row in range(side):
            sums = [None] * side
            for row_shift in range(-2, 3):
                source_row = row + sign * row_shift
                if not 0 <= source_row < side:
                    continue
                cells = [
                    source_ref[pl.ds((source_row * side + col) * slots, slots), lanes]
                    for col in range(side)
                ]
                for col_shift in range(-2, 3):
                    tap = taps[(row_shift + 2) * 5 + col_shift + 2]
                    for col in range(side):
                        source_col = col + sign * col_shift
                        if not 0 <= source_col < side:
                            continue
                        term = tap * cells[source_col]
                        sums[col] = term if sums[col] is None else sums[col] + term
            for col in range(side):
                emit(pl.ds((row * side + col) * slots, slots), lanes, sums[col])
        return carry

    lax.fori_loop(0, channels // LANES, chunk, 0)


def deal(replica_ref, rows_ref, give_ref, hold_ref):
    low = replica_ref[0] & 1
    count, block = give_ref.shape[0], give_ref.shape[1]
    for at in range(count):
        give_ref[at] = rows_ref[pl.ds(pl.multiple_of((2 * at + 1 - low) * block, block), block), :]
        hold_ref[at] = rows_ref[pl.ds(pl.multiple_of((2 * at + low) * block, block), block), :]


def forward_kernel(replica_ref, own_ref, place_ref, fetch_ref, weight_ref, kernel_ref, *refs, sizes, side):
    _, _, sections, capacity = sizes
    slots = sections * capacity
    got_refs, refs = refs[: sections - 1], refs[sections - 1 :]
    back_refs, refs = refs[: sections - 1], refs[sections - 1 :]
    give_refs, refs = refs[: sections - 1], refs[sections - 1 :]
    hold_refs, refs = refs[: sections - 1], refs[sections - 1 :]
    final_ref, active_ref, scaled_ref, inverse_ref, source_ref, turned_ref = refs
    source_ref[...] = gather_slots(own_ref, place_ref, got_refs)

    def emit(rows, lanes, value):
        scaled_ref[rows, lanes] = value

    correlate(source_ref, kernel_ref, side, slots, 1, emit)
    block = side * slots
    for row in range(side):
        rows = pl.ds(row * block, block)
        mixed = scaled_ref[rows, :]
        inverse = lax.rsqrt(jnp.mean(mixed * mixed, axis=-1, keepdims=True) + EPS)
        scaled = mixed * inverse
        scaled_ref[rows, :] = scaled
        inverse_ref[rows, :] = jnp.broadcast_to(inverse, (block, LANES))
        active_ref[rows, :] = (scaled * jax.nn.sigmoid(scaled)).astype(BF16)
    branch = pick(active_ref[...], weight_ref[...])
    final_ref[...] = (source_ref[...] + branch).astype(BF16)
    return_slots(final_ref[...], fetch_ref, back_refs)
    for at in range(sections - 1):
        turned = lax.dot_general(
            active_ref[...], fetch_ref[at], (((0,), (1,)), ((), ())), preferred_element_type=F32
        )
        turned_ref[...] = turned.astype(BF16)
        deal(replica_ref, turned_ref, give_refs[at], hold_refs[at])


def own_point_kernel(replica_ref, active_ref, own_ref, give_ref, hold_ref, total_ref):
    total_ref[...] = lax.dot_general(
        active_ref[...], own_ref[...], (((0,), (0,)), ((), ())), preferred_element_type=F32
    )
    deal(replica_ref, total_ref, give_ref, hold_ref)


def point_kernel(own_ref, *refs):
    out_ref = refs[-1]
    active_refs, got_refs = refs[: len(refs) // 2], refs[len(refs) // 2 : -1]
    shape = own_ref.shape
    total = own_ref[...].reshape(shape[0] * shape[1], shape[2])
    for active_ref, got_ref in zip(active_refs, got_refs):
        active = active_ref[...].reshape(shape[0] * shape[1], active_ref.shape[2])
        total = total + pick(active, got_ref[...])
    out_ref[...] = total.reshape(shape).astype(out_ref.dtype)


def fold_kernel(replica_ref, keep_ref, got_ref, send_ref, left_ref, *, strides, bits):
    core = replica_ref[0] & 1
    mine = jnp.where(core == 0, (replica_ref[0] // bits[0]) & 1, (replica_ref[0] // bits[1]) & 1)
    for at in range(send_ref.shape[0]):
        low, high = [(at // stride) * 2 * stride + at % stride for stride in strides]
        base = jnp.where(core == 0, low, high)
        step = jnp.where(core == 0, strides[0], strides[1])
        give = base + step * (1 - mine)
        hold = base + step * mine
        send_ref[at] = (keep_ref[give] + got_ref[give].astype(F32)).astype(BF16)
        left_ref[at] = keep_ref[hold] + got_ref[hold].astype(F32)


def last_kernel(replica_ref, keep_ref, got_ref, taps_ref, came_ref, point_ref, out_ref):
    point_ref[...] = keep_ref[0] + got_ref[0].astype(F32)
    core = replica_ref[0] & 1
    half = taps_ref.shape[-1]
    out_ref[:, :, pl.ds(pl.multiple_of(core * half, LANES), half)] = taps_ref[...]
    out_ref[:, :, pl.ds(pl.multiple_of((1 - core) * half, LANES), half)] = came_ref[...]


def mixed_kernel(own_ref, place_ref, weight_ref, scaled_ref, inverse_ref, *refs, block):
    got_refs, (slot_grads_ref, mixed_ref, work_ref) = refs[:-3], refs[-3:]
    slot_grads_ref[...] = gather_slots(own_ref, place_ref, got_refs).astype(BF16)
    work_ref[...] = lax.dot_general(
        slot_grads_ref[...], weight_ref[...], (((1,), (1,)), ((), ())), preferred_element_type=F32
    )
    for at in range(0, work_ref.shape[0], block):
        rows = pl.ds(at, block)
        scaled = scaled_ref[rows, :]
        logistic = jax.nn.sigmoid(scaled)
        grad_scaled = work_ref[rows, :] * logistic * (1.0 + scaled * (1.0 - logistic))
        mean = jnp.mean(grad_scaled * scaled, axis=-1, keepdims=True)
        mixed_ref[rows, :] = inverse_ref[rows, :1] * (grad_scaled - scaled * mean)


def backward_kernel(slot_grads_ref, fetch_ref, kernel_ref, mixed_ref, *refs, side, slots):
    back_refs, grad_in_ref, work_ref = refs[:-2], refs[-2], refs[-1]

    def emit(rows, lanes, value):
        work_ref[rows, lanes] = value

    correlate(mixed_ref, kernel_ref, side, slots, -1, emit)
    grad_in_ref[...] = (slot_grads_ref[...].astype(F32) + work_ref[...]).astype(BF16)
    return_slots(grad_in_ref[...], fetch_ref, back_refs)


def taps_kernel(at_ref, replica_ref, mixed_ref, source_ref, out_ref, *, side, slots, flip):
    kind = lax.rem(at_ref[0], 3)
    half = out_ref.shape[-1]
    which = (replica_ref[0] & 1) ^ flip

    def chunk(at, carry):
        lanes = pl.ds(pl.multiple_of(which * half + at * LANES, LANES), LANES)
        target = pl.ds(pl.multiple_of(at * LANES, LANES), LANES)

        def cells(ref, row):
            return [ref[pl.ds((row * side + col) * slots, slots), lanes] for col in range(side)]

        sums = [None] * 25
        for row in range(side):
            grads = cells(mixed_ref, row)
            for row_shift in range(-2, 3):
                if not 0 <= row + row_shift < side:
                    continue
                source = cells(source_ref, row + row_shift)
                for col_shift in range(-2, 3):
                    tap = (row_shift + 2) * 5 + col_shift + 2
                    for col in range(side):
                        if not 0 <= col + col_shift < side:
                            continue
                        term = grads[col] * source[col + col_shift]
                        sums[tap] = term if sums[tap] is None else sums[tap] + term
        for tap in range(25):
            out_ref[tap, :, target] = (
                jnp.sum(sums[tap], axis=0, keepdims=True) * tap_keep(kind, tap)
            )
        return carry

    lax.fori_loop(0, half // LANES, chunk, 0)


def call(kernel, outs, in_specs, scratch=(), megabytes=20):
    return pl.pallas_call(
        kernel,
        out_shape=outs,
        in_specs=in_specs,
        out_specs=jax.tree.map(lambda _: VMEM, outs),
        scratch_shapes=list(scratch),
        compiler_params=pltpu.CompilerParams(vmem_limit_bytes=megabytes * 1024 * 1024),
    )


def window(feature_maps, path_lists, point_weight, depth_kernel, cotangent):
    sections = lax.axis_size("segment")
    ways = lax.axis_size("rep")
    at = lax.axis_index("segment").astype(jnp.int32).reshape(1)
    replica = lax.axis_index("rep").astype(jnp.int32).reshape(1)
    samples, side, _, channels = feature_maps.shape
    places = side * side
    capacity = max(max(2, samples // 4), (samples + sections - 1) // sections)
    slots = sections * capacity
    sizes = (places, samples, sections, capacity)
    path = path_lists[0, :, 0]
    weight = point_weight[0, 0]
    kernel = depth_kernel[0, 0].reshape(25, 1, channels)
    others = range(1, sections)

    def rows_of(maps):
        return jnp.transpose(maps, (1, 2, 0, 3)).reshape(places * samples, channels)

    def maps_of(rows):
        return jnp.transpose(rows.reshape(side, side, samples, channels), (2, 0, 1, 3))

    def shape(*dims, dtype=F32):
        return jax.ShapeDtypeStruct(dims, dtype)

    packed = shape(places * capacity, channels, dtype=BF16)

    def swap(pieces, direction):
        return [
            lax.ppermute(
                piece,
                "segment",
                [(i, (i + direction * shift) % sections) for i in range(sections)],
            )
            for shift, piece in zip(others, pieces)
        ]

    def unpack(slot_rows, pieces):
        return call(
            unpack_kernel, shape(places * samples, channels, dtype=BF16), [VMEM] * (3 + len(pieces))
        )(home, merge, slot_rows, *pieces)

    def trade(value, pair):
        return lax.ppermute(value, "rep", [(i, i ^ pair[i & 1]) for i in range(ways)])

    maps, grads = rows_of(feature_maps), rows_of(cotangent)
    code_shape = jax.ShapeDtypeStruct((8, places * samples), jnp.int32)
    *packs, code_row = call(
        functools.partial(first_pack_kernel, sizes=sizes),
        [packed for _ in others] + [code_shape],
        [SMEM, SMEM, VMEM],
        megabytes=56,
    )(path, at, maps)
    got_maps = swap(packs, 1)
    packs = call(
        functools.partial(second_pack_kernel, sizes=sizes),
        [packed for _ in others],
        [VMEM, SMEM, VMEM],
    )(code_row, at, grads)
    got_grads = swap(packs, 1)

    slot_shape = shape(places * slots, channels)
    slot_half = shape(places * slots, channels, dtype=BF16)
    tap_shape = shape(25, 1, channels)
    own_maps, own_grads, kernel, place, fetch, home, merge = call(
        functools.partial(prepare_kernel, sizes=sizes),
        [
            slot_half,
            slot_half,
            tap_shape,
            shape(sections - 1, places * slots, places * capacity, dtype=BF16),
            shape(sections - 1, places * capacity, places * slots, dtype=BF16),
            shape(places * samples, places * slots, dtype=BF16),
            shape(sections - 1, places * samples, places * capacity, dtype=BF16),
        ],
        [SMEM, SMEM, VMEM, VMEM, VMEM, VMEM],
    )(path, at, code_row, maps, grads, kernel)
    block = channels // ways
    turned = shape(ways // 2, block, places * capacity, dtype=BF16)
    results = call(
        functools.partial(forward_kernel, sizes=sizes, side=side),
        [packed for _ in others]
        + [turned for _ in others] * 2
        + [slot_half, slot_half, slot_shape, shape(places * slots, LANES), slot_shape],
        [SMEM] + [VMEM] * (5 + len(got_maps)),
        [pltpu.VMEM((channels, places * capacity), BF16)],
    )(replica, own_maps, place, fetch, weight, kernel, *got_maps)
    count = sections - 1
    back, active_give, active_hold = [results[i * count : (i + 1) * count] for i in range(3)]
    slot_final, active, scaled, inverse, source = results[3 * count :]

    part = shape(ways // 2, block, channels)
    own_give, own_hold = call(
        own_point_kernel, [part, part], [SMEM, VMEM, VMEM], [pltpu.VMEM((channels, channels), F32)]
    )(replica, active, own_grads)
    got_final = swap(back, -1)

    send = call(
        point_kernel, shape(ways // 2, block, channels, dtype=BF16), [VMEM] * (1 + 2 * count)
    )(own_give, *active_give, *got_grads)
    got = trade(send, (1, 1))
    keep = call(point_kernel, part, [VMEM] * (1 + 2 * count))(own_hold, *active_hold, *got_grads)

    slot_grads, mixed = call(
        functools.partial(mixed_kernel, block=side * slots),
        [slot_half, slot_shape],
        [VMEM] * (5 + len(got_grads)),
        [pltpu.VMEM((places * slots, channels), F32)],
    )(own_grads, place, weight, scaled, inverse, *got_grads)
    *back, slot_in = call(
        functools.partial(backward_kernel, side=side, slots=slots),
        [packed for _ in others] + [slot_half],
        [VMEM] * 4,
        [pltpu.VMEM((places * slots, channels), F32)],
    )(slot_grads, fetch, kernel, mixed)
    got_in = swap(back, -1)

    half_shape = shape(25, 1, channels // 2)

    def tap_sums(flip):
        return call(
            functools.partial(taps_kernel, side=side, slots=slots, flip=flip),
            half_shape,
            [SMEM, SMEM, VMEM, VMEM],
        )(at, replica, mixed, source)

    give, taps = tap_sums(1), tap_sums(0)

    bits = [1 << i for i in range(1, ways.bit_length() - 1)]
    swapped = bits[1::-1] + bits[2:] if len(bits) > 2 else bits
    for step, pair in enumerate(zip(bits, swapped)):
        count = (ways // 4) >> step
        strides = []
        for order in (bits, swapped):
            done = order[:step]
            strides.append(1 << sum(1 for other in bits if other < order[step] and other not in done))
        send, keep = call(
            functools.partial(fold_kernel, strides=strides, bits=pair),
            [shape(count, block, channels, dtype=BF16), shape(count, block, channels)],
            [SMEM, VMEM, VMEM],
        )(replica, keep, got)
        got = trade(send, pair)

    later = bits[:-1]
    pairs = [(1, 1), (bits[-1], bits[-1])] + list(zip(later, later[1:] + later[:1]))
    for step, pair in enumerate(pairs):
        came = trade(give if step == 0 else taps, pair)
        taps = taps + came
    came = trade(taps, (1, 1))
    point_grad, taps = call(
        last_kernel, [shape(block, channels), tap_shape], [SMEM] + [VMEM] * 4
    )(replica, keep, got, taps, came)

    final_maps = maps_of(unpack(slot_final, got_final))
    input_grad = maps_of(unpack(slot_in, got_in))
    return (
        final_maps,
        input_grad,
        point_grad.reshape(1, 1, block, channels),
        taps.reshape(1, 1, 25, channels),
    )


def solution(mesh):
    placed = (
        P(("segment", "rep"), None, None, None),
        P(None, ("segment", "rep"), None),
        P(None, "segment", None, None),
        P(None, "segment", None, None),
        P(("segment", "rep"), None, None, None),
    )
    return jax.shard_map(
        window,
        mesh=mesh,
        in_specs=placed,
        out_specs=(
            P(("segment", "rep"), None, None, None),
            P(("segment", "rep"), None, None, None),
            P(None, "segment", "rep", None),
            P(None, "segment", None, None),
        ),
        check_vma=False,
    )
```

time: 63.8 us -> 62.9 us (0.986)
  waiting for transfers between devices: 20.2 us -> 16.7 us
  local copies, waits for them, and re-layouts: 2.95 us -> 5.27 us
  starting transfers between devices: 14.3 us -> 15.1 us
    ppermute x4, waiting for transfers between devices: 10.1 us -> 3.37 us  [swap(): lax.ppermute(piece, 'segment', [(i, (i + direction * shift) % sections) f...]
    ppermute x10 -> x9, waiting for transfers between devices: 10.1 us -> 13.3 us  [trade(): lax.ppermute(value, 'rep', [(i, i ^ pair[i & 1]) for i in range(ways)])]
    unnamed x14 -> x16, local copies, waits for them, and re-layouts: 2.95 us -> 5.27 us
    pallas_call x11 -> x15, Pallas kernels: 18.7 us -> 17.5 us  [the longest x2 3.36 us: unpack(): call(unpack_kernel, shape(places * samples, channels, dtype=BF16), [VMEM]...]
    ppermute x10 -> x9, starting transfers between devices: 9.09 us -> 10.1 us  [trade(): lax.ppermute(value, 'rep', [(i, i ^ pair[i & 1]) for i in range(ways)])]
  transfers between devices with their start and end apart: 14 -> 13, of which waited for: 7 -> 7; matrix products, arithmetic and copies ran while one was open for 1% -> 0% of each run, Pallas kernels for 31% -> 33%
where the time goes in v4:
time: 62.9 us; the launch traced here: 62.5 us
  Pallas kernels  24.4 us (39%)
  waiting for transfers between devices  16.7 us (27%)
  starting transfers between devices  15.1 us (24%)
  local copies, waits for them, and re-layouts  5.27 us (8%)
  between operations  0.8 us (1%)
    ppermute x9, waiting for transfers between devices, trade(): lax.ppermute(value, 'rep', [(i, i ^ pair[i & 1]) for i in range(ways)])  13.3 us
    ppermute x9, starting transfers between devices, trade(): lax.ppermute(value, 'rep', [(i, i ^ pair[i & 1]) for i in range(ways)])  10.1 us
    unnamed x16, local copies, waits for them, and re-layouts  5.27 us
    ppermute x4, starting transfers between devices, swap(): lax.ppermute(piece, 'segment', [(i, (i + direction * shift) % sections) f...  5.05 us
    pallas_call x1, Pallas kernels, window(): call(functools.partial(forward_kernel, sizes=sizes, side=side), [packed f...  5 us
    ppermute x4, waiting for transfers between devices, swap(): lax.ppermute(piece, 'segment', [(i, (i + direction * shift) % sections) f...  3.37 us
    pallas_call x2, Pallas kernels, unpack(): call(unpack_kernel, shape(places * samples, channels, dtype=BF16), [VMEM]...  3.36 us
    pallas_call x2, Pallas kernels, tap_sums(): call(functools.partial(taps_kernel, side=side, slots=slots, flip=flip), h...  2.86 us
  transfers between devices with their start and end apart: 13, of which 7 were waited for; matrix products, arithmetic and copies ran while one was open for 0% of the time, Pallas kernels for 33%

profile of v4, /device:TPU:0, one launch (start us, length us, event | category | flops | bytes accessed | tf_op | source)
XLA Modules:
  0.0 62.5 jit_solution(17032576833462695371)
XLA Ops:
  0.7 2.5 %shard_map.84 = (bf16[196,1024]{1,0:T(8,128)(2,1)}, s32[8,392]{1,0:T(8,128)}) custom-call(s32[8]{0:T(128)} %bitcast.28, s32[1]{0:T(128)} %bitcast.1.at_ref, bf16[392,1024]{1,0:T(8,128)(2,1)} %bitcast.23), custom_call_target="tpu_custom_call" | custom-call | tf_op jit(solution)/shard_map/pallas_call | solution.py:394
  3.1 3.0 %collective-permute-start = (bf16[196,1024]{1,0:T(8,128)(2,1)}, bf16[196,1024]{1,0:T(8,128)(2,1)}, u32[]{:S(2)}, u32[]{:S(2)}) collective-permute-start(bf16[196,1024]{1,0:T(8,128)(2,1)} %get-tuple-element.42), channel_id=1, source_target_pairs={{0,16},{16,0},{1,17},{17,1},{2,18},{18,2},{3,19},{19,3},{4,20},{20... | collective-permute-start | bytes 1204232 | tf_op jit(solution)/shard_map/ppermute | solution.py:376
  6.1 1.1 %copy-done.2 = bf16[8,7,7,1024]{3,0,2,1:T(8,128)(2,1)S(1)} copy-done((bf16[8,7,7,1024]{3,0,2,1:T(8,128)(2,1)S(1)}, bf16[8,7,7,1024]{3,0,2,1:T(8,128)(2,1)}, u32[]{:S(2)}) %copy-start.2) | copy-done | bytes 802840
  7.2 0.7 %copy-done.5 = s32[8,392]{1,0:T(8,128)S(1)} copy-done((s32[8,392]{1,0:T(8,128)S(1)}, s32[8,392]{1,0:T(8,128)}, u32[]{:S(2)}) %copy-start.5) | copy-done | bytes 12568
  7.9 1.2 %shard_map.88 = bf16[196,1024]{1,0:T(8,128)(2,1)} custom-call(s32[8,392]{1,0:T(8,128)S(1)} %copy-done.5, s32[1]{0:T(128)} %bitcast.1.at_ref, bf16[392,1024]{1,0:T(8,128)(2,1)S(1)} %bitcast.25), custom_call_target="tpu_custom_call" | custom-call | tf_op jit(solution)/shard_map/pallas_call | solution.py:401
  9.1 0.0 collective-permute-start.2
  9.1 1.1 %copy-done.3 = bf16[8,7,7,1024]{3,0,2,1:T(8,128)(2,1)S(1)} copy-done((bf16[8,7,7,1024]{3,0,2,1:T(8,128)(2,1)S(1)}, bf16[8,7,7,1024]{3,0,2,1:T(8,128)(2,1)}, u32[]{:S(2)}) %copy-start.3) | copy-done | bytes 802840
  10.2 0.9 %copy-done.4 = f32[1,1,25,1024]{3,1,2,0:T(1,128)S(1)} copy-done((f32[1,1,25,1024]{3,1,2,0:T(1,128)S(1)}, f32[1,1,25,1024]{3,1,2,0:T(1,128)}, u32[]{:S(2)}) %copy-start.4) | copy-done | bytes 102424
  11.1 0.7 %copy-done.6 = s32[8,392]{1,0:T(8,128)S(1)} copy-done((s32[8,392]{1,0:T(8,128)S(1)}, s32[8,392]{1,0:T(8,128)}, u32[]{:S(2)}) %copy-start.6) | copy-done | bytes 12568
  11.9 0.7 %copy-done.7 = s32[1,8,1]{1,2,0:T(1,128)S(1)} copy-done((s32[1,8,1]{1,2,0:T(1,128)S(1)}, s32[1,8,1]{1,2,0:T(1,128)}, u32[]{:S(2)}) %copy-start.7) | copy-done | bytes 56
  12.5 1.9 %shard_map.85 = (bf16[392,1024]{1,0:T(8,128)(2,1)S(1)}, bf16[392,1024]{1,0:T(8,128)(2,1)S(1)}, f32[25,1,1024]{2,1,0:T(1,128)S(1)}, bf16[1,392,196]{2,1,0:T(8,128...) custom-call(s32[8]{0:T(128)S(1)} %bitcast.29, ...), custom_call_target="tpu_custom_call" | custom-call | tf_op jit(solution)/shard_map/pallas_call | solution.py:411
  14.4 2.3 %collective-permute-done.refs_0_ = bf16[196,1024]{1,0:T(8,128)(2,1)} collective-permute-done((bf16[196,1024]{1,0:T(8,128)(2,1)}, bf16[196,1024]{1,0:T(8,128)(2,1)}, u32[]{:S(2)}, u32[]{:S(2)}) %collective-permute-start) | collective-permute-done | bytes 401440 | tf_op jit(solution)/shard_map/ppermute | solution.py:376
  16.7 5.0 %shard_map.86 = (bf16[196,1024]{1,0:T(8,128)(2,1)S(1)}, bf16[8,64,196]{2,1,0:T(8,128)(2,1)S(1)}, bf16[8,64,196]{2,1,0:T(8,128)(2,1)S(1)}, bf16[392,1024]{1,0:T(8...) custom-call(s32[1]{0:T(128)} %bitcast.7.replica_ref, ...), custom_call_target="tpu_custom_call" | custom-call | tf_op jit(solution)/shard_map/pallas_call | solution.py:426
  21.7 1.7 %shard_map.92 = (f32[8,64,1024]{2,1,0:T(8,128)S(1)}, f32[8,64,1024]{2,1,0:T(8,128)S(1)}) custom-call(s32[1]{0:T(128)} %bitcast.7.replica_ref, bf16[392,1024]{1,0:T(8,128)(2,1)S(1)} %get-tuple-element.52.active_ref, bf16[392,1024]{1,0:T(8,128)(2,1)S(1)} %get-tuple-element.45.own_ref), custom_call_target="tpu_custom_call" | custom-call | tf_op jit(solution)/shard_map/pallas_call | solution.py:439
  23.5 1.1 %collective-permute-done.2.refs_0_.refs_1_ = bf16[196,1024]{1,0:T(8,128)(2,1)S(1)} collective-permute-done((bf16[196,1024]{1,0:T(8,128)(2,1)}, bf16[196,1024]{1,0:T(8,128)(2,1)S(1)}, u32[]{:S(2)}, u32[]{:S(2)}) %collective-permute-start.2) | collective-permute-done | bytes 401440 | tf_op jit(solution)/shard_map/ppermute | solution.py:376
  24.5 0.4 shard_map.94
  25.0 0.1 collective-permute-start.4
  25.0 0.4 shard_map.93.keep_ref
  25.5 2.2 %collective-permute-done.4.got_ref = bf16[8,64,1024]{2,1,0:T(8,128)(2,1)S(1)} collective-permute-done((bf16[8,64,1024]{2,1,0:T(8,128)(2,1)S(1)}, bf16[8,64,1024]{2,1,0:T(8,128)(2,1)S(1)}, u32[]{:S(2)}, u32[]{:S(2)}) %collective-permute-start.4) | collective-permute-done | bytes 1048608 | tf_op jit(solution)/shard_map/ppermute | solution.py:390
  27.7 0.2 shard_map.95
  27.9 1.8 %collective-permute-start.5 = (bf16[4,64,1024]{2,1,0:T(8,128)(2,1)S(1)}, bf16[4,64,1024]{2,1,0:T(8,128)(2,1)S(1)}, u32[]{:S(2)}, u32[]{:S(2)}) collective-permute-start(bf16[4,64,1024]{2,1,0:T(8,128)(2,1)S(1)} %get-tuple-element.58), channel_id=1, source_target_pairs={{0,2},{1,5},{2,0},{3,7},{4,6},{5,1},{6,4},{7,3},{8,10},{9,13},{10,... | collective-permute-start | bytes 1572872 | tf_op jit(solution)/shard_map/ppermute | solution.py:390
  29.7 1.5 %collective-permute-start.1 = (bf16[196,1024]{1,0:T(8,128)(2,1)S(1)}, bf16[196,1024]{1,0:T(8,128)(2,1)S(1)}, u32[]{:S(2)}, u32[]{:S(2)}) collective-permute-start(bf16[196,1024]{1,0:T(8,128)(2,1)S(1)} %get-tuple-element.44), channel_id=1, source_target_pairs={{0,16},{16,0},{1,17},{17,1},{2,18},{18,2},{3,19},{19,3},{4,20},{20... | collective-permute-start | bytes 1204232 | tf_op jit(solution)/shard_map/ppermute | solution.py:376
  31.2 1.5 %shard_map.89 = (bf16[392,1024]{1,0:T(8,128)(2,1)S(1)}, f32[392,1024]{1,0:T(8,128)S(1)}) custom-call(bf16[392,1024]{1,0:T(8,128)(2,1)S(1)} %get-tuple-element.45.own_ref, bf16[1,392,196]{2,1,0:T(8,128)(2,1)S(1)} %get-tuple-element.39.place_ref, bf16[1024,1024]{1,0:T(8,128)(2,1)S(1)} %bitcast.22, f32[392,1024]{1,0:T(8,128)S(1)} %get-tuple-element.46.scaled_ref, ...), custom_call_target="tpu_custom_call" | custom-call | tf_op jit(solution)/shard_map/pallas_call | solution.py:450
  32.7 2.4 %shard_map.90 = (bf16[196,1024]{1,0:T(8,128)(2,1)S(1)}, bf16[392,1024]{1,0:T(8,128)(2,1)S(1)}) custom-call(bf16[392,1024]{1,0:T(8,128)(2,1)S(1)} %get-tuple-element.48.slot_grads_ref, bf16[1,196,392]{2,1,0:T(8,128)(2,1)S(1)} %get-tuple-element.40.fetch_ref, f32[25,1,1024]{2,1,0:T(1,128)S(1)} %get-tuple-element.41.kernel_ref, ...), custom_call_target="tpu_custom_call" | custom-call | tf_op jit(solution)/shard_map/pallas_call | solution.py:456
  35.2 0.6 collective-permute-start.3
  35.8 1.3 %collective-permute-done.5.got_ref = bf16[4,64,1024]{2,1,0:T(8,128)(2,1)S(1)} collective-permute-done((bf16[4,64,1024]{2,1,0:T(8,128)(2,1)S(1)}, bf16[4,64,1024]{2,1,0:T(8,128)(2,1)S(1)}, u32[]{:S(2)}, u32[]{:S(2)}) %collective-permute-start.5) | collective-permute-done | bytes 524320 | tf_op jit(solution)/shard_map/ppermute | solution.py:390
  37.1 0.1 shard_map.96
  37.2 1.9 %collective-permute-start.6 = (bf16[2,64,1024]{2,1,0:T(8,128)(2,1)S(1)}, bf16[2,64,1024]{2,1,0:T(8,128)(2,1)S(1)}, u32[]{:S(2)}, u32[]{:S(2)}) collective-permute-start(bf16[2,64,1024]{2,1,0:T(8,128)(2,1)S(1)} %get-tuple-element.60), channel_id=1, source_target_pairs={{0,4},{1,3},{2,6},{3,1},{4,0},{5,7},{6,2},{7,5},{8,12},{9,11},{10,... | collective-permute-start | bytes 786440 | tf_op jit(solution)/shard_map/ppermute | solution.py:390
  39.1 1.4 %shard_map.99 = f32[25,1,512]{2,1,0:T(1,128)S(1)} custom-call(s32[1]{0:T(128)} %bitcast.1.at_ref, s32[1]{0:T(128)} %bitcast.7.replica_ref, f32[392,1024]{1,0:T(8,128)S(1)} %get-tuple-element.49.mixed_ref, f32[392,1024]{1,0:T(8,128)S(1)} %get-tuple-element.63.source_ref), custom_call_target="tpu_custom_call" | custom-call | tf_op jit(solution)/shard_map/pallas_call | solution.py:467
  40.5 0.1 collective-permute-start.8
  40.6 1.4 %shard_map.98 = f32[25,1,512]{2,1,0:T(1,128)S(1)} custom-call(s32[1]{0:T(128)} %bitcast.1.at_ref, s32[1]{0:T(128)} %bitcast.7.replica_ref, f32[392,1024]{1,0:T(8,128)S(1)} %get-tuple-element.49.mixed_ref, f32[392,1024]{1,0:T(8,128)S(1)} %get-tuple-element.63.source_ref), custom_call_target="tpu_custom_call" | custom-call | tf_op jit(solution)/shard_map/pallas_call | solution.py:467
  42.1 0.1 add.12
  42.1 2.7 %collective-permute-start.9 = (f32[25,1,512]{2,1,0:T(1,128)S(1)}, f32[25,1,512]{2,1,0:T(1,128)S(1)}, u32[]{:S(2)}, u32[]{:S(2)}) collective-permute-start(f32[25,1,512]{2,1,0:T(1,128)S(1)} %add.12), channel_id=1, source_target_pairs={{0,8},{1,9},{2,10},{3,11},{4,12},{5,13},{6,14},{7,15},{8,0},{9,1},... | collective-permute-start | bytes 153608 | tf_op jit(solution)/shard_map/ppermute | solution.py:390
  44.8 3.4 %collective-permute-done.9 = f32[25,1,512]{2,1,0:T(1,128)S(1)} collective-permute-done((f32[25,1,512]{2,1,0:T(1,128)S(1)}, f32[25,1,512]{2,1,0:T(1,128)S(1)}, u32[]{:S(2)}, u32[]{:S(2)}) %collective-permute-start.9) | collective-permute-done | bytes 51232 | tf_op jit(solution)/shard_map/ppermute | solution.py:390
  48.2 0.1 add.13
  48.3 1.6 %collective-permute-start.10 = (f32[25,1,512]{2,1,0:T(1,128)S(1)}, f32[25,1,512]{2,1,0:T(1,128)S(1)}, u32[]{:S(2)}, u32[]{:S(2)}) collective-permute-start(f32[25,1,512]{2,1,0:T(1,128)S(1)} %add.13), channel_id=1, source_target_pairs={{0,2},{1,5},{2,0},{3,7},{4,6},{5,1},{6,4},{7,3},{8,10},{9,13},{10,... | collective-permute-start | bytes 153608 | tf_op jit(solution)/shard_map/ppermute | solution.py:390
  49.9 0.0 collective-permute-done.6.got_ref
  49.9 1.8 %collective-permute-start.7 = (bf16[1,64,1024]{2,1,0:T(8,128)(2,1)S(1)}, bf16[1,64,1024]{2,1,0:T(8,128)(2,1)S(1)}, u32[]{:S(2)}, u32[]{:S(2)}) collective-permute-start(bf16[1,64,1024]{2,1,0:T(8,128)(2,1)S(1)} %get-tuple-element.62), channel_id=1, source_target_pairs={{0,8},{1,9},{2,10},{3,11},{4,12},{5,13},{6,14},{7,15},{8,0},{9,1},... | collective-permute-start | bytes 393224 | tf_op jit(solution)/shard_map/ppermute | solution.py:390
  51.7 0.7 %collective-permute-done.10 = f32[25,1,512]{2,1,0:T(1,128)S(1)} collective-permute-done((f32[25,1,512]{2,1,0:T(1,128)S(1)}, f32[25,1,512]{2,1,0:T(1,128)S(1)}, u32[]{:S(2)}, u32[]{:S(2)}) %collective-permute-start.10) | collective-permute-done | bytes 51232 | tf_op jit(solution)/shard_map/ppermute | solution.py:390
  52.4 0.1 add.14
  52.5 0.1 collective-permute-start.11
  52.6 5.6 %collective-permute-done.11 = f32[25,1,512]{2,1,0:T(1,128)S(1)} collective-permute-done((f32[25,1,512]{2,1,0:T(1,128)S(1)}, f32[25,1,512]{2,1,0:T(1,128)S(1)}, u32[]{:S(2)}, u32[]{:S(2)}) %collective-permute-start.11) | collective-permute-done | bytes 51232 | tf_op jit(solution)/shard_map/ppermute | solution.py:390
  58.2 0.1 add.15.taps_ref
  58.3 0.1 collective-permute-start.12
  58.4 1.7 %shard_map.87 = bf16[392,1024]{1,0:T(8,128)(2,1)} custom-call(bf16[392,392]{1,0:T(8,128)(2,1)S(1)} %get-tuple-element.36.home_ref, bf16[1,392,196]{2,1,0:T(8,128)(2,1)S(1)} %get-tuple-element.37.merge_ref, bf16[392,1024]{1,0:T(8,128)(2,1)S(1)} %get-tuple-element.43.slots_ref, bf16[196,1024]{1,0:T(8,128)(2,1)S(1)} %collective-permute-done.1.refs_0_), custom_call_target="tpu_custom_call" | custom-call | tf_op jit(solution)/shard_map/pallas_call | solution.py:385
  60.1 0.0 collective-permute-done.3.refs_0_
  60.1 1.7 %shard_map.91 = bf16[392,1024]{1,0:T(8,128)(2,1)} custom-call(bf16[392,392]{1,0:T(8,128)(2,1)S(1)} %get-tuple-element.36.home_ref, bf16[1,392,196]{2,1,0:T(8,128)(2,1)S(1)} %get-tuple-element.37.merge_ref, bf16[392,1024]{1,0:T(8,128)(2,1)S(1)} %get-tuple-element.50.slots_ref, bf16[196,1024]{1,0:T(8,128)(2,1)S(1)} %collective-permute-done.3.refs_0_), custom_call_target="tpu_custom_call" | custom-call | tf_op jit(solution)/shard_map/pallas_call | solution.py:385
  61.7 0.8 %shard_map.100 = (f32[64,1024]{1,0:T(8,128)}, f32[25,1,1024]{2,1,0:T(1,128)}) custom-call(s32[1]{0:T(128)} %bitcast.7.replica_ref, f32[1,64,1024]{2,1,0:T(8,128)S(1)} %get-tuple-element.61.keep_ref, bf16[1,64,1024]{2,1,0:T(8,128)(2,1)S(1)} %collective-permute-done.7.got_ref, f32[25,1,512]{2,1,0:T(1,128)S(1)} %add.15.taps_ref, ...), custom_call_target="tpu_custom_call" | custom-call | tf_op jit(solution)/shard_map/pallas_call | solution.py:496
  (15 shorter events, 0.1 us)
Async XLA Ops:
  0.6 8.5 %copy-start.1 = (bf16[8,7,7,1024]{3,0,2,1:T(8,128)(2,1)S(1)}, bf16[8,7,7,1024]{3,0,2,1:T(8,128)(2,1)}, u32[]{:S(2)}) copy-start(bf16[8,7,7,1024]{3,0,2,1:T(8,128)(2,1)} %param.5) | copy-start | bytes 2408452
  0.6 16.1 %copy-start = (bf16[1,1,1024,1024]{3,2,1,0:T(8,128)(2,1)S(1)}, bf16[1,1,1024,1024]{3,2,1,0:T(8,128)(2,1)}, u32[]{:S(2)}) copy-start(bf16[1,1,1024,1024]{3,2,1,0:T(8,128)(2,1)} %param.7) | copy-start | bytes 6291460
  3.1 13.6 %collective-permute-start = (bf16[196,1024]{1,0:T(8,128)(2,1)}, bf16[196,1024]{1,0:T(8,128)(2,1)}, u32[]{:S(2)}, u32[]{:S(2)}) collective-permute-start(bf16[196,1024]{1,0:T(8,128)(2,1)} %get-tuple-element.42), channel_id=1, source_target_pairs={{0,16},{16,0},{1,17},{17,1},{2,18},{18,2},{3,19},{19,3},{4,20},{20... | collective-permute-start | bytes 1204232 | tf_op jit(solution)/shard_map/ppermute | solution.py:376
  6.1 1.1 %copy-start.2 = (bf16[8,7,7,1024]{3,0,2,1:T(8,128)(2,1)S(1)}, bf16[8,7,7,1024]{3,0,2,1:T(8,128)(2,1)}, u32[]{:S(2)}) copy-start(bf16[8,7,7,1024]{3,0,2,1:T(8,128)(2,1)} %param.9) | copy-start | bytes 2408452
  7.2 0.7 %copy-start.5 = (s32[8,392]{1,0:T(8,128)S(1)}, s32[8,392]{1,0:T(8,128)}, u32[]{:S(2)}) copy-start(s32[8,392]{1,0:T(8,128)} %get-tuple-element.35.code_ref) | copy-start | bytes 37636
  9.1 15.4 %collective-permute-start.2 = (bf16[196,1024]{1,0:T(8,128)(2,1)}, bf16[196,1024]{1,0:T(8,128)(2,1)S(1)}, u32[]{:S(2)}, u32[]{:S(2)}) collective-permute-start(bf16[196,1024]{1,0:T(8,128)(2,1)} %shard_map.88), channel_id=1, source_target_pairs={{0,16},{16,0},{1,17},{17,1},{2,18},{18,2},{3,19},{19,3},{4,20},{20... | collective-permute-start | bytes 1204232 | tf_op jit(solution)/shard_map/ppermute | solution.py:376
  9.1 1.1 %copy-start.3 = (bf16[8,7,7,1024]{3,0,2,1:T(8,128)(2,1)S(1)}, bf16[8,7,7,1024]{3,0,2,1:T(8,128)(2,1)}, u32[]{:S(2)}) copy-start(bf16[8,7,7,1024]{3,0,2,1:T(8,128)(2,1)} %param.9) | copy-start | bytes 2408452
  10.2 0.9 %copy-start.4 = (f32[1,1,25,1024]{3,1,2,0:T(1,128)S(1)}, f32[1,1,25,1024]{3,1,2,0:T(1,128)}, u32[]{:S(2)}) copy-start(f32[1,1,25,1024]{3,1,2,0:T(1,128)} %param.8) | copy-start | bytes 307204
  11.1 0.7 %copy-start.6 = (s32[8,392]{1,0:T(8,128)S(1)}, s32[8,392]{1,0:T(8,128)}, u32[]{:S(2)}) copy-start(s32[8,392]{1,0:T(8,128)} %get-tuple-element.35.code_ref) | copy-start | bytes 37636
  11.9 0.7 %copy-start.7 = (s32[1,8,1]{1,2,0:T(1,128)S(1)}, s32[1,8,1]{1,2,0:T(1,128)}, u32[]{:S(2)}) copy-start(s32[1,8,1]{1,2,0:T(1,128)} %param.6) | copy-start | bytes 100
  25.0 2.7 %collective-permute-start.4 = (bf16[8,64,1024]{2,1,0:T(8,128)(2,1)S(1)}, bf16[8,64,1024]{2,1,0:T(8,128)(2,1)S(1)}, u32[]{:S(2)}, u32[]{:S(2)}) collective-permute-start(bf16[8,64,1024]{2,1,0:T(8,128)(2,1)S(1)} %shard_map.94), channel_id=1, source_target_pairs={{0,1},{1,0},{2,3},{3,2},{4,5},{5,4},{6,7},{7,6},{8,9},{9,8},{10,11... | collective-permute-start | bytes 3145736 | tf_op jit(solution)/shard_map/ppermute | solution.py:390
  27.9 9.2 %collective-permute-start.5 = (bf16[4,64,1024]{2,1,0:T(8,128)(2,1)S(1)}, bf16[4,64,1024]{2,1,0:T(8,128)(2,1)S(1)}, u32[]{:S(2)}, u32[]{:S(2)}) collective-permute-start(bf16[4,64,1024]{2,1,0:T(8,128)(2,1)S(1)} %get-tuple-element.58), channel_id=1, source_target_pairs={{0,2},{1,5},{2,0},{3,7},{4,6},{5,1},{6,4},{7,3},{8,10},{9,13},{10,... | collective-permute-start | bytes 1572872 | tf_op jit(solution)/shard_map/ppermute | solution.py:390
  29.7 28.7 %collective-permute-start.1 = (bf16[196,1024]{1,0:T(8,128)(2,1)S(1)}, bf16[196,1024]{1,0:T(8,128)(2,1)S(1)}, u32[]{:S(2)}, u32[]{:S(2)}) collective-permute-start(bf16[196,1024]{1,0:T(8,128)(2,1)S(1)} %get-tuple-element.44), channel_id=1, source_target_pairs={{0,16},{16,0},{1,17},{17,1},{2,18},{18,2},{3,19},{19,3},{4,20},{20... | collective-permute-start | bytes 1204232 | tf_op jit(solution)/shard_map/ppermute | solution.py:376
  35.2 24.9 %collective-permute-start.3 = (bf16[196,1024]{1,0:T(8,128)(2,1)S(1)}, bf16[196,1024]{1,0:T(8,128)(2,1)S(1)}, u32[]{:S(2)}, u32[]{:S(2)}) collective-permute-start(bf16[196,1024]{1,0:T(8,128)(2,1)S(1)} %get-tuple-element.51), channel_id=1, source_target_pairs={{0,16},{16,0},{1,17},{17,1},{2,18},{18,2},{3,19},{19,3},{4,20},{20... | collective-permute-start | bytes 1204232 | tf_op jit(solution)/shard_map/ppermute | solution.py:376
  37.2 12.7 %collective-permute-start.6 = (bf16[2,64,1024]{2,1,0:T(8,128)(2,1)S(1)}, bf16[2,64,1024]{2,1,0:T(8,128)(2,1)S(1)}, u32[]{:S(2)}, u32[]{:S(2)}) collective-permute-start(bf16[2,64,1024]{2,1,0:T(8,128)(2,1)S(1)} %get-tuple-element.60), channel_id=1, source_target_pairs={{0,4},{1,3},{2,6},{3,1},{4,0},{5,7},{6,2},{7,5},{8,12},{9,11},{10,... | collective-permute-start | bytes 786440 | tf_op jit(solution)/shard_map/ppermute | solution.py:390
  40.5 1.5 %collective-permute-start.8 = (f32[25,1,512]{2,1,0:T(1,128)S(1)}, f32[25,1,512]{2,1,0:T(1,128)S(1)}, u32[]{:S(2)}, u32[]{:S(2)}) collective-permute-start(f32[25,1,512]{2,1,0:T(1,128)S(1)} %shard_map.99), channel_id=1, source_target_pairs={{0,1},{1,0},{2,3},{3,2},{4,5},{5,4},{6,7},{7,6},{8,9},{9,8},{10,11... | collective-permute-start | bytes 153608 | tf_op jit(solution)/shard_map/ppermute | solution.py:390
  42.1 6.1 %collective-permute-start.9 = (f32[25,1,512]{2,1,0:T(1,128)S(1)}, f32[25,1,512]{2,1,0:T(1,128)S(1)}, u32[]{:S(2)}, u32[]{:S(2)}) collective-permute-start(f32[25,1,512]{2,1,0:T(1,128)S(1)} %add.12), channel_id=1, source_target_pairs={{0,8},{1,9},{2,10},{3,11},{4,12},{5,13},{6,14},{7,15},{8,0},{9,1},... | collective-permute-start | bytes 153608 | tf_op jit(solution)/shard_map/ppermute | solution.py:390
  48.3 4.2 %collective-permute-start.10 = (f32[25,1,512]{2,1,0:T(1,128)S(1)}, f32[25,1,512]{2,1,0:T(1,128)S(1)}, u32[]{:S(2)}, u32[]{:S(2)}) collective-permute-start(f32[25,1,512]{2,1,0:T(1,128)S(1)} %add.13), channel_id=1, source_target_pairs={{0,2},{1,5},{2,0},{3,7},{4,6},{5,1},{6,4},{7,3},{8,10},{9,13},{10,... | collective-permute-start | bytes 153608 | tf_op jit(solution)/shard_map/ppermute | solution.py:390
  49.9 11.8 %collective-permute-start.7 = (bf16[1,64,1024]{2,1,0:T(8,128)(2,1)S(1)}, bf16[1,64,1024]{2,1,0:T(8,128)(2,1)S(1)}, u32[]{:S(2)}, u32[]{:S(2)}) collective-permute-start(bf16[1,64,1024]{2,1,0:T(8,128)(2,1)S(1)} %get-tuple-element.62), channel_id=1, source_target_pairs={{0,8},{1,9},{2,10},{3,11},{4,12},{5,13},{6,14},{7,15},{8,0},{9,1},... | collective-permute-start | bytes 393224 | tf_op jit(solution)/shard_map/ppermute | solution.py:390
  52.5 5.7 %collective-permute-start.11 = (f32[25,1,512]{2,1,0:T(1,128)S(1)}, f32[25,1,512]{2,1,0:T(1,128)S(1)}, u32[]{:S(2)}, u32[]{:S(2)}) collective-permute-start(f32[25,1,512]{2,1,0:T(1,128)S(1)} %add.14), channel_id=1, source_target_pairs={{0,4},{1,3},{2,6},{3,1},{4,0},{5,7},{6,2},{7,5},{8,12},{9,11},{10,... | collective-permute-start | bytes 153608 | tf_op jit(solution)/shard_map/ppermute | solution.py:390
  58.3 3.5 %collective-permute-start.12 = (f32[25,1,512]{2,1,0:T(1,128)S(1)}, f32[25,1,512]{2,1,0:T(1,128)S(1)}, u32[]{:S(2)}, u32[]{:S(2)}) collective-permute-start(f32[25,1,512]{2,1,0:T(1,128)S(1)} %add.15.taps_ref), channel_id=1, source_target_pairs={{0,1},{1,0},{2,3},{3,2},{4,5},{5,4},{6,7},{7,6},{8,9},{9,8},{10,11... | collective-permute-start | bytes 153608 | tf_op jit(solution)/shard_map/ppermute | solution.py:390

commit v5 on v4

--- a/solution.py
+++ b/solution.py
@@ -320,11 +320,14 @@
                 source = cells(source_ref, row + row_shift)
                 for col_shift in range(-2, 3):
                     tap = (row_shift + 2) * 5 + col_shift + 2
-                    for col in range(side):
-                        if not 0 <= col + col_shift < side:
-                            continue
-                        term = grads[col] * source[col + col_shift]
-                        sums[tap] = term if sums[tap] is None else sums[tap] + term
+                    terms = [
+                        grads[col] * source[col + col_shift]
+                        for col in range(side)
+                        if 0 <= col + col_shift < side
+                    ]
+                    while len(terms) > 1:
+                        terms = [sum(terms[i + 1 : i + 2], terms[i]) for i in range(0, len(terms), 2)]
+                    sums[tap] = terms[0] if sums[tap] is None else sums[tap] + terms[0]
         for tap in range(25):
             out_ref[tap, :, target] = (
                 jnp.sum(sums[tap], axis=0, keepdims=True) * tap_keep(kind, tap)

time: 62.9 us -> 62.5 us (level)
  no operation moved by 1% of the time
where the time goes in v5:
time: 62.5 us; the launch traced here: 62.1 us
  Pallas kernels  24.1 us (39%)
  waiting for transfers between devices  16.7 us (27%)
  starting transfers between devices  15 us (24%)
  local copies, waits for them, and re-layouts  5.27 us (8%)
  between operations  0.8 us (1%)
    ppermute x9, waiting for transfers between devices, trade(): lax.ppermute(value, 'rep', [(i, i ^ pair[i & 1]) for i in range(ways)])  13.3 us
    ppermute x9, starting transfers between devices, trade(): lax.ppermute(value, 'rep', [(i, i ^ pair[i & 1]) for i in range(ways)])  9.99 us
    unnamed x16, local copies, waits for them, and re-layouts  5.27 us
    ppermute x4, starting transfers between devices, swap(): lax.ppermute(piece, 'segment', [(i, (i + direction * shift) % sections) f...  5.05 us
    pallas_call x1, Pallas kernels, window(): call(functools.partial(forward_kernel, sizes=sizes, side=side), [packed f...  5 us
    ppermute x4, waiting for transfers between devices, swap(): lax.ppermute(piece, 'segment', [(i, (i + direction * shift) % sections) f...  3.37 us
    pallas_call x2, Pallas kernels, unpack(): call(unpack_kernel, shape(places * samples, channels, dtype=BF16), [VMEM]...  3.36 us
    pallas_call x2, Pallas kernels, tap_sums(): call(functools.partial(taps_kernel, side=side, slots=slots, flip=flip), h...  2.58 us
  transfers between devices with their start and end apart: 13, of which 7 were waited for; matrix products, arithmetic and copies ran while one was open for 0% of the time, Pallas kernels for 33%

profile of v5, /device:TPU:0, one launch (start us, length us, event | category | flops | bytes accessed | tf_op | source)
XLA Modules:
  0.0 62.1 jit_solution(1610091310134870344)
XLA Ops:
  0.7 2.5 %shard_map.84 = (bf16[196,1024]{1,0:T(8,128)(2,1)}, s32[8,392]{1,0:T(8,128)}) custom-call(s32[8]{0:T(128)} %bitcast.28, s32[1]{0:T(128)} %bitcast.1.at_ref, bf16[392,1024]{1,0:T(8,128)(2,1)} %bitcast.23), custom_call_target="tpu_custom_call" | custom-call | tf_op jit(solution)/shard_map/pallas_call | solution.py:397
  3.1 3.0 %collective-permute-start = (bf16[196,1024]{1,0:T(8,128)(2,1)}, bf16[196,1024]{1,0:T(8,128)(2,1)}, u32[]{:S(2)}, u32[]{:S(2)}) collective-permute-start(bf16[196,1024]{1,0:T(8,128)(2,1)} %get-tuple-element.42), channel_id=1, source_target_pairs={{0,16},{16,0},{1,17},{17,1},{2,18},{18,2},{3,19},{19,3},{4,20},{20... | collective-permute-start | bytes 1204232 | tf_op jit(solution)/shard_map/ppermute | solution.py:379
  6.1 1.1 %copy-done.2 = bf16[8,7,7,1024]{3,0,2,1:T(8,128)(2,1)S(1)} copy-done((bf16[8,7,7,1024]{3,0,2,1:T(8,128)(2,1)S(1)}, bf16[8,7,7,1024]{3,0,2,1:T(8,128)(2,1)}, u32[]{:S(2)}) %copy-start.2) | copy-done | bytes 802840
  7.2 0.7 %copy-done.5 = s32[8,392]{1,0:T(8,128)S(1)} copy-done((s32[8,392]{1,0:T(8,128)S(1)}, s32[8,392]{1,0:T(8,128)}, u32[]{:S(2)}) %copy-start.5) | copy-done | bytes 12568
  7.9 1.2 %shard_map.88 = bf16[196,1024]{1,0:T(8,128)(2,1)} custom-call(s32[8,392]{1,0:T(8,128)S(1)} %copy-done.5, s32[1]{0:T(128)} %bitcast.1.at_ref, bf16[392,1024]{1,0:T(8,128)(2,1)S(1)} %bitcast.25), custom_call_target="tpu_custom_call" | custom-call | tf_op jit(solution)/shard_map/pallas_call | solution.py:404
  9.1 0.0 collective-permute-start.2
  9.1 1.1 %copy-done.3 = bf16[8,7,7,1024]{3,0,2,1:T(8,128)(2,1)S(1)} copy-done((bf16[8,7,7,1024]{3,0,2,1:T(8,128)(2,1)S(1)}, bf16[8,7,7,1024]{3,0,2,1:T(8,128)(2,1)}, u32[]{:S(2)}) %copy-start.3) | copy-done | bytes 802840
  10.2 0.9 %copy-done.4 = f32[1,1,25,1024]{3,1,2,0:T(1,128)S(1)} copy-done((f32[1,1,25,1024]{3,1,2,0:T(1,128)S(1)}, f32[1,1,25,1024]{3,1,2,0:T(1,128)}, u32[]{:S(2)}) %copy-start.4) | copy-done | bytes 102424
  11.1 0.7 %copy-done.6 = s32[8,392]{1,0:T(8,128)S(1)} copy-done((s32[8,392]{1,0:T(8,128)S(1)}, s32[8,392]{1,0:T(8,128)}, u32[]{:S(2)}) %copy-start.6) | copy-done | bytes 12568
  11.9 0.7 %copy-done.7 = s32[1,8,1]{1,2,0:T(1,128)S(1)} copy-done((s32[1,8,1]{1,2,0:T(1,128)S(1)}, s32[1,8,1]{1,2,0:T(1,128)}, u32[]{:S(2)}) %copy-start.7) | copy-done | bytes 56
  12.5 1.9 %shard_map.85 = (bf16[392,1024]{1,0:T(8,128)(2,1)S(1)}, bf16[392,1024]{1,0:T(8,128)(2,1)S(1)}, f32[25,1,1024]{2,1,0:T(1,128)S(1)}, bf16[1,392,196]{2,1,0:T(8,128...) custom-call(s32[8]{0:T(128)S(1)} %bitcast.29, ...), custom_call_target="tpu_custom_call" | custom-call | tf_op jit(solution)/shard_map/pallas_call | solution.py:414
  14.4 2.3 %collective-permute-done.refs_0_ = bf16[196,1024]{1,0:T(8,128)(2,1)} collective-permute-done((bf16[196,1024]{1,0:T(8,128)(2,1)}, bf16[196,1024]{1,0:T(8,128)(2,1)}, u32[]{:S(2)}, u32[]{:S(2)}) %collective-permute-start) | collective-permute-done | bytes 401440 | tf_op jit(solution)/shard_map/ppermute | solution.py:379
  16.7 5.0 %shard_map.86 = (bf16[196,1024]{1,0:T(8,128)(2,1)S(1)}, bf16[8,64,196]{2,1,0:T(8,128)(2,1)S(1)}, bf16[8,64,196]{2,1,0:T(8,128)(2,1)S(1)}, bf16[392,1024]{1,0:T(8...) custom-call(s32[1]{0:T(128)} %bitcast.7.replica_ref, ...), custom_call_target="tpu_custom_call" | custom-call | tf_op jit(solution)/shard_map/pallas_call | solution.py:429
  21.7 1.7 %shard_map.92 = (f32[8,64,1024]{2,1,0:T(8,128)S(1)}, f32[8,64,1024]{2,1,0:T(8,128)S(1)}) custom-call(s32[1]{0:T(128)} %bitcast.7.replica_ref, bf16[392,1024]{1,0:T(8,128)(2,1)S(1)} %get-tuple-element.52.active_ref, bf16[392,1024]{1,0:T(8,128)(2,1)S(1)} %get-tuple-element.45.own_ref), custom_call_target="tpu_custom_call" | custom-call | tf_op jit(solution)/shard_map/pallas_call | solution.py:442
  23.5 1.1 %collective-permute-done.2.refs_0_.refs_1_ = bf16[196,1024]{1,0:T(8,128)(2,1)S(1)} collective-permute-done((bf16[196,1024]{1,0:T(8,128)(2,1)}, bf16[196,1024]{1,0:T(8,128)(2,1)S(1)}, u32[]{:S(2)}, u32[]{:S(2)}) %collective-permute-start.2) | collective-permute-done | bytes 401440 | tf_op jit(solution)/shard_map/ppermute | solution.py:379
  24.5 0.4 shard_map.94
  25.0 0.1 collective-permute-start.4
  25.0 0.4 shard_map.93.keep_ref
  25.5 2.2 %collective-permute-done.4.got_ref = bf16[8,64,1024]{2,1,0:T(8,128)(2,1)S(1)} collective-permute-done((bf16[8,64,1024]{2,1,0:T(8,128)(2,1)S(1)}, bf16[8,64,1024]{2,1,0:T(8,128)(2,1)S(1)}, u32[]{:S(2)}, u32[]{:S(2)}) %collective-permute-start.4) | collective-permute-done | bytes 1048608 | tf_op jit(solution)/shard_map/ppermute | solution.py:393
  27.7 0.2 shard_map.95
  27.9 1.8 %collective-permute-start.5 = (bf16[4,64,1024]{2,1,0:T(8,128)(2,1)S(1)}, bf16[4,64,1024]{2,1,0:T(8,128)(2,1)S(1)}, u32[]{:S(2)}, u32[]{:S(2)}) collective-permute-start(bf16[4,64,1024]{2,1,0:T(8,128)(2,1)S(1)} %get-tuple-element.58), channel_id=1, source_target_pairs={{0,2},{1,5},{2,0},{3,7},{4,6},{5,1},{6,4},{7,3},{8,10},{9,13},{10,... | collective-permute-start | bytes 1572872 | tf_op jit(solution)/shard_map/ppermute | solution.py:393
  29.7 1.5 %collective-permute-start.1 = (bf16[196,1024]{1,0:T(8,128)(2,1)S(1)}, bf16[196,1024]{1,0:T(8,128)(2,1)S(1)}, u32[]{:S(2)}, u32[]{:S(2)}) collective-permute-start(bf16[196,1024]{1,0:T(8,128)(2,1)S(1)} %get-tuple-element.44), channel_id=1, source_target_pairs={{0,16},{16,0},{1,17},{17,1},{2,18},{18,2},{3,19},{19,3},{4,20},{20... | collective-permute-start | bytes 1204232 | tf_op jit(solution)/shard_map/ppermute | solution.py:379
  31.2 1.5 %shard_map.89 = (bf16[392,1024]{1,0:T(8,128)(2,1)S(1)}, f32[392,1024]{1,0:T(8,128)S(1)}) custom-call(bf16[392,1024]{1,0:T(8,128)(2,1)S(1)} %get-tuple-element.45.own_ref, bf16[1,392,196]{2,1,0:T(8,128)(2,1)S(1)} %get-tuple-element.39.place_ref, bf16[1024,1024]{1,0:T(8,128)(2,1)S(1)} %bitcast.22, f32[392,1024]{1,0:T(8,128)S(1)} %get-tuple-element.46.scaled_ref, ...), custom_call_target="tpu_custom_call" | custom-call | tf_op jit(solution)/shard_map/pallas_call | solution.py:453
  32.7 2.4 %shard_map.90 = (bf16[196,1024]{1,0:T(8,128)(2,1)S(1)}, bf16[392,1024]{1,0:T(8,128)(2,1)S(1)}) custom-call(bf16[392,1024]{1,0:T(8,128)(2,1)S(1)} %get-tuple-element.48.slot_grads_ref, bf16[1,196,392]{2,1,0:T(8,128)(2,1)S(1)} %get-tuple-element.40.fetch_ref, f32[25,1,1024]{2,1,0:T(1,128)S(1)} %get-tuple-element.41.kernel_ref, ...), custom_call_target="tpu_custom_call" | custom-call | tf_op jit(solution)/shard_map/pallas_call | solution.py:459
  35.2 0.6 collective-permute-start.3
  35.8 1.3 %collective-permute-done.5.got_ref = bf16[4,64,1024]{2,1,0:T(8,128)(2,1)S(1)} collective-permute-done((bf16[4,64,1024]{2,1,0:T(8,128)(2,1)S(1)}, bf16[4,64,1024]{2,1,0:T(8,128)(2,1)S(1)}, u32[]{:S(2)}, u32[]{:S(2)}) %collective-permute-start.5) | collective-permute-done | bytes 524320 | tf_op jit(solution)/shard_map/ppermute | solution.py:393
  37.1 0.1 shard_map.96
  37.2 1.9 %collective-permute-start.6 = (bf16[2,64,1024]{2,1,0:T(8,128)(2,1)S(1)}, bf16[2,64,1024]{2,1,0:T(8,128)(2,1)S(1)}, u32[]{:S(2)}, u32[]{:S(2)}) collective-permute-start(bf16[2,64,1024]{2,1,0:T(8,128)(2,1)S(1)} %get-tuple-element.60), channel_id=1, source_target_pairs={{0,4},{1,3},{2,6},{3,1},{4,0},{5,7},{6,2},{7,5},{8,12},{9,11},{10,... | collective-permute-start | bytes 786440 | tf_op jit(solution)/shard_map/ppermute | solution.py:393
  39.1 1.3 %shard_map.99 = f32[25,1,512]{2,1,0:T(1,128)S(1)} custom-call(s32[1]{0:T(128)} %bitcast.1.at_ref, s32[1]{0:T(128)} %bitcast.7.replica_ref, f32[392,1024]{1,0:T(8,128)S(1)} %get-tuple-element.49.mixed_ref, f32[392,1024]{1,0:T(8,128)S(1)} %get-tuple-element.63.source_ref), custom_call_target="tpu_custom_call" | custom-call | tf_op jit(solution)/shard_map/pallas_call | solution.py:470
  40.4 0.1 collective-permute-start.8
  40.5 1.3 %shard_map.98 = f32[25,1,512]{2,1,0:T(1,128)S(1)} custom-call(s32[1]{0:T(128)} %bitcast.1.at_ref, s32[1]{0:T(128)} %bitcast.7.replica_ref, f32[392,1024]{1,0:T(8,128)S(1)} %get-tuple-element.49.mixed_ref, f32[392,1024]{1,0:T(8,128)S(1)} %get-tuple-element.63.source_ref), custom_call_target="tpu_custom_call" | custom-call | tf_op jit(solution)/shard_map/pallas_call | solution.py:470
  41.8 0.0 collective-permute-done.8
  41.8 0.1 add.12
  41.9 2.7 %collective-permute-start.9 = (f32[25,1,512]{2,1,0:T(1,128)S(1)}, f32[25,1,512]{2,1,0:T(1,128)S(1)}, u32[]{:S(2)}, u32[]{:S(2)}) collective-permute-start(f32[25,1,512]{2,1,0:T(1,128)S(1)} %add.12), channel_id=1, source_target_pairs={{0,8},{1,9},{2,10},{3,11},{4,12},{5,13},{6,14},{7,15},{8,0},{9,1},... | collective-permute-start | bytes 153608 | tf_op jit(solution)/shard_map/ppermute | solution.py:393
  44.5 3.5 %collective-permute-done.9 = f32[25,1,512]{2,1,0:T(1,128)S(1)} collective-permute-done((f32[25,1,512]{2,1,0:T(1,128)S(1)}, f32[25,1,512]{2,1,0:T(1,128)S(1)}, u32[]{:S(2)}, u32[]{:S(2)}) %collective-permute-start.9) | collective-permute-done | bytes 51232 | tf_op jit(solution)/shard_map/ppermute | solution.py:393
  48.0 0.1 add.13
  48.1 1.6 %collective-permute-start.10 = (f32[25,1,512]{2,1,0:T(1,128)S(1)}, f32[25,1,512]{2,1,0:T(1,128)S(1)}, u32[]{:S(2)}, u32[]{:S(2)}) collective-permute-start(f32[25,1,512]{2,1,0:T(1,128)S(1)} %add.13), channel_id=1, source_target_pairs={{0,2},{1,5},{2,0},{3,7},{4,6},{5,1},{6,4},{7,3},{8,10},{9,13},{10,... | collective-permute-start | bytes 153608 | tf_op jit(solution)/shard_map/ppermute | solution.py:393
  49.7 1.7 %collective-permute-start.7 = (bf16[1,64,1024]{2,1,0:T(8,128)(2,1)S(1)}, bf16[1,64,1024]{2,1,0:T(8,128)(2,1)S(1)}, u32[]{:S(2)}, u32[]{:S(2)}) collective-permute-start(bf16[1,64,1024]{2,1,0:T(8,128)(2,1)S(1)} %get-tuple-element.62), channel_id=1, source_target_pairs={{0,8},{1,9},{2,10},{3,11},{4,12},{5,13},{6,14},{7,15},{8,0},{9,1},... | collective-permute-start | bytes 393224 | tf_op jit(solution)/shard_map/ppermute | solution.py:393
  51.4 0.8 %collective-permute-done.10 = f32[25,1,512]{2,1,0:T(1,128)S(1)} collective-permute-done((f32[25,1,512]{2,1,0:T(1,128)S(1)}, f32[25,1,512]{2,1,0:T(1,128)S(1)}, u32[]{:S(2)}, u32[]{:S(2)}) %collective-permute-start.10) | collective-permute-done | bytes 51232 | tf_op jit(solution)/shard_map/ppermute | solution.py:393
  52.2 0.1 add.14
  52.3 0.1 collective-permute-start.11
  52.4 5.5 %collective-permute-done.11 = f32[25,1,512]{2,1,0:T(1,128)S(1)} collective-permute-done((f32[25,1,512]{2,1,0:T(1,128)S(1)}, f32[25,1,512]{2,1,0:T(1,128)S(1)}, u32[]{:S(2)}, u32[]{:S(2)}) %collective-permute-start.11) | collective-permute-done | bytes 51232 | tf_op jit(solution)/shard_map/ppermute | solution.py:393
  57.8 0.1 add.15.taps_ref
  57.9 0.1 collective-permute-start.12
  58.0 1.7 %shard_map.87 = bf16[392,1024]{1,0:T(8,128)(2,1)} custom-call(bf16[392,392]{1,0:T(8,128)(2,1)S(1)} %get-tuple-element.36.home_ref, bf16[1,392,196]{2,1,0:T(8,128)(2,1)S(1)} %get-tuple-element.37.merge_ref, bf16[392,1024]{1,0:T(8,128)(2,1)S(1)} %get-tuple-element.43.slots_ref, bf16[196,1024]{1,0:T(8,128)(2,1)S(1)} %collective-permute-done.1.refs_0_), custom_call_target="tpu_custom_call" | custom-call | tf_op jit(solution)/shard_map/pallas_call | solution.py:388
  59.7 0.0 collective-permute-done.3.refs_0_
  59.7 1.7 %shard_map.91 = bf16[392,1024]{1,0:T(8,128)(2,1)} custom-call(bf16[392,392]{1,0:T(8,128)(2,1)S(1)} %get-tuple-element.36.home_ref, bf16[1,392,196]{2,1,0:T(8,128)(2,1)S(1)} %get-tuple-element.37.merge_ref, bf16[392,1024]{1,0:T(8,128)(2,1)S(1)} %get-tuple-element.50.slots_ref, bf16[196,1024]{1,0:T(8,128)(2,1)S(1)} %collective-permute-done.3.refs_0_), custom_call_target="tpu_custom_call" | custom-call | tf_op jit(solution)/shard_map/pallas_call | solution.py:388
  61.3 0.8 %shard_map.100 = (f32[64,1024]{1,0:T(8,128)}, f32[25,1,1024]{2,1,0:T(1,128)}) custom-call(s32[1]{0:T(128)} %bitcast.7.replica_ref, f32[1,64,1024]{2,1,0:T(8,128)S(1)} %get-tuple-element.61.keep_ref, bf16[1,64,1024]{2,1,0:T(8,128)(2,1)S(1)} %collective-permute-done.7.got_ref, f32[25,1,512]{2,1,0:T(1,128)S(1)} %add.15.taps_ref, ...), custom_call_target="tpu_custom_call" | custom-call | tf_op jit(solution)/shard_map/pallas_call | solution.py:499
  (15 shorter events, 0.1 us)
Async XLA Ops:
  0.6 8.5 %copy-start.1 = (bf16[8,7,7,1024]{3,0,2,1:T(8,128)(2,1)S(1)}, bf16[8,7,7,1024]{3,0,2,1:T(8,128)(2,1)}, u32[]{:S(2)}) copy-start(bf16[8,7,7,1024]{3,0,2,1:T(8,128)(2,1)} %param.5) | copy-start | bytes 2408452
  0.6 16.1 %copy-start = (bf16[1,1,1024,1024]{3,2,1,0:T(8,128)(2,1)S(1)}, bf16[1,1,1024,1024]{3,2,1,0:T(8,128)(2,1)}, u32[]{:S(2)}) copy-start(bf16[1,1,1024,1024]{3,2,1,0:T(8,128)(2,1)} %param.7) | copy-start | bytes 6291460
  3.1 13.6 %collective-permute-start = (bf16[196,1024]{1,0:T(8,128)(2,1)}, bf16[196,1024]{1,0:T(8,128)(2,1)}, u32[]{:S(2)}, u32[]{:S(2)}) collective-permute-start(bf16[196,1024]{1,0:T(8,128)(2,1)} %get-tuple-element.42), channel_id=1, source_target_pairs={{0,16},{16,0},{1,17},{17,1},{2,18},{18,2},{3,19},{19,3},{4,20},{20... | collective-permute-start | bytes 1204232 | tf_op jit(solution)/shard_map/ppermute | solution.py:379
  6.1 1.1 %copy-start.2 = (bf16[8,7,7,1024]{3,0,2,1:T(8,128)(2,1)S(1)}, bf16[8,7,7,1024]{3,0,2,1:T(8,128)(2,1)}, u32[]{:S(2)}) copy-start(bf16[8,7,7,1024]{3,0,2,1:T(8,128)(2,1)} %param.9) | copy-start | bytes 2408452
  7.2 0.7 %copy-start.5 = (s32[8,392]{1,0:T(8,128)S(1)}, s32[8,392]{1,0:T(8,128)}, u32[]{:S(2)}) copy-start(s32[8,392]{1,0:T(8,128)} %get-tuple-element.35.code_ref) | copy-start | bytes 37636
  9.1 15.4 %collective-permute-start.2 = (bf16[196,1024]{1,0:T(8,128)(2,1)}, bf16[196,1024]{1,0:T(8,128)(2,1)S(1)}, u32[]{:S(2)}, u32[]{:S(2)}) collective-permute-start(bf16[196,1024]{1,0:T(8,128)(2,1)} %shard_map.88), channel_id=1, source_target_pairs={{0,16},{16,0},{1,17},{17,1},{2,18},{18,2},{3,19},{19,3},{4,20},{20... | collective-permute-start | bytes 1204232 | tf_op jit(solution)/shard_map/ppermute | solution.py:379
  9.1 1.1 %copy-start.3 = (bf16[8,7,7,1024]{3,0,2,1:T(8,128)(2,1)S(1)}, bf16[8,7,7,1024]{3,0,2,1:T(8,128)(2,1)}, u32[]{:S(2)}) copy-start(bf16[8,7,7,1024]{3,0,2,1:T(8,128)(2,1)} %param.9) | copy-start | bytes 2408452
  10.2 0.9 %copy-start.4 = (f32[1,1,25,1024]{3,1,2,0:T(1,128)S(1)}, f32[1,1,25,1024]{3,1,2,0:T(1,128)}, u32[]{:S(2)}) copy-start(f32[1,1,25,1024]{3,1,2,0:T(1,128)} %param.8) | copy-start | bytes 307204
  11.1 0.7 %copy-start.6 = (s32[8,392]{1,0:T(8,128)S(1)}, s32[8,392]{1,0:T(8,128)}, u32[]{:S(2)}) copy-start(s32[8,392]{1,0:T(8,128)} %get-tuple-element.35.code_ref) | copy-start | bytes 37636
  11.9 0.7 %copy-start.7 = (s32[1,8,1]{1,2,0:T(1,128)S(1)}, s32[1,8,1]{1,2,0:T(1,128)}, u32[]{:S(2)}) copy-start(s32[1,8,1]{1,2,0:T(1,128)} %param.6) | copy-start | bytes 100
  25.0 2.7 %collective-permute-start.4 = (bf16[8,64,1024]{2,1,0:T(8,128)(2,1)S(1)}, bf16[8,64,1024]{2,1,0:T(8,128)(2,1)S(1)}, u32[]{:S(2)}, u32[]{:S(2)}) collective-permute-start(bf16[8,64,1024]{2,1,0:T(8,128)(2,1)S(1)} %shard_map.94), channel_id=1, source_target_pairs={{0,1},{1,0},{2,3},{3,2},{4,5},{5,4},{6,7},{7,6},{8,9},{9,8},{10,11... | collective-permute-start | bytes 3145736 | tf_op jit(solution)/shard_map/ppermute | solution.py:393
  27.9 9.2 %collective-permute-start.5 = (bf16[4,64,1024]{2,1,0:T(8,128)(2,1)S(1)}, bf16[4,64,1024]{2,1,0:T(8,128)(2,1)S(1)}, u32[]{:S(2)}, u32[]{:S(2)}) collective-permute-start(bf16[4,64,1024]{2,1,0:T(8,128)(2,1)S(1)} %get-tuple-element.58), channel_id=1, source_target_pairs={{0,2},{1,5},{2,0},{3,7},{4,6},{5,1},{6,4},{7,3},{8,10},{9,13},{10,... | collective-permute-start | bytes 1572872 | tf_op jit(solution)/shard_map/ppermute | solution.py:393
  29.7 28.3 %collective-permute-start.1 = (bf16[196,1024]{1,0:T(8,128)(2,1)S(1)}, bf16[196,1024]{1,0:T(8,128)(2,1)S(1)}, u32[]{:S(2)}, u32[]{:S(2)}) collective-permute-start(bf16[196,1024]{1,0:T(8,128)(2,1)S(1)} %get-tuple-element.44), channel_id=1, source_target_pairs={{0,16},{16,0},{1,17},{17,1},{2,18},{18,2},{3,19},{19,3},{4,20},{20... | collective-permute-start | bytes 1204232 | tf_op jit(solution)/shard_map/ppermute | solution.py:379
  35.2 24.5 %collective-permute-start.3 = (bf16[196,1024]{1,0:T(8,128)(2,1)S(1)}, bf16[196,1024]{1,0:T(8,128)(2,1)S(1)}, u32[]{:S(2)}, u32[]{:S(2)}) collective-permute-start(bf16[196,1024]{1,0:T(8,128)(2,1)S(1)} %get-tuple-element.51), channel_id=1, source_target_pairs={{0,16},{16,0},{1,17},{17,1},{2,18},{18,2},{3,19},{19,3},{4,20},{20... | collective-permute-start | bytes 1204232 | tf_op jit(solution)/shard_map/ppermute | solution.py:379
  37.2 12.5 %collective-permute-start.6 = (bf16[2,64,1024]{2,1,0:T(8,128)(2,1)S(1)}, bf16[2,64,1024]{2,1,0:T(8,128)(2,1)S(1)}, u32[]{:S(2)}, u32[]{:S(2)}) collective-permute-start(bf16[2,64,1024]{2,1,0:T(8,128)(2,1)S(1)} %get-tuple-element.60), channel_id=1, source_target_pairs={{0,4},{1,3},{2,6},{3,1},{4,0},{5,7},{6,2},{7,5},{8,12},{9,11},{10,... | collective-permute-start | bytes 786440 | tf_op jit(solution)/shard_map/ppermute | solution.py:393
  40.4 1.4 %collective-permute-start.8 = (f32[25,1,512]{2,1,0:T(1,128)S(1)}, f32[25,1,512]{2,1,0:T(1,128)S(1)}, u32[]{:S(2)}, u32[]{:S(2)}) collective-permute-start(f32[25,1,512]{2,1,0:T(1,128)S(1)} %shard_map.99), channel_id=1, source_target_pairs={{0,1},{1,0},{2,3},{3,2},{4,5},{5,4},{6,7},{7,6},{8,9},{9,8},{10,11... | collective-permute-start | bytes 153608 | tf_op jit(solution)/shard_map/ppermute | solution.py:393
  41.9 6.1 %collective-permute-start.9 = (f32[25,1,512]{2,1,0:T(1,128)S(1)}, f32[25,1,512]{2,1,0:T(1,128)S(1)}, u32[]{:S(2)}, u32[]{:S(2)}) collective-permute-start(f32[25,1,512]{2,1,0:T(1,128)S(1)} %add.12), channel_id=1, source_target_pairs={{0,8},{1,9},{2,10},{3,11},{4,12},{5,13},{6,14},{7,15},{8,0},{9,1},... | collective-permute-start | bytes 153608 | tf_op jit(solution)/shard_map/ppermute | solution.py:393
  48.1 4.2 %collective-permute-start.10 = (f32[25,1,512]{2,1,0:T(1,128)S(1)}, f32[25,1,512]{2,1,0:T(1,128)S(1)}, u32[]{:S(2)}, u32[]{:S(2)}) collective-permute-start(f32[25,1,512]{2,1,0:T(1,128)S(1)} %add.13), channel_id=1, source_target_pairs={{0,2},{1,5},{2,0},{3,7},{4,6},{5,1},{6,4},{7,3},{8,10},{9,13},{10,... | collective-permute-start | bytes 153608 | tf_op jit(solution)/shard_map/ppermute | solution.py:393
  49.7 11.6 %collective-permute-start.7 = (bf16[1,64,1024]{2,1,0:T(8,128)(2,1)S(1)}, bf16[1,64,1024]{2,1,0:T(8,128)(2,1)S(1)}, u32[]{:S(2)}, u32[]{:S(2)}) collective-permute-start(bf16[1,64,1024]{2,1,0:T(8,128)(2,1)S(1)} %get-tuple-element.62), channel_id=1, source_target_pairs={{0,8},{1,9},{2,10},{3,11},{4,12},{5,13},{6,14},{7,15},{8,0},{9,1},... | collective-permute-start | bytes 393224 | tf_op jit(solution)/shard_map/ppermute | solution.py:393
  52.3 5.5 %collective-permute-start.11 = (f32[25,1,512]{2,1,0:T(1,128)S(1)}, f32[25,1,512]{2,1,0:T(1,128)S(1)}, u32[]{:S(2)}, u32[]{:S(2)}) collective-permute-start(f32[25,1,512]{2,1,0:T(1,128)S(1)} %add.14), channel_id=1, source_target_pairs={{0,4},{1,3},{2,6},{3,1},{4,0},{5,7},{6,2},{7,5},{8,12},{9,11},{10,... | collective-permute-start | bytes 153608 | tf_op jit(solution)/shard_map/ppermute | solution.py:393
  57.9 3.5 %collective-permute-start.12 = (f32[25,1,512]{2,1,0:T(1,128)S(1)}, f32[25,1,512]{2,1,0:T(1,128)S(1)}, u32[]{:S(2)}, u32[]{:S(2)}) collective-permute-start(f32[25,1,512]{2,1,0:T(1,128)S(1)} %add.15.taps_ref), channel_id=1, source_target_pairs={{0,1},{1,0},{2,3},{3,2},{4,5},{5,4},{6,7},{7,6},{8,9},{9,8},{10,11... | collective-permute-start | bytes 153608 | tf_op jit(solution)/shard_map/ppermute | solution.py:393

commit v6 on v5

--- a/solution.py
+++ b/solution.py
@@ -234,22 +234,26 @@
         deal(replica_ref, turned_ref, give_refs[at], hold_refs[at])
 
 
-def own_point_kernel(replica_ref, active_ref, own_ref, give_ref, hold_ref, total_ref):
-    total_ref[...] = lax.dot_general(
+def own_point_kernel(active_ref, own_ref, total_ref):
+    total = lax.dot_general(
         active_ref[...], own_ref[...], (((0,), (0,)), ((), ())), preferred_element_type=F32
     )
-    deal(replica_ref, total_ref, give_ref, hold_ref)
-
-
-def point_kernel(own_ref, *refs):
+    total_ref[...] = total.reshape(total_ref.shape)
+
+
+def point_kernel(replica_ref, own_ref, *refs, flip):
     out_ref = refs[-1]
     active_refs, got_refs = refs[: len(refs) // 2], refs[len(refs) // 2 : -1]
-    shape = own_ref.shape
-    total = own_ref[...].reshape(shape[0] * shape[1], shape[2])
+    count, block, _ = out_ref.shape
+    total = None
     for active_ref, got_ref in zip(active_refs, got_refs):
-        active = active_ref[...].reshape(shape[0] * shape[1], active_ref.shape[2])
-        total = total + pick(active, got_ref[...])
-    out_ref[...] = total.reshape(shape).astype(out_ref.dtype)
+        active = active_ref[...].reshape(count * block, active_ref.shape[2])
+        share = pick(active, got_ref[...])
+        total = share if total is None else total + share
+    total = total.reshape(out_ref.shape)
+    which = (replica_ref[0] & 1) ^ flip
+    for at in range(count):
+        out_ref[at] = (total[at] + own_ref[2 * at + which]).astype(out_ref.dtype)
 
 
 def fold_kernel(replica_ref, keep_ref, got_ref, send_ref, left_ref, *, strides, bits):
@@ -439,16 +443,19 @@
     slot_final, active, scaled, inverse, source = results[3 * count :]
 
     part = shape(ways // 2, block, channels)
-    own_give, own_hold = call(
-        own_point_kernel, [part, part], [SMEM, VMEM, VMEM], [pltpu.VMEM((channels, channels), F32)]
-    )(replica, active, own_grads)
+    own_point = call(
+        own_point_kernel, shape(ways, block, channels), [VMEM, VMEM]
+    )(active, own_grads)
     got_final = swap(back, -1)
 
-    send = call(
-        point_kernel, shape(ways // 2, block, channels, dtype=BF16), [VMEM] * (1 + 2 * count)
-    )(own_give, *active_give, *got_grads)
+    def point(flip, out, active_blocks):
+        return call(
+            functools.partial(point_kernel, flip=flip), out, [SMEM] + [VMEM] * (1 + 2 * count)
+        )(replica, own_point, *active_blocks, *got_grads)
+
+    send = point(1, shape(*part.shape, dtype=BF16), active_give)
     got = trade(send, (1, 1))
-    keep = call(point_kernel, part, [VMEM] * (1 + 2 * count))(own_hold, *active_hold, *got_grads)
+    keep = point(0, part, active_hold)
 
     slot_grads, mixed = call(
         functools.partial(mixed_kernel, block=side * slots),

time: 62.5 us -> 62.5 us (level)
  transfers between devices with their start and end apart: 13 -> 13, of which waited for: 7 -> 7; matrix products, arithmetic and copies ran while one was open for 0% -> 0% of each run, Pallas kernels for 33% -> 32%
where the time goes in v6:
time: 62.5 us; the launch traced here: 62.1 us
  Pallas kernels  23.8 us (38%)
  waiting for transfers between devices  17 us (27%)
  starting transfers between devices  15 us (24%)
  local copies, waits for them, and re-layouts  5.27 us (8%)
  between operations  0.79 us (1%)
    ppermute x9, waiting for transfers between devices, trade(): lax.ppermute(value, 'rep', [(i, i ^ pair[i & 1]) for i in range(ways)])  13.2 us
    ppermute x9, starting transfers between devices, trade(): lax.ppermute(value, 'rep', [(i, i ^ pair[i & 1]) for i in range(ways)])  9.98 us
    unnamed x16, local copies, waits for them, and re-layouts  5.27 us
    ppermute x4, starting transfers between devices, swap(): lax.ppermute(piece, 'segment', [(i, (i + direction * shift) % sections) f...  5.05 us
    pallas_call x1, Pallas kernels, window(): call(functools.partial(forward_kernel, sizes=sizes, side=side), [packed f...  5.03 us
    ppermute x4, waiting for transfers between devices, swap(): lax.ppermute(piece, 'segment', [(i, (i + direction * shift) % sections) f...  3.78 us
    pallas_call x2, Pallas kernels, unpack(): call(unpack_kernel, shape(places * samples, channels, dtype=BF16), [VMEM]...  3.36 us
    pallas_call x2, Pallas kernels, tap_sums(): call(functools.partial(taps_kernel, side=side, slots=slots, flip=flip), h...  2.58 us
  transfers between devices with their start and end apart: 13, of which 7 were waited for; matrix products, arithmetic and copies ran while one was open for 0% of the time, Pallas kernels for 32%

profile of v6, /device:TPU:0, one launch (start us, length us, event | category | flops | bytes accessed | tf_op | source)
XLA Modules:
  0.0 62.1 jit_solution(18041821944255117344)
XLA Ops:
  0.7 2.5 %shard_map.84 = (bf16[196,1024]{1,0:T(8,128)(2,1)}, s32[8,392]{1,0:T(8,128)}) custom-call(s32[8]{0:T(128)} %bitcast.28, s32[1]{0:T(128)} %bitcast.1.at_ref, bf16[392,1024]{1,0:T(8,128)(2,1)} %bitcast.23), custom_call_target="tpu_custom_call" | custom-call | tf_op jit(solution)/shard_map/pallas_call | solution.py:401
  3.1 3.0 %collective-permute-start = (bf16[196,1024]{1,0:T(8,128)(2,1)}, bf16[196,1024]{1,0:T(8,128)(2,1)}, u32[]{:S(2)}, u32[]{:S(2)}) collective-permute-start(bf16[196,1024]{1,0:T(8,128)(2,1)} %get-tuple-element.40), channel_id=1, source_target_pairs={{0,16},{16,0},{1,17},{17,1},{2,18},{18,2},{3,19},{19,3},{4,20},{20... | collective-permute-start | bytes 1204232 | tf_op jit(solution)/shard_map/ppermute | solution.py:383
  6.1 1.1 %copy-done.2 = bf16[8,7,7,1024]{3,0,2,1:T(8,128)(2,1)S(1)} copy-done((bf16[8,7,7,1024]{3,0,2,1:T(8,128)(2,1)S(1)}, bf16[8,7,7,1024]{3,0,2,1:T(8,128)(2,1)}, u32[]{:S(2)}) %copy-start.2) | copy-done | bytes 802840
  7.2 0.7 %copy-done.5 = s32[8,392]{1,0:T(8,128)S(1)} copy-done((s32[8,392]{1,0:T(8,128)S(1)}, s32[8,392]{1,0:T(8,128)}, u32[]{:S(2)}) %copy-start.5) | copy-done | bytes 12568
  7.9 1.2 %shard_map.88 = bf16[196,1024]{1,0:T(8,128)(2,1)} custom-call(s32[8,392]{1,0:T(8,128)S(1)} %copy-done.5, s32[1]{0:T(128)} %bitcast.1.at_ref, bf16[392,1024]{1,0:T(8,128)(2,1)S(1)} %bitcast.25), custom_call_target="tpu_custom_call" | custom-call | tf_op jit(solution)/shard_map/pallas_call | solution.py:408
  9.1 0.0 collective-permute-start.2
  9.1 1.1 %copy-done.3 = bf16[8,7,7,1024]{3,0,2,1:T(8,128)(2,1)S(1)} copy-done((bf16[8,7,7,1024]{3,0,2,1:T(8,128)(2,1)S(1)}, bf16[8,7,7,1024]{3,0,2,1:T(8,128)(2,1)}, u32[]{:S(2)}) %copy-start.3) | copy-done | bytes 802840
  10.2 0.9 %copy-done.4 = f32[1,1,25,1024]{3,1,2,0:T(1,128)S(1)} copy-done((f32[1,1,25,1024]{3,1,2,0:T(1,128)S(1)}, f32[1,1,25,1024]{3,1,2,0:T(1,128)}, u32[]{:S(2)}) %copy-start.4) | copy-done | bytes 102424
  11.1 0.7 %copy-done.6 = s32[8,392]{1,0:T(8,128)S(1)} copy-done((s32[8,392]{1,0:T(8,128)S(1)}, s32[8,392]{1,0:T(8,128)}, u32[]{:S(2)}) %copy-start.6) | copy-done | bytes 12568
  11.9 0.7 %copy-done.7 = s32[1,8,1]{1,2,0:T(1,128)S(1)} copy-done((s32[1,8,1]{1,2,0:T(1,128)S(1)}, s32[1,8,1]{1,2,0:T(1,128)}, u32[]{:S(2)}) %copy-start.7) | copy-done | bytes 56
  12.5 1.9 %shard_map.85 = (bf16[392,1024]{1,0:T(8,128)(2,1)S(1)}, bf16[392,1024]{1,0:T(8,128)(2,1)S(1)}, f32[25,1,1024]{2,1,0:T(1,128)S(1)}, bf16[1,392,196]{2,1,0:T(8,128...) custom-call(s32[8]{0:T(128)S(1)} %bitcast.29, ...), custom_call_target="tpu_custom_call" | custom-call | tf_op jit(solution)/shard_map/pallas_call | solution.py:418
  14.4 2.3 %collective-permute-done.refs_0_ = bf16[196,1024]{1,0:T(8,128)(2,1)} collective-permute-done((bf16[196,1024]{1,0:T(8,128)(2,1)}, bf16[196,1024]{1,0:T(8,128)(2,1)}, u32[]{:S(2)}, u32[]{:S(2)}) %collective-permute-start) | collective-permute-done | bytes 401440 | tf_op jit(solution)/shard_map/ppermute | solution.py:383
  16.7 5.0 %shard_map.86 = (bf16[196,1024]{1,0:T(8,128)(2,1)S(1)}, bf16[8,64,196]{2,1,0:T(8,128)(2,1)S(1)}, bf16[8,64,196]{2,1,0:T(8,128)(2,1)S(1)}, bf16[392,1024]{1,0:T(8...) custom-call(s32[1]{0:T(128)} %bitcast.7.replica_ref, ...), custom_call_target="tpu_custom_call" | custom-call | tf_op jit(solution)/shard_map/pallas_call | solution.py:433
  21.7 1.3 %shard_map.92.own_ref = f32[16,64,1024]{2,1,0:T(8,128)S(1)} custom-call(bf16[392,1024]{1,0:T(8,128)(2,1)S(1)} %get-tuple-element.50.active_ref, bf16[392,1024]{1,0:T(8,128)(2,1)S(1)} %get-tuple-element.43.own_ref), custom_call_target="tpu_custom_call" | custom-call | tf_op jit(solution)/shard_map/pallas_call | solution.py:446
  23.0 1.5 %collective-permute-done.2.refs_0_.refs_1_ = bf16[196,1024]{1,0:T(8,128)(2,1)S(1)} collective-permute-done((bf16[196,1024]{1,0:T(8,128)(2,1)}, bf16[196,1024]{1,0:T(8,128)(2,1)S(1)}, u32[]{:S(2)}, u32[]{:S(2)}) %collective-permute-start.2) | collective-permute-done | bytes 401440 | tf_op jit(solution)/shard_map/ppermute | solution.py:383
  24.5 0.4 shard_map.94
  25.0 0.1 collective-permute-start.4
  25.0 0.5 shard_map.93.keep_ref
  25.5 2.2 %collective-permute-done.4.got_ref = bf16[8,64,1024]{2,1,0:T(8,128)(2,1)S(1)} collective-permute-done((bf16[8,64,1024]{2,1,0:T(8,128)(2,1)S(1)}, bf16[8,64,1024]{2,1,0:T(8,128)(2,1)S(1)}, u32[]{:S(2)}, u32[]{:S(2)}) %collective-permute-start.4) | collective-permute-done | bytes 1048608 | tf_op jit(solution)/shard_map/ppermute | solution.py:397
  27.7 0.2 shard_map.95
  27.9 1.8 %collective-permute-start.5 = (bf16[4,64,1024]{2,1,0:T(8,128)(2,1)S(1)}, bf16[4,64,1024]{2,1,0:T(8,128)(2,1)S(1)}, u32[]{:S(2)}, u32[]{:S(2)}) collective-permute-start(bf16[4,64,1024]{2,1,0:T(8,128)(2,1)S(1)} %get-tuple-element.54), channel_id=1, source_target_pairs={{0,2},{1,5},{2,0},{3,7},{4,6},{5,1},{6,4},{7,3},{8,10},{9,13},{10,... | collective-permute-start | bytes 1572872 | tf_op jit(solution)/shard_map/ppermute | solution.py:397
  29.7 1.5 %collective-permute-start.1 = (bf16[196,1024]{1,0:T(8,128)(2,1)S(1)}, bf16[196,1024]{1,0:T(8,128)(2,1)S(1)}, u32[]{:S(2)}, u32[]{:S(2)}) collective-permute-start(bf16[196,1024]{1,0:T(8,128)(2,1)S(1)} %get-tuple-element.42), channel_id=1, source_target_pairs={{0,16},{16,0},{1,17},{17,1},{2,18},{18,2},{3,19},{19,3},{4,20},{20... | collective-permute-start | bytes 1204232 | tf_op jit(solution)/shard_map/ppermute | solution.py:383
  31.2 1.6 %shard_map.89 = (bf16[392,1024]{1,0:T(8,128)(2,1)S(1)}, f32[392,1024]{1,0:T(8,128)S(1)}) custom-call(bf16[392,1024]{1,0:T(8,128)(2,1)S(1)} %get-tuple-element.43.own_ref, bf16[1,392,196]{2,1,0:T(8,128)(2,1)S(1)} %get-tuple-element.37.place_ref, bf16[1024,1024]{1,0:T(8,128)(2,1)S(1)} %bitcast.22, f32[392,1024]{1,0:T(8,128)S(1)} %get-tuple-element.44.scaled_ref, ...), custom_call_target="tpu_custom_call" | custom-call | tf_op jit(solution)/shard_map/pallas_call | solution.py:460
  32.8 2.4 %shard_map.90 = (bf16[196,1024]{1,0:T(8,128)(2,1)S(1)}, bf16[392,1024]{1,0:T(8,128)(2,1)S(1)}) custom-call(bf16[392,1024]{1,0:T(8,128)(2,1)S(1)} %get-tuple-element.46.slot_grads_ref, bf16[1,196,392]{2,1,0:T(8,128)(2,1)S(1)} %get-tuple-element.38.fetch_ref, f32[25,1,1024]{2,1,0:T(1,128)S(1)} %get-tuple-element.39.kernel_ref, ...), custom_call_target="tpu_custom_call" | custom-call | tf_op jit(solution)/shard_map/pallas_call | solution.py:466
  35.2 0.6 collective-permute-start.3
  35.8 1.3 %collective-permute-done.5.got_ref = bf16[4,64,1024]{2,1,0:T(8,128)(2,1)S(1)} collective-permute-done((bf16[4,64,1024]{2,1,0:T(8,128)(2,1)S(1)}, bf16[4,64,1024]{2,1,0:T(8,128)(2,1)S(1)}, u32[]{:S(2)}, u32[]{:S(2)}) %collective-permute-start.5) | collective-permute-done | bytes 524320 | tf_op jit(solution)/shard_map/ppermute | solution.py:397
  37.1 0.1 shard_map.96
  37.2 1.9 %collective-permute-start.6 = (bf16[2,64,1024]{2,1,0:T(8,128)(2,1)S(1)}, bf16[2,64,1024]{2,1,0:T(8,128)(2,1)S(1)}, u32[]{:S(2)}, u32[]{:S(2)}) collective-permute-start(bf16[2,64,1024]{2,1,0:T(8,128)(2,1)S(1)} %get-tuple-element.56), channel_id=1, source_target_pairs={{0,4},{1,3},{2,6},{3,1},{4,0},{5,7},{6,2},{7,5},{8,12},{9,11},{10,... | collective-permute-start | bytes 786440 | tf_op jit(solution)/shard_map/ppermute | solution.py:397
  39.1 1.3 %shard_map.99 = f32[25,1,512]{2,1,0:T(1,128)S(1)} custom-call(s32[1]{0:T(128)} %bitcast.1.at_ref, s32[1]{0:T(128)} %bitcast.7.replica_ref, f32[392,1024]{1,0:T(8,128)S(1)} %get-tuple-element.47.mixed_ref, f32[392,1024]{1,0:T(8,128)S(1)} %get-tuple-element.59.source_ref), custom_call_target="tpu_custom_call" | custom-call | tf_op jit(solution)/shard_map/pallas_call | solution.py:477
  40.4 0.1 collective-permute-start.8
  40.5 1.3 %shard_map.98 = f32[25,1,512]{2,1,0:T(1,128)S(1)} custom-call(s32[1]{0:T(128)} %bitcast.1.at_ref, s32[1]{0:T(128)} %bitcast.7.replica_ref, f32[392,1024]{1,0:T(8,128)S(1)} %get-tuple-element.47.mixed_ref, f32[392,1024]{1,0:T(8,128)S(1)} %get-tuple-element.59.source_ref), custom_call_target="tpu_custom_call" | custom-call | tf_op jit(solution)/shard_map/pallas_call | solution.py:477
  41.8 0.1 add.12
  41.9 2.7 %collective-permute-start.9 = (f32[25,1,512]{2,1,0:T(1,128)S(1)}, f32[25,1,512]{2,1,0:T(1,128)S(1)}, u32[]{:S(2)}, u32[]{:S(2)}) collective-permute-start(f32[25,1,512]{2,1,0:T(1,128)S(1)} %add.12), channel_id=1, source_target_pairs={{0,8},{1,9},{2,10},{3,11},{4,12},{5,13},{6,14},{7,15},{8,0},{9,1},... | collective-permute-start | bytes 153608 | tf_op jit(solution)/shard_map/ppermute | solution.py:397
  44.5 3.5 %collective-permute-done.9 = f32[25,1,512]{2,1,0:T(1,128)S(1)} collective-permute-done((f32[25,1,512]{2,1,0:T(1,128)S(1)}, f32[25,1,512]{2,1,0:T(1,128)S(1)}, u32[]{:S(2)}, u32[]{:S(2)}) %collective-permute-start.9) | collective-permute-done | bytes 51232 | tf_op jit(solution)/shard_map/ppermute | solution.py:397
  48.0 0.1 add.13
  48.1 1.6 %collective-permute-start.10 = (f32[25,1,512]{2,1,0:T(1,128)S(1)}, f32[25,1,512]{2,1,0:T(1,128)S(1)}, u32[]{:S(2)}, u32[]{:S(2)}) collective-permute-start(f32[25,1,512]{2,1,0:T(1,128)S(1)} %add.13), channel_id=1, source_target_pairs={{0,2},{1,5},{2,0},{3,7},{4,6},{5,1},{6,4},{7,3},{8,10},{9,13},{10,... | collective-permute-start | bytes 153608 | tf_op jit(solution)/shard_map/ppermute | solution.py:397
  49.7 0.0 collective-permute-done.6.got_ref
  49.7 1.7 %collective-permute-start.7 = (bf16[1,64,1024]{2,1,0:T(8,128)(2,1)S(1)}, bf16[1,64,1024]{2,1,0:T(8,128)(2,1)S(1)}, u32[]{:S(2)}, u32[]{:S(2)}) collective-permute-start(bf16[1,64,1024]{2,1,0:T(8,128)(2,1)S(1)} %get-tuple-element.58), channel_id=1, source_target_pairs={{0,8},{1,9},{2,10},{3,11},{4,12},{5,13},{6,14},{7,15},{8,0},{9,1},... | collective-permute-start | bytes 393224 | tf_op jit(solution)/shard_map/ppermute | solution.py:397
  51.4 0.8 %collective-permute-done.10 = f32[25,1,512]{2,1,0:T(1,128)S(1)} collective-permute-done((f32[25,1,512]{2,1,0:T(1,128)S(1)}, f32[25,1,512]{2,1,0:T(1,128)S(1)}, u32[]{:S(2)}, u32[]{:S(2)}) %collective-permute-start.10) | collective-permute-done | bytes 51232 | tf_op jit(solution)/shard_map/ppermute | solution.py:397
  52.2 0.1 add.14
  52.3 0.1 collective-permute-start.11
  52.4 5.4 %collective-permute-done.11 = f32[25,1,512]{2,1,0:T(1,128)S(1)} collective-permute-done((f32[25,1,512]{2,1,0:T(1,128)S(1)}, f32[25,1,512]{2,1,0:T(1,128)S(1)}, u32[]{:S(2)}, u32[]{:S(2)}) %collective-permute-start.11) | collective-permute-done | bytes 51232 | tf_op jit(solution)/shard_map/ppermute | solution.py:397
  57.8 0.1 add.15.taps_ref
  57.9 0.1 collective-permute-start.12
  58.0 1.7 %shard_map.87 = bf16[392,1024]{1,0:T(8,128)(2,1)} custom-call(bf16[392,392]{1,0:T(8,128)(2,1)S(1)} %get-tuple-element.34.home_ref, bf16[1,392,196]{2,1,0:T(8,128)(2,1)S(1)} %get-tuple-element.35.merge_ref, bf16[392,1024]{1,0:T(8,128)(2,1)S(1)} %get-tuple-element.41.slots_ref, bf16[196,1024]{1,0:T(8,128)(2,1)S(1)} %collective-permute-done.1.refs_0_), custom_call_target="tpu_custom_call" | custom-call | tf_op jit(solution)/shard_map/pallas_call | solution.py:392
  59.7 1.7 %shard_map.91 = bf16[392,1024]{1,0:T(8,128)(2,1)} custom-call(bf16[392,392]{1,0:T(8,128)(2,1)S(1)} %get-tuple-element.34.home_ref, bf16[1,392,196]{2,1,0:T(8,128)(2,1)S(1)} %get-tuple-element.35.merge_ref, bf16[392,1024]{1,0:T(8,128)(2,1)S(1)} %get-tuple-element.48.slots_ref, bf16[196,1024]{1,0:T(8,128)(2,1)S(1)} %collective-permute-done.3.refs_0_), custom_call_target="tpu_custom_call" | custom-call | tf_op jit(solution)/shard_map/pallas_call | solution.py:392
  61.3 0.0 collective-permute-done.12.came_ref
  61.3 0.8 %shard_map.100 = (f32[64,1024]{1,0:T(8,128)}, f32[25,1,1024]{2,1,0:T(1,128)}) custom-call(s32[1]{0:T(128)} %bitcast.7.replica_ref, f32[1,64,1024]{2,1,0:T(8,128)S(1)} %get-tuple-element.57.keep_ref, bf16[1,64,1024]{2,1,0:T(8,128)(2,1)S(1)} %collective-permute-done.7.got_ref, f32[25,1,512]{2,1,0:T(1,128)S(1)} %add.15.taps_ref, ...), custom_call_target="tpu_custom_call" | custom-call | tf_op jit(solution)/shard_map/pallas_call | solution.py:506
  (15 shorter events, 0.1 us)
Async XLA Ops:
  0.6 8.5 %copy-start.1 = (bf16[8,7,7,1024]{3,0,2,1:T(8,128)(2,1)S(1)}, bf16[8,7,7,1024]{3,0,2,1:T(8,128)(2,1)}, u32[]{:S(2)}) copy-start(bf16[8,7,7,1024]{3,0,2,1:T(8,128)(2,1)} %param.5) | copy-start | bytes 2408452
  0.6 16.1 %copy-start = (bf16[1,1,1024,1024]{3,2,1,0:T(8,128)(2,1)S(1)}, bf16[1,1,1024,1024]{3,2,1,0:T(8,128)(2,1)}, u32[]{:S(2)}) copy-start(bf16[1,1,1024,1024]{3,2,1,0:T(8,128)(2,1)} %param.7) | copy-start | bytes 6291460
  3.1 13.6 %collective-permute-start = (bf16[196,1024]{1,0:T(8,128)(2,1)}, bf16[196,1024]{1,0:T(8,128)(2,1)}, u32[]{:S(2)}, u32[]{:S(2)}) collective-permute-start(bf16[196,1024]{1,0:T(8,128)(2,1)} %get-tuple-element.40), channel_id=1, source_target_pairs={{0,16},{16,0},{1,17},{17,1},{2,18},{18,2},{3,19},{19,3},{4,20},{20... | collective-permute-start | bytes 1204232 | tf_op jit(solution)/shard_map/ppermute | solution.py:383
  6.1 1.1 %copy-start.2 = (bf16[8,7,7,1024]{3,0,2,1:T(8,128)(2,1)S(1)}, bf16[8,7,7,1024]{3,0,2,1:T(8,128)(2,1)}, u32[]{:S(2)}) copy-start(bf16[8,7,7,1024]{3,0,2,1:T(8,128)(2,1)} %param.9) | copy-start | bytes 2408452
  7.2 0.7 %copy-start.5 = (s32[8,392]{1,0:T(8,128)S(1)}, s32[8,392]{1,0:T(8,128)}, u32[]{:S(2)}) copy-start(s32[8,392]{1,0:T(8,128)} %get-tuple-element.33.code_ref) | copy-start | bytes 37636
  9.1 15.4 %collective-permute-start.2 = (bf16[196,1024]{1,0:T(8,128)(2,1)}, bf16[196,1024]{1,0:T(8,128)(2,1)S(1)}, u32[]{:S(2)}, u32[]{:S(2)}) collective-permute-start(bf16[196,1024]{1,0:T(8,128)(2,1)} %shard_map.88), channel_id=1, source_target_pairs={{0,16},{16,0},{1,17},{17,1},{2,18},{18,2},{3,19},{19,3},{4,20},{20... | collective-permute-start | bytes 1204232 | tf_op jit(solution)/shard_map/ppermute | solution.py:383
  9.1 1.1 %copy-start.3 = (bf16[8,7,7,1024]{3,0,2,1:T(8,128)(2,1)S(1)}, bf16[8,7,7,1024]{3,0,2,1:T(8,128)(2,1)}, u32[]{:S(2)}) copy-start(bf16[8,7,7,1024]{3,0,2,1:T(8,128)(2,1)} %param.9) | copy-start | bytes 2408452
  10.2 0.9 %copy-start.4 = (f32[1,1,25,1024]{3,1,2,0:T(1,128)S(1)}, f32[1,1,25,1024]{3,1,2,0:T(1,128)}, u32[]{:S(2)}) copy-start(f32[1,1,25,1024]{3,1,2,0:T(1,128)} %param.8) | copy-start | bytes 307204
  11.1 0.7 %copy-start.6 = (s32[8,392]{1,0:T(8,128)S(1)}, s32[8,392]{1,0:T(8,128)}, u32[]{:S(2)}) copy-start(s32[8,392]{1,0:T(8,128)} %get-tuple-element.33.code_ref) | copy-start | bytes 37636
  11.9 0.7 %copy-start.7 = (s32[1,8,1]{1,2,0:T(1,128)S(1)}, s32[1,8,1]{1,2,0:T(1,128)}, u32[]{:S(2)}) copy-start(s32[1,8,1]{1,2,0:T(1,128)} %param.6) | copy-start | bytes 100
  25.0 2.7 %collective-permute-start.4 = (bf16[8,64,1024]{2,1,0:T(8,128)(2,1)S(1)}, bf16[8,64,1024]{2,1,0:T(8,128)(2,1)S(1)}, u32[]{:S(2)}, u32[]{:S(2)}) collective-permute-start(bf16[8,64,1024]{2,1,0:T(8,128)(2,1)S(1)} %shard_map.94), channel_id=1, source_target_pairs={{0,1},{1,0},{2,3},{3,2},{4,5},{5,4},{6,7},{7,6},{8,9},{9,8},{10,11... | collective-permute-start | bytes 3145736 | tf_op jit(solution)/shard_map/ppermute | solution.py:397
  27.9 9.2 %collective-permute-start.5 = (bf16[4,64,1024]{2,1,0:T(8,128)(2,1)S(1)}, bf16[4,64,1024]{2,1,0:T(8,128)(2,1)S(1)}, u32[]{:S(2)}, u32[]{:S(2)}) collective-permute-start(bf16[4,64,1024]{2,1,0:T(8,128)(2,1)S(1)} %get-tuple-element.54), channel_id=1, source_target_pairs={{0,2},{1,5},{2,0},{3,7},{4,6},{5,1},{6,4},{7,3},{8,10},{9,13},{10,... | collective-permute-start | bytes 1572872 | tf_op jit(solution)/shard_map/ppermute | solution.py:397
  29.7 28.3 %collective-permute-start.1 = (bf16[196,1024]{1,0:T(8,128)(2,1)S(1)}, bf16[196,1024]{1,0:T(8,128)(2,1)S(1)}, u32[]{:S(2)}, u32[]{:S(2)}) collective-permute-start(bf16[196,1024]{1,0:T(8,128)(2,1)S(1)} %get-tuple-element.42), channel_id=1, source_target_pairs={{0,16},{16,0},{1,17},{17,1},{2,18},{18,2},{3,19},{19,3},{4,20},{20... | collective-permute-start | bytes 1204232 | tf_op jit(solution)/shard_map/ppermute | solution.py:383
  35.2 24.4 %collective-permute-start.3 = (bf16[196,1024]{1,0:T(8,128)(2,1)S(1)}, bf16[196,1024]{1,0:T(8,128)(2,1)S(1)}, u32[]{:S(2)}, u32[]{:S(2)}) collective-permute-start(bf16[196,1024]{1,0:T(8,128)(2,1)S(1)} %get-tuple-element.49), channel_id=1, source_target_pairs={{0,16},{16,0},{1,17},{17,1},{2,18},{18,2},{3,19},{19,3},{4,20},{20... | collective-permute-start | bytes 1204232 | tf_op jit(solution)/shard_map/ppermute | solution.py:383
  37.2 12.4 %collective-permute-start.6 = (bf16[2,64,1024]{2,1,0:T(8,128)(2,1)S(1)}, bf16[2,64,1024]{2,1,0:T(8,128)(2,1)S(1)}, u32[]{:S(2)}, u32[]{:S(2)}) collective-permute-start(bf16[2,64,1024]{2,1,0:T(8,128)(2,1)S(1)} %get-tuple-element.56), channel_id=1, source_target_pairs={{0,4},{1,3},{2,6},{3,1},{4,0},{5,7},{6,2},{7,5},{8,12},{9,11},{10,... | collective-permute-start | bytes 786440 | tf_op jit(solution)/shard_map/ppermute | solution.py:397
  40.4 1.4 %collective-permute-start.8 = (f32[25,1,512]{2,1,0:T(1,128)S(1)}, f32[25,1,512]{2,1,0:T(1,128)S(1)}, u32[]{:S(2)}, u32[]{:S(2)}) collective-permute-start(f32[25,1,512]{2,1,0:T(1,128)S(1)} %shard_map.99), channel_id=1, source_target_pairs={{0,1},{1,0},{2,3},{3,2},{4,5},{5,4},{6,7},{7,6},{8,9},{9,8},{10,11... | collective-permute-start | bytes 153608 | tf_op jit(solution)/shard_map/ppermute | solution.py:397
  41.9 6.2 %collective-permute-start.9 = (f32[25,1,512]{2,1,0:T(1,128)S(1)}, f32[25,1,512]{2,1,0:T(1,128)S(1)}, u32[]{:S(2)}, u32[]{:S(2)}) collective-permute-start(f32[25,1,512]{2,1,0:T(1,128)S(1)} %add.12), channel_id=1, source_target_pairs={{0,8},{1,9},{2,10},{3,11},{4,12},{5,13},{6,14},{7,15},{8,0},{9,1},... | collective-permute-start | bytes 153608 | tf_op jit(solution)/shard_map/ppermute | solution.py:397
  48.1 4.2 %collective-permute-start.10 = (f32[25,1,512]{2,1,0:T(1,128)S(1)}, f32[25,1,512]{2,1,0:T(1,128)S(1)}, u32[]{:S(2)}, u32[]{:S(2)}) collective-permute-start(f32[25,1,512]{2,1,0:T(1,128)S(1)} %add.13), channel_id=1, source_target_pairs={{0,2},{1,5},{2,0},{3,7},{4,6},{5,1},{6,4},{7,3},{8,10},{9,13},{10,... | collective-permute-start | bytes 153608 | tf_op jit(solution)/shard_map/ppermute | solution.py:397
  49.7 11.6 %collective-permute-start.7 = (bf16[1,64,1024]{2,1,0:T(8,128)(2,1)S(1)}, bf16[1,64,1024]{2,1,0:T(8,128)(2,1)S(1)}, u32[]{:S(2)}, u32[]{:S(2)}) collective-permute-start(bf16[1,64,1024]{2,1,0:T(8,128)(2,1)S(1)} %get-tuple-element.58), channel_id=1, source_target_pairs={{0,8},{1,9},{2,10},{3,11},{4,12},{5,13},{6,14},{7,15},{8,0},{9,1},... | collective-permute-start | bytes 393224 | tf_op jit(solution)/shard_map/ppermute | solution.py:397
  52.3 5.5 %collective-permute-start.11 = (f32[25,1,512]{2,1,0:T(1,128)S(1)}, f32[25,1,512]{2,1,0:T(1,128)S(1)}, u32[]{:S(2)}, u32[]{:S(2)}) collective-permute-start(f32[25,1,512]{2,1,0:T(1,128)S(1)} %add.14), channel_id=1, source_target_pairs={{0,4},{1,3},{2,6},{3,1},{4,0},{5,7},{6,2},{7,5},{8,12},{9,11},{10,... | collective-permute-start | bytes 153608 | tf_op jit(solution)/shard_map/ppermute | solution.py:397
  57.9 3.5 %collective-permute-start.12 = (f32[25,1,512]{2,1,0:T(1,128)S(1)}, f32[25,1,512]{2,1,0:T(1,128)S(1)}, u32[]{:S(2)}, u32[]{:S(2)}) collective-permute-start(f32[25,1,512]{2,1,0:T(1,128)S(1)} %add.15.taps_ref), channel_id=1, source_target_pairs={{0,1},{1,0},{2,3},{3,2},{4,5},{5,4},{6,7},{7,6},{8,9},{9,8},{10,11... | collective-permute-start | bytes 153608 | tf_op jit(solution)/shard_map/ppermute | solution.py:397
